TPU v7x, 256 devices: a whole 4x4x8 slice. The times are simulated.
256 devices in a mesh: row: 8 (over z_hi, core), col: 32 (over x, y, z_lo).
Axes of the slice: x: 4, y: 4, z: 8 (z_hi: 4, z_lo: 2; z = z_hi * 2 + z_lo), core: 2. Of those that a mesh axis runs over, the one named last changes fastest.
Arguments:
- object_re: float32 [2048, 8192], P('row', 'col'), may hold values from -6 to 6
- object_im: float32 [2048, 8192], P('row', 'col'), may hold values from -6 to 6
- probe_re: float32 [256, 256], replicated, may hold values from -4 to 4
- probe_im: float32 [256, 256], replicated, may hold values from -4 to 4
- intensity: float32 [8, 32, 4, 256, 256], P('row', 'col'), may hold values from 0.05 to 4
- offsets: int32 [8, 32, 4, 2], P('row', 'col'), may hold values from 48 to 208
- counts: int32 [8, 32], P('row', 'col'), may hold values from 2 to 4
Outputs:
- final_re: float32 [2048, 8192], P('row', 'col')
- final_im: float32 [2048, 8192], P('row', 'col')
All inputs are finite; a program needn't handle non-finite values.
Results may differ from a plain program's by a relative error of at most 0.00024.
Values sent between devices are 32-bit elements; how exact they have to be, the bound alone decides.
No kernel may reach another device: no remote copies, remote signals or barrier semaphores. Data moves between devices by JAX's collectives and lax.ppermute only.
A program may use at most 64 MiB of HBM per device.

v0:
```python
import functools
import math

import jax
import jax.numpy as jnp
import numpy as np
from jax import lax
from jax.experimental import pallas as pl
from jax.experimental.pallas import tpu as pltpu
from jax.sharding import PartitionSpec as P

ITERS = 2

smoothing = 0.01
step_size = 0.25

W = 256
H = 128
REACH = 80
EXT = W + 2 * REACH

VMEM = pl.BlockSpec(memory_space=pltpu.VMEM)
SMEM = pl.BlockSpec(memory_space=pltpu.SMEM)
f32 = jnp.float32
bf16 = jnp.bfloat16


def shape(*dims):
    return jax.ShapeDtypeStruct(dims, f32)


def dft_tables():
    k = np.arange(H)[:, None]
    mats = []
    for odd in (0, 1):
        freq = 2 * np.arange(H)[None, :] + odd
        angle = -2.0 * math.pi * ((k * freq) % W) / W
        c, s = np.cos(angle) / 16.0, np.sin(angle) / 16.0
        mats.append(np.block([[c, s], [-s, c]]))
    mats = [mats[0], mats[1], mats[0].T, mats[1].T]
    out = []
    for m in mats:
        m = m.astype(np.float32)
        hi = m.astype(jnp.bfloat16)
        lo = (m - hi.astype(np.float32)).astype(jnp.bfloat16)
        out.extend([hi, lo])
    return np.stack(out)


def split(x):
    hi = x.astype(bf16)
    lo = (x - hi.astype(f32)).astype(bf16)
    return hi, lo


def dot(a, b):
    return lax.dot_general(a, b, (((1,), (0,)), ((), ())), preferred_element_type=f32)


def right(x, tables, i):
    hi, lo = split(x)
    t_hi, t_lo = tables[2 * i], tables[2 * i + 1]
    return dot(
        jnp.concatenate([hi, lo, hi], axis=1), jnp.concatenate([t_hi, t_hi, t_lo], axis=0)
    )


def left(tables, i, x):
    hi, lo = split(x)
    t_hi, t_lo = tables[2 * i], tables[2 * i + 1]
    return dot(
        jnp.concatenate([t_hi, t_hi, t_lo], axis=1), jnp.concatenate([hi, lo, hi], axis=0)
    )


def cat(a, b, axis):
    return jnp.concatenate([a, b], axis=axis)


def roots_kernel(intensity, out):
    row = lax.broadcasted_iota(jnp.int32, (W, W), 0)
    col = lax.broadcasted_iota(jnp.int32, (W, W), 1)
    source = jnp.where(col < H, 2 * col, 2 * (col - H) + 1)
    perm = jnp.where(row == source, 1.0, 0.0).astype(bf16)
    perm3 = jnp.concatenate([perm, perm, perm], axis=0)
    for p in range(out.shape[0]):
        x = jnp.sqrt(intensity[p])
        hi = x.astype(bf16)
        rest = x - hi.astype(f32)
        mid = rest.astype(bf16)
        lo = (rest - mid.astype(f32)).astype(bf16)
        y = dot(jnp.concatenate([hi, mid, lo], axis=1), perm3)
        y = y.reshape(H, 2, W)
        out[p, pl.ds(0, H), :] = y[:, 0, :]
        out[p, pl.ds(H, H), :] = y[:, 1, :]


def columns_kernel(re, im, to_left, to_right):
    for comp, x in enumerate((re, im)):
        to_left[comp] = x[:, 0:H].T[:REACH]
        to_right[comp] = x[:, H:W].T[H - REACH :]


def fill_sides(mid, from_left, from_right):
    blank = jnp.zeros((H - REACH, W), f32)
    for comp in range(2):
        mid[comp, 0] = jnp.concatenate([blank, from_left[comp]], axis=0).T
        mid[comp, 3] = jnp.concatenate([from_right[comp], blank], axis=0).T


def widen_kernel(re, im, from_left, from_right, mid, top, bottom):
    for comp, x in enumerate((re, im)):
        mid[comp, 1] = x[:, 0:H]
        mid[comp, 2] = x[:, H:W]
    fill_sides(mid, from_left, from_right)
    top[...] = mid[:, :, 0:REACH, :]
    bottom[...] = mid[:, :, W - REACH : W, :]


def gradient_kernel(
    offsets, counts, from_top, mid, from_bottom, roots, probe_re, probe_im, tables,
    to_top, centre, to_bottom, ext, acc,
):
    ext[:, :, 0:REACH, :] = from_top[...]
    ext[:, :, REACH : REACH + W, :] = mid[...]
    ext[:, :, REACH + W :, :] = from_bottom[...]
    acc[...] = jnp.zeros(acc.shape, f32)
    lane = lax.broadcasted_iota(jnp.int32, (W, H), 1)

    def position(p, carry):
        row = offsets[p, 0] - (H - REACH)
        base = lax.rem(p, 2)
        shift = offsets[p, 1] - H * base
        rows = pl.ds(row, W)
        o = []
        for comp in range(2):
            rolled = [pltpu.roll(ext[comp, base + j, rows, :], H - shift, 1) for j in range(3)]
            o.append([jnp.where(lane < H - shift, rolled[j], rolled[j + 1]) for j in range(2)])
        w_re, w_im = [], []
        for j in range(2):
            p_re, p_im = probe_re[:, j * H : (j + 1) * H], probe_im[:, j * H : (j + 1) * H]
            w_re.append(o[0][j] * p_re - o[1][j] * p_im)
            w_im.append(o[0][j] * p_im + o[1][j] * p_re)
        e = right(cat(w_re[0] + w_re[1], w_im[0] + w_im[1], 1), tables, 0)
        d = right(cat(w_re[0] - w_re[1], w_im[0] - w_im[1], 1), tables, 1)
        h_re = cat(e[:, :H], d[:, :H], 1)
        h_im = cat(e[:, H:], d[:, H:], 1)
        far_e = left(tables, 2, cat(h_re[:H] + h_re[H:], h_im[:H] + h_im[H:], 0))
        far_d = left(tables, 3, cat(h_re[:H] - h_re[H:], h_im[:H] - h_im[H:], 0))

        def residual(far, root):
            power = far[:H] * far[:H] + far[H:] * far[H:] + smoothing
            factor = 1.0 - root * lax.rsqrt(power)
            return far * cat(factor, factor, 0)

        a = left(tables, 0, residual(far_e, roots[p, pl.ds(0, H), :]))
        b = left(tables, 1, residual(far_d, roots[p, pl.ds(H, H), :]))
        upper, lower = a + b, a - b
        h_re = cat(upper[:H], lower[:H], 0)
        h_im = cat(upper[H:], lower[H:], 0)
        a = right(cat(h_re[:, :H], h_im[:, :H], 1), tables, 2)
        b = right(cat(h_re[:, H:], h_im[:, H:], 1), tables, 3)
        weight = jnp.where(p < counts[0, 0], 1.0, 0.0).astype(f32)
        g_re, g_im = [], []
        for j, x in enumerate((a + b, a - b)):
            p_re, p_im = probe_re[:, j * H : (j + 1) * H], probe_im[:, j * H : (j + 1) * H]
            p_re, p_im = p_re * weight, p_im * weight
            g_re.append(x[:, :H] * p_re + x[:, H:] * p_im)
            g_im.append(x[:, H:] * p_re - x[:, :H] * p_im)
        for comp, g in enumerate((g_re, g_im)):
            r = [pltpu.roll(g[j], shift, 1) for j in range(2)]
            acc[comp, base, rows, :] += jnp.where(lane >= shift, r[0], 0.0)
            acc[comp, base + 1, rows, :] += jnp.where(lane >= shift, r[1], r[0])
            acc[comp, base + 2, rows, :] += jnp.where(lane < shift, r[1], 0.0)
        return carry

    lax.fori_loop(0, roots.shape[0], position, 0)
    to_top[...] = acc[:, :, 0:REACH, :]
    centre[...] = acc[:, :, REACH : REACH + W, :]
    to_bottom[...] = acc[:, :, REACH + W :, :]


def add_rows(centre, from_top, from_bottom, total):
    total[...] = centre[...]
    total[:, :, 0:REACH, :] += from_top[...]
    total[:, :, W - REACH : W, :] += from_bottom[...]


def rows_kernel(reach, centre, from_top, from_bottom, total, to_left, to_right):
    add_rows(centre, from_top, from_bottom, total)
    for comp in range(2):
        to_left[comp, 0:REACH] = total[comp, 0].T[H - REACH :]
        to_right[comp, reach - REACH :] = total[comp, 3].T[:REACH]
        if reach > REACH:
            to_left[comp, REACH:] = total[comp, 1].T[:REACH]
            to_right[comp, 0:REACH] = total[comp, 2].T[H - REACH :]


def step_kernel(edges, mid, total, from_left, from_right, out, top, bottom):
    blank = jnp.zeros((H - REACH, W), f32)
    keep_left = jnp.where(edges[0] != 0, 0.0, 1.0).astype(f32)
    keep_right = jnp.where(edges[1] != 0, 0.0, 1.0).astype(f32)
    for comp in range(2):
        add = [
            cat(blank, from_left[comp, 0:REACH], 0).T,
            cat(from_left[comp, REACH:], blank, 0).T,
            cat(blank, from_right[comp, 0:REACH], 0).T,
            cat(from_right[comp, REACH:], blank, 0).T,
        ]
        keep = [keep_left, None, None, keep_right]
        for j in range(4):
            value = mid[comp, j] - step_size * (total[comp, j] + add[j])
            out[comp, j] = value if keep[j] is None else value * keep[j]
    top[...] = out[:, :, 0:REACH, :]
    bottom[...] = out[:, :, W - REACH : W, :]


def final_kernel(mid, total, from_left, from_right, out_re, out_im):
    blank = jnp.zeros((H - REACH, W), f32)
    for comp, out in enumerate((out_re, out_im)):
        add = [
            cat(from_left[comp], blank, 0).T,
            cat(blank, from_right[comp], 0).T,
        ]
        for j in range(2):
            value = mid[comp, j + 1] - step_size * (total[comp, j + 1] + add[j])
            out[:, j * H : (j + 1) * H] = value


def call(kernel, specs, out_shape, *args, scratch=(), flops=0, read=0):
    return pl.pallas_call(
        kernel,
        in_specs=specs,
        out_specs=jax.tree.map(lambda _: VMEM, out_shape),
        out_shape=out_shape,
        scratch_shapes=scratch,
        compiler_params=pltpu.CompilerParams(vmem_limit_bytes=48 * 1024 * 1024),
        cost_estimate=pl.CostEstimate(flops=flops, bytes_accessed=read, transcendentals=0),
    )(*args)


def exchange(axis, to_before, to_after):
    size = lax.axis_size(axis)
    up = [(i, i + 1) for i in range(size - 1)]
    down = [(j, i) for i, j in up]
    return lax.ppermute(to_after, axis, up), lax.ppermute(to_before, axis, down)


def shards(object_re, object_im, probe_re, probe_im, intensity, offsets, counts):
    slots = intensity.shape[2]
    placed = offsets[0, 0]
    tables = jnp.asarray(dft_tables())
    column = lax.axis_index("col")
    last = lax.axis_size("col") - 1
    edges = jnp.stack([column == 0, column == last]).astype(jnp.int32)

    strip = shape(2, REACH, W)
    wide = shape(2, 2 * REACH, W)
    rows = shape(2, 4, REACH, H)
    full = shape(2, 4, W, H)

    to_left, to_right = call(columns_kernel, [VMEM] * 2, (strip, strip), object_re, object_im, read=1 << 20)
    from_left, from_right = exchange("col", to_left, to_right)
    roots = call(roots_kernel, [VMEM], shape(slots, W, W), intensity[0, 0], flops=1 << 29, read=1 << 21)
    mid, top, bottom = call(
        widen_kernel, [VMEM] * 4, (full, rows, rows), object_re, object_im, from_left, from_right, read=1 << 21
    )
    for sweep in range(ITERS):
        from_top, from_bottom = exchange("row", top, bottom)
        to_top, centre, to_bottom = call(
            gradient_kernel,
            [SMEM, SMEM] + [VMEM] * 7,
            (rows, full, rows),
            placed, counts, from_top, mid, from_bottom, roots, probe_re, probe_im, tables,
            scratch=[pltpu.VMEM((2, 4, EXT, H), f32)] * 2,
            flops=1 << 32,
            read=1 << 23,
        )
        from_top, from_bottom = exchange("row", to_top, to_bottom)
        final = sweep == ITERS - 1
        reach = REACH if final else 2 * REACH
        strips = strip if final else wide
        total, to_left, to_right = call(
            functools.partial(rows_kernel, reach),
            [VMEM] * 3,
            (full, strips, strips),
            centre, from_top, from_bottom,
            read=1 << 21,
        )
        from_left, from_right = exchange("col", to_left, to_right)
        if final:
            tile = shape(W, W)
            return call(
                final_kernel, [VMEM] * 4, (tile, tile), mid, total, from_left, from_right, read=1 << 21
            )
        mid, top, bottom = call(
            step_kernel, [SMEM] + [VMEM] * 4, (full, rows, rows),
            edges, mid, total, from_left, from_right, read=1 << 21,
        )


def solution(mesh):
    return jax.shard_map(
        shards,
        mesh=mesh,
        in_specs=(
            P("row", "col"),
            P("row", "col"),
            P(),
            P(),
            P("row", "col", None, None, None),
            P("row", "col", None, None),
            P("row", "col"),
        ),
        out_specs=(P("row", "col"), P("row", "col")),
        check_vma=False,
    )
```

profile of v0, /device:TPU:69, one launch (start us, length us, event | category | flops | bytes accessed | tf_op | source)
XLA Modules:
  0.0 133.5 jit_solution(7181313828006786542)
XLA Ops:
  0.6 0.0 copy-start
  0.6 0.0 copy-start.1
  0.6 1.0 copy-done.1
  1.7 0.9 copy-done.2
  2.6 0.2 shard_map.95
  2.8 3.5 %collective-permute-start = (f32[2,80,256]{2,1,0:T(8,128)S(1)}, f32[2,80,256]{2,1,0:T(8,128)S(1)}, u32[]{:S(2)}, u32[]{:S(2)}) collective-permute-start(f32[2,80,256]{2,1,0:T(8,128)S(1)} %get-tuple-element.22), channel_id=1, source_target_pairs={{0,1},{1,2},{2,3},{3,4},{4,5},{5,6},{6,7},{7,8},{8,9},{9,10},{10,1... | collective-permute-start | bytes 491528 | tf_op jit(solution)/shard_map/ppermute | solution.py:246
  6.4 4.7 %collective-permute-start.1 = (f32[2,80,256]{2,1,0:T(8,128)S(1)}, f32[2,80,256]{2,1,0:T(8,128)S(1)}, u32[]{:S(2)}, u32[]{:S(2)}) collective-permute-start(f32[2,80,256]{2,1,0:T(8,128)S(1)} %get-tuple-element.23), channel_id=1, source_target_pairs={{1,0},{2,1},{3,2},{4,3},{5,4},{6,5},{7,6},{8,7},{9,8},{10,9},{11,1... | collective-permute-start | bytes 491528 | tf_op jit(solution)/shard_map/ppermute | solution.py:246
  11.1 1.7 %collective-permute-done.from_left = f32[2,80,256]{2,1,0:T(8,128)S(1)} collective-permute-done((f32[2,80,256]{2,1,0:T(8,128)S(1)}, f32[2,80,256]{2,1,0:T(8,128)S(1)}, u32[]{:S(2)}, u32[]{:S(2)}) %collective-permute-start) | collective-permute-done | bytes 163872 | tf_op jit(solution)/shard_map/ppermute | solution.py:246
  12.8 1.7 %collective-permute-done.1.from_right = f32[2,80,256]{2,1,0:T(8,128)S(1)} collective-permute-done((f32[2,80,256]{2,1,0:T(8,128)S(1)}, f32[2,80,256]{2,1,0:T(8,128)S(1)}, u32[]{:S(2)}, u32[]{:S(2)}) %collective-permute-start.1) | collective-permute-done | bytes 163872 | tf_op jit(solution)/shard_map/ppermute | solution.py:246
  14.5 1.0 shard_map.96
  15.5 7.3 %collective-permute-start.2 = (f32[2,4,80,128]{3,2,1,0:T(8,128)}, f32[2,4,80,128]{3,2,1,0:T(8,128)S(1)}, u32[]{:S(2)}, u32[]{:S(2)}) collective-permute-start(f32[2,4,80,128]{3,2,1,0:T(8,128)} %get-tuple-element.25), channel_id=1, source_target_pairs={{0,32},{32,64},{64,96},{96,128},{128,160},{160,192},{192,224},{1,3... | collective-permute-start | bytes 983048 | tf_op jit(solution)/shard_map/ppermute | solution.py:246
  22.9 1.9 %collective-permute-start.3 = (f32[2,4,80,128]{3,2,1,0:T(8,128)}, f32[2,4,80,128]{3,2,1,0:T(8,128)}, u32[]{:S(2)}, u32[]{:S(2)}) collective-permute-start(f32[2,4,80,128]{3,2,1,0:T(8,128)} %get-tuple-element.26), channel_id=1, source_target_pairs={{32,0},{64,32},{96,64},{128,96},{160,128},{192,160},{224,192},{33,... | collective-permute-start | bytes 983048 | tf_op jit(solution)/shard_map/ppermute | solution.py:246
  25.5 0.0 copy-start.9
  25.5 0.7 copy-done.9
  26.1 0.1 copy.10.offsets
  26.2 0.0 copy-done
  26.3 1.5 %shard_map.97.roots = f32[4,256,256]{2,1,0:T(8,128)S(1)} custom-call(f32[4,256,256]{2,1,0:T(8,128)S(1)} %bitcast.4), custom_call_target="tpu_custom_call" | custom-call | flops 536870912 | bytes 2097152 | tf_op jit(solution)/shard_map/pallas_call | solution.py:231
  27.8 2.9 %collective-permute-done.2.from_top = f32[2,4,80,128]{3,2,1,0:T(8,128)S(1)} collective-permute-done((f32[2,4,80,128]{3,2,1,0:T(8,128)}, f32[2,4,80,128]{3,2,1,0:T(8,128)S(1)}, u32[]{:S(2)}, u32[]{:S(2)}) %collective-permute-start.2) | collective-permute-done | bytes 327712 | tf_op jit(solution)/shard_map/ppermute | solution.py:246
  30.7 6.4 %collective-permute-done.3.from_bottom = f32[2,4,80,128]{3,2,1,0:T(8,128)} collective-permute-done((f32[2,4,80,128]{3,2,1,0:T(8,128)}, f32[2,4,80,128]{3,2,1,0:T(8,128)}, u32[]{:S(2)}, u32[]{:S(2)}) %collective-permute-start.3) | collective-permute-done | bytes 327712 | tf_op jit(solution)/shard_map/ppermute | solution.py:246
  37.1 0.0 copy-done.3
  37.1 8.7 %shard_map.98 = (f32[2,4,80,128]{3,2,1,0:T(8,128)S(1)}, f32[2,4,256,128]{3,2,1,0:T(8,128)S(1)}, f32[2,4,80,128]{3,2,1,0:T(8,128)S(1)}) custom-call(s32[4,2]{1,0:T(4,128)S(1)} %copy.10.offsets, s32[1,1]{1,0:T(1,128)S(6)} %copy.12.counts, f32[2,4,80,128]{3,2,1,0:T(8,128)S(1)} %collective-permute-done.2.from_top, f32[2,4,256,128]{3,2,1,0:T(8,128)S(1)} %get-tuple-element.24.mid, ...), custom_call_target="tpu_custom_call" | custom-call | flops 4294967296 | bytes 8388608 | tf_op jit(solution)/shard_map/pallas_call | solution.py:231
  45.8 1.9 %collective-permute-start.4 = (f32[2,4,80,128]{3,2,1,0:T(8,128)S(1)}, f32[2,4,80,128]{3,2,1,0:T(8,128)S(1)}, u32[]{:S(2)}, u32[]{:S(2)}) collective-permute-start(f32[2,4,80,128]{3,2,1,0:T(8,128)S(1)} %get-tuple-element.28), channel_id=1, source_target_pairs={{0,32},{32,64},{64,96},{96,128},{128,160},{160,192},{192,224},{1,3... | collective-permute-start | bytes 983048 | tf_op jit(solution)/shard_map/ppermute | solution.py:246
  47.8 2.4 %collective-permute-start.5 = (f32[2,4,80,128]{3,2,1,0:T(8,128)S(1)}, f32[2,4,80,128]{3,2,1,0:T(8,128)S(1)}, u32[]{:S(2)}, u32[]{:S(2)}) collective-permute-start(f32[2,4,80,128]{3,2,1,0:T(8,128)S(1)} %get-tuple-element.29), channel_id=1, source_target_pairs={{32,0},{64,32},{96,64},{128,96},{160,128},{192,160},{224,192},{33,... | collective-permute-start | bytes 983048 | tf_op jit(solution)/shard_map/ppermute | solution.py:246
  50.2 3.1 %collective-permute-done.4.from_top = f32[2,4,80,128]{3,2,1,0:T(8,128)S(1)} collective-permute-done((f32[2,4,80,128]{3,2,1,0:T(8,128)S(1)}, f32[2,4,80,128]{3,2,1,0:T(8,128)S(1)}, u32[]{:S(2)}, u32[]{:S(2)}) %collective-permute-start.4) | collective-permute-done | bytes 327712 | tf_op jit(solution)/shard_map/ppermute | solution.py:246
  53.3 5.4 %collective-permute-done.5.from_bottom = f32[2,4,80,128]{3,2,1,0:T(8,128)S(1)} collective-permute-done((f32[2,4,80,128]{3,2,1,0:T(8,128)S(1)}, f32[2,4,80,128]{3,2,1,0:T(8,128)S(1)}, u32[]{:S(2)}, u32[]{:S(2)}) %collective-permute-start.5) | collective-permute-done | bytes 327712 | tf_op jit(solution)/shard_map/ppermute | solution.py:246
  58.7 1.1 shard_map.99
  59.8 5.3 %collective-permute-start.6 = (f32[2,160,256]{2,1,0:T(8,128)}, f32[2,160,256]{2,1,0:T(8,128)S(1)}, u32[]{:S(2)}, u32[]{:S(2)}) collective-permute-start(f32[2,160,256]{2,1,0:T(8,128)} %get-tuple-element.31), channel_id=1, source_target_pairs={{0,1},{1,2},{2,3},{3,4},{4,5},{5,6},{6,7},{7,8},{8,9},{9,10},{10,1... | collective-permute-start | bytes 983048 | tf_op jit(solution)/shard_map/ppermute | solution.py:246
  65.1 4.0 %collective-permute-start.7 = (f32[2,160,256]{2,1,0:T(8,128)}, f32[2,160,256]{2,1,0:T(8,128)}, u32[]{:S(2)}, u32[]{:S(2)}) collective-permute-start(f32[2,160,256]{2,1,0:T(8,128)} %get-tuple-element.32), channel_id=1, source_target_pairs={{1,0},{2,1},{3,2},{4,3},{5,4},{6,5},{7,6},{8,7},{9,8},{10,9},{11,1... | collective-permute-start | bytes 983048 | tf_op jit(solution)/shard_map/ppermute | solution.py:246
  69.1 0.1 add_convert_fusion.edges
  69.2 6.2 %collective-permute-done.6.from_left = f32[2,160,256]{2,1,0:T(8,128)S(1)} collective-permute-done((f32[2,160,256]{2,1,0:T(8,128)}, f32[2,160,256]{2,1,0:T(8,128)S(1)}, u32[]{:S(2)}, u32[]{:S(2)}) %collective-permute-start.6) | collective-permute-done | bytes 327712 | tf_op jit(solution)/shard_map/ppermute | solution.py:246
  75.3 4.1 %collective-permute-done.7.from_right = f32[2,160,256]{2,1,0:T(8,128)} collective-permute-done((f32[2,160,256]{2,1,0:T(8,128)}, f32[2,160,256]{2,1,0:T(8,128)}, u32[]{:S(2)}, u32[]{:S(2)}) %collective-permute-start.7) | collective-permute-done | bytes 327712 | tf_op jit(solution)/shard_map/ppermute | solution.py:246
  79.5 1.4 %shard_map.100 = (f32[2,4,256,128]{3,2,1,0:T(8,128)S(1)}, f32[2,4,80,128]{3,2,1,0:T(8,128)S(1)}, f32[2,4,80,128]{3,2,1,0:T(8,128)S(1)}) custom-call(s32[2]{0:T(128)S(1)} %add_convert_fusion.edges, f32[2,4,256,128]{3,2,1,0:T(8,128)S(1)} %get-tuple-element.24.mid, f32[2,4,256,128]{3,2,1,0:T(8,128)S(1)} %get-tuple-element.30.total, ...), custom_call_target="tpu_custom_call" | custom-call | bytes 2097152 | tf_op jit(solution)/shard_map/pallas_call | solution.py:231
  80.9 2.8 %collective-permute-start.8 = (f32[2,4,80,128]{3,2,1,0:T(8,128)S(1)}, f32[2,4,80,128]{3,2,1,0:T(8,128)S(1)}, u32[]{:S(2)}, u32[]{:S(2)}) collective-permute-start(f32[2,4,80,128]{3,2,1,0:T(8,128)S(1)} %get-tuple-element.34), channel_id=1, source_target_pairs={{0,32},{32,64},{64,96},{96,128},{128,160},{160,192},{192,224},{1,3... | collective-permute-start | bytes 983048 | tf_op jit(solution)/shard_map/ppermute | solution.py:246
  83.7 1.9 %collective-permute-start.9 = (f32[2,4,80,128]{3,2,1,0:T(8,128)S(1)}, f32[2,4,80,128]{3,2,1,0:T(8,128)S(1)}, u32[]{:S(2)}, u32[]{:S(2)}) collective-permute-start(f32[2,4,80,128]{3,2,1,0:T(8,128)S(1)} %get-tuple-element.35), channel_id=1, source_target_pairs={{32,0},{64,32},{96,64},{128,96},{160,128},{192,160},{224,192},{33,... | collective-permute-start | bytes 983048 | tf_op jit(solution)/shard_map/ppermute | solution.py:246
  85.7 3.0 %collective-permute-done.8.from_top = f32[2,4,80,128]{3,2,1,0:T(8,128)S(1)} collective-permute-done((f32[2,4,80,128]{3,2,1,0:T(8,128)S(1)}, f32[2,4,80,128]{3,2,1,0:T(8,128)S(1)}, u32[]{:S(2)}, u32[]{:S(2)}) %collective-permute-start.8) | collective-permute-done | bytes 327712 | tf_op jit(solution)/shard_map/ppermute | solution.py:246
  88.7 8.9 %collective-permute-done.9.from_bottom = f32[2,4,80,128]{3,2,1,0:T(8,128)S(1)} collective-permute-done((f32[2,4,80,128]{3,2,1,0:T(8,128)S(1)}, f32[2,4,80,128]{3,2,1,0:T(8,128)S(1)}, u32[]{:S(2)}, u32[]{:S(2)}) %collective-permute-start.9) | collective-permute-done | bytes 327712 | tf_op jit(solution)/shard_map/ppermute | solution.py:246
  97.5 0.0 copy-done.4
  97.6 8.3 %shard_map.101 = (f32[2,4,80,128]{3,2,1,0:T(8,128)S(1)}, f32[2,4,256,128]{3,2,1,0:T(8,128)S(1)}, f32[2,4,80,128]{3,2,1,0:T(8,128)S(1)}) custom-call(s32[4,2]{1,0:T(4,128)S(1)} %copy.10.offsets, s32[1,1]{1,0:T(1,128)S(6)} %copy.12.counts, f32[2,4,80,128]{3,2,1,0:T(8,128)S(1)} %collective-permute-done.8.from_top, ...), custom_call_target="tpu_custom_call" | custom-call | flops 4294967296 | bytes 8388608 | tf_op jit(solution)/shard_map/pallas_call | solution.py:231
  105.9 1.9 %collective-permute-start.10 = (f32[2,4,80,128]{3,2,1,0:T(8,128)S(1)}, f32[2,4,80,128]{3,2,1,0:T(8,128)S(1)}, u32[]{:S(2)}, u32[]{:S(2)}) collective-permute-start(f32[2,4,80,128]{3,2,1,0:T(8,128)S(1)} %get-tuple-element.37), channel_id=1, source_target_pairs={{0,32},{32,64},{64,96},{96,128},{128,160},{160,192},{192,224},{1,3... | collective-permute-start | bytes 983048 | tf_op jit(solution)/shard_map/ppermute | solution.py:246
  107.8 2.4 %collective-permute-start.11 = (f32[2,4,80,128]{3,2,1,0:T(8,128)S(1)}, f32[2,4,80,128]{3,2,1,0:T(8,128)S(1)}, u32[]{:S(2)}, u32[]{:S(2)}) collective-permute-start(f32[2,4,80,128]{3,2,1,0:T(8,128)S(1)} %get-tuple-element.38), channel_id=1, source_target_pairs={{32,0},{64,32},{96,64},{128,96},{160,128},{192,160},{224,192},{33,... | collective-permute-start | bytes 983048 | tf_op jit(solution)/shard_map/ppermute | solution.py:246
  110.2 4.2 %collective-permute-done.10.from_top = f32[2,4,80,128]{3,2,1,0:T(8,128)S(1)} collective-permute-done((f32[2,4,80,128]{3,2,1,0:T(8,128)S(1)}, f32[2,4,80,128]{3,2,1,0:T(8,128)S(1)}, u32[]{:S(2)}, u32[]{:S(2)}) %collective-permute-start.10) | collective-permute-done | bytes 327712 | tf_op jit(solution)/shard_map/ppermute | solution.py:246
  114.4 7.4 %collective-permute-done.11.from_bottom = f32[2,4,80,128]{3,2,1,0:T(8,128)S(1)} collective-permute-done((f32[2,4,80,128]{3,2,1,0:T(8,128)S(1)}, f32[2,4,80,128]{3,2,1,0:T(8,128)S(1)}, u32[]{:S(2)}, u32[]{:S(2)}) %collective-permute-start.11) | collective-permute-done | bytes 327712 | tf_op jit(solution)/shard_map/ppermute | solution.py:246
  121.8 0.2 shard_map.102
  122.0 1.9 %collective-permute-start.12 = (f32[2,80,256]{2,1,0:T(8,128)S(1)}, f32[2,80,256]{2,1,0:T(8,128)S(1)}, u32[]{:S(2)}, u32[]{:S(2)}) collective-permute-start(f32[2,80,256]{2,1,0:T(8,128)S(1)} %get-tuple-element.40), channel_id=1, source_target_pairs={{0,1},{1,2},{2,3},{3,4},{4,5},{5,6},{6,7},{7,8},{8,9},{9,10},{10,1... | collective-permute-start | bytes 491528 | tf_op jit(solution)/shard_map/ppermute | solution.py:246
  123.9 6.4 %collective-permute-start.13 = (f32[2,80,256]{2,1,0:T(8,128)S(1)}, f32[2,80,256]{2,1,0:T(8,128)S(1)}, u32[]{:S(2)}, u32[]{:S(2)}) collective-permute-start(f32[2,80,256]{2,1,0:T(8,128)S(1)} %get-tuple-element.41), channel_id=1, source_target_pairs={{1,0},{2,1},{3,2},{4,3},{5,4},{6,5},{7,6},{8,7},{9,8},{10,9},{11,1... | collective-permute-start | bytes 491528 | tf_op jit(solution)/shard_map/ppermute | solution.py:246
  130.3 1.3 %collective-permute-done.12.from_left = f32[2,80,256]{2,1,0:T(8,128)S(1)} collective-permute-done((f32[2,80,256]{2,1,0:T(8,128)S(1)}, f32[2,80,256]{2,1,0:T(8,128)S(1)}, u32[]{:S(2)}, u32[]{:S(2)}) %collective-permute-start.12) | collective-permute-done | bytes 163872 | tf_op jit(solution)/shard_map/ppermute | solution.py:246
  131.7 0.9 collective-permute-done.13.from_right
  132.6 0.9 shard_map.103
  (11 shorter events, 0.0 us)
Async XLA Ops:
  0.6 25.6 %copy-start = (f32[1,1,4,256,256]{4,3,2,1,0:T(8,128)S(1)}, f32[1,1,4,256,256]{4,3,2,1,0:T(8,128)}, u32[]{:S(2)}) copy-start(f32[1,1,4,256,256]{4,3,2,1,0:T(8,128)} %param.12) | copy-start | bytes 3145732
  0.6 1.0 copy-start.1
  1.7 0.9 copy-start.2
  2.8 10.0 %collective-permute-start = (f32[2,80,256]{2,1,0:T(8,128)S(1)}, f32[2,80,256]{2,1,0:T(8,128)S(1)}, u32[]{:S(2)}, u32[]{:S(2)}) collective-permute-start(f32[2,80,256]{2,1,0:T(8,128)S(1)} %get-tuple-element.22), channel_id=1, source_target_pairs={{0,1},{1,2},{2,3},{3,4},{4,5},{5,6},{6,7},{7,8},{8,9},{9,10},{10,1... | collective-permute-start | bytes 491528 | tf_op jit(solution)/shard_map/ppermute | solution.py:246
  6.4 8.1 %collective-permute-start.1 = (f32[2,80,256]{2,1,0:T(8,128)S(1)}, f32[2,80,256]{2,1,0:T(8,128)S(1)}, u32[]{:S(2)}, u32[]{:S(2)}) collective-permute-start(f32[2,80,256]{2,1,0:T(8,128)S(1)} %get-tuple-element.23), channel_id=1, source_target_pairs={{1,0},{2,1},{3,2},{4,3},{5,4},{6,5},{7,6},{8,7},{9,8},{10,9},{11,1... | collective-permute-start | bytes 491528 | tf_op jit(solution)/shard_map/ppermute | solution.py:246
  15.5 15.1 %collective-permute-start.2 = (f32[2,4,80,128]{3,2,1,0:T(8,128)}, f32[2,4,80,128]{3,2,1,0:T(8,128)S(1)}, u32[]{:S(2)}, u32[]{:S(2)}) collective-permute-start(f32[2,4,80,128]{3,2,1,0:T(8,128)} %get-tuple-element.25), channel_id=1, source_target_pairs={{0,32},{32,64},{64,96},{96,128},{128,160},{160,192},{192,224},{1,3... | collective-permute-start | bytes 983048 | tf_op jit(solution)/shard_map/ppermute | solution.py:246
  22.9 14.2 %collective-permute-start.3 = (f32[2,4,80,128]{3,2,1,0:T(8,128)}, f32[2,4,80,128]{3,2,1,0:T(8,128)}, u32[]{:S(2)}, u32[]{:S(2)}) collective-permute-start(f32[2,4,80,128]{3,2,1,0:T(8,128)} %get-tuple-element.26), channel_id=1, source_target_pairs={{32,0},{64,32},{96,64},{128,96},{160,128},{192,160},{224,192},{33,... | collective-permute-start | bytes 983048 | tf_op jit(solution)/shard_map/ppermute | solution.py:246
  25.5 0.7 copy-start.9
  26.2 10.8 %copy-start.3 = (f32[256,256]{1,0:T(8,128)S(1)}, f32[256,256]{1,0:T(8,128)}, u32[]{:S(2)}) copy-start(f32[256,256]{1,0:T(8,128)} %probe_re.3) | copy-start | bytes 786436
  26.2 10.8 %copy-start.5 = (f32[256,256]{1,0:T(8,128)S(1)}, f32[256,256]{1,0:T(8,128)}, u32[]{:S(2)}) copy-start(f32[256,256]{1,0:T(8,128)} %probe_im.3) | copy-start | bytes 786436
  26.2 10.8 %copy-start.7 = (bf16[8,256,256]{2,1,0:T(8,128)(2,1)S(1)}, bf16[8,256,256]{2,1,0:T(8,128)(2,1)}, u32[]{:S(2)}) copy-start(bf16[8,256,256]{2,1,0:T(8,128)(2,1)} %constant.10.clone.tables) | copy-start | bytes 3145732
  45.8 7.5 %collective-permute-start.4 = (f32[2,4,80,128]{3,2,1,0:T(8,128)S(1)}, f32[2,4,80,128]{3,2,1,0:T(8,128)S(1)}, u32[]{:S(2)}, u32[]{:S(2)}) collective-permute-start(f32[2,4,80,128]{3,2,1,0:T(8,128)S(1)} %get-tuple-element.28), channel_id=1, source_target_pairs={{0,32},{32,64},{64,96},{96,128},{128,160},{160,192},{192,224},{1,3... | collective-permute-start | bytes 983048 | tf_op jit(solution)/shard_map/ppermute | solution.py:246
  47.8 10.9 %collective-permute-start.5 = (f32[2,4,80,128]{3,2,1,0:T(8,128)S(1)}, f32[2,4,80,128]{3,2,1,0:T(8,128)S(1)}, u32[]{:S(2)}, u32[]{:S(2)}) collective-permute-start(f32[2,4,80,128]{3,2,1,0:T(8,128)S(1)} %get-tuple-element.29), channel_id=1, source_target_pairs={{32,0},{64,32},{96,64},{128,96},{160,128},{192,160},{224,192},{33,... | collective-permute-start | bytes 983048 | tf_op jit(solution)/shard_map/ppermute | solution.py:246
  59.8 15.5 %collective-permute-start.6 = (f32[2,160,256]{2,1,0:T(8,128)}, f32[2,160,256]{2,1,0:T(8,128)S(1)}, u32[]{:S(2)}, u32[]{:S(2)}) collective-permute-start(f32[2,160,256]{2,1,0:T(8,128)} %get-tuple-element.31), channel_id=1, source_target_pairs={{0,1},{1,2},{2,3},{3,4},{4,5},{5,6},{6,7},{7,8},{8,9},{9,10},{10,1... | collective-permute-start | bytes 983048 | tf_op jit(solution)/shard_map/ppermute | solution.py:246
  65.1 14.3 %collective-permute-start.7 = (f32[2,160,256]{2,1,0:T(8,128)}, f32[2,160,256]{2,1,0:T(8,128)}, u32[]{:S(2)}, u32[]{:S(2)}) collective-permute-start(f32[2,160,256]{2,1,0:T(8,128)} %get-tuple-element.32), channel_id=1, source_target_pairs={{1,0},{2,1},{3,2},{4,3},{5,4},{6,5},{7,6},{8,7},{9,8},{10,9},{11,1... | collective-permute-start | bytes 983048 | tf_op jit(solution)/shard_map/ppermute | solution.py:246
  79.5 18.1 %copy-start.4 = (f32[256,256]{1,0:T(8,128)S(1)}, f32[256,256]{1,0:T(8,128)}, u32[]{:S(2)}) copy-start(f32[256,256]{1,0:T(8,128)} %probe_re.3) | copy-start | bytes 786436
  79.5 18.1 %copy-start.6 = (f32[256,256]{1,0:T(8,128)S(1)}, f32[256,256]{1,0:T(8,128)}, u32[]{:S(2)}) copy-start(f32[256,256]{1,0:T(8,128)} %probe_im.3) | copy-start | bytes 786436
  79.5 18.1 %copy-start.8 = (bf16[8,256,256]{2,1,0:T(8,128)(2,1)S(1)}, bf16[8,256,256]{2,1,0:T(8,128)(2,1)}, u32[]{:S(2)}) copy-start(bf16[8,256,256]{2,1,0:T(8,128)(2,1)} %constant.10.clone.tables) | copy-start | bytes 3145732
  80.9 7.8 %collective-permute-start.8 = (f32[2,4,80,128]{3,2,1,0:T(8,128)S(1)}, f32[2,4,80,128]{3,2,1,0:T(8,128)S(1)}, u32[]{:S(2)}, u32[]{:S(2)}) collective-permute-start(f32[2,4,80,128]{3,2,1,0:T(8,128)S(1)} %get-tuple-element.34), channel_id=1, source_target_pairs={{0,32},{32,64},{64,96},{96,128},{128,160},{160,192},{192,224},{1,3... | collective-permute-start | bytes 983048 | tf_op jit(solution)/shard_map/ppermute | solution.py:246
  83.7 13.8 %collective-permute-start.9 = (f32[2,4,80,128]{3,2,1,0:T(8,128)S(1)}, f32[2,4,80,128]{3,2,1,0:T(8,128)S(1)}, u32[]{:S(2)}, u32[]{:S(2)}) collective-permute-start(f32[2,4,80,128]{3,2,1,0:T(8,128)S(1)} %get-tuple-element.35), channel_id=1, source_target_pairs={{32,0},{64,32},{96,64},{128,96},{160,128},{192,160},{224,192},{33,... | collective-permute-start | bytes 983048 | tf_op jit(solution)/shard_map/ppermute | solution.py:246
  105.9 8.5 %collective-permute-start.10 = (f32[2,4,80,128]{3,2,1,0:T(8,128)S(1)}, f32[2,4,80,128]{3,2,1,0:T(8,128)S(1)}, u32[]{:S(2)}, u32[]{:S(2)}) collective-permute-start(f32[2,4,80,128]{3,2,1,0:T(8,128)S(1)} %get-tuple-element.37), channel_id=1, source_target_pairs={{0,32},{32,64},{64,96},{96,128},{128,160},{160,192},{192,224},{1,3... | collective-permute-start | bytes 983048 | tf_op jit(solution)/shard_map/ppermute | solution.py:246
  107.8 14.0 %collective-permute-start.11 = (f32[2,4,80,128]{3,2,1,0:T(8,128)S(1)}, f32[2,4,80,128]{3,2,1,0:T(8,128)S(1)}, u32[]{:S(2)}, u32[]{:S(2)}) collective-permute-start(f32[2,4,80,128]{3,2,1,0:T(8,128)S(1)} %get-tuple-element.38), channel_id=1, source_target_pairs={{32,0},{64,32},{96,64},{128,96},{160,128},{192,160},{224,192},{33,... | collective-permute-start | bytes 983048 | tf_op jit(solution)/shard_map/ppermute | solution.py:246
  122.0 9.6 %collective-permute-start.12 = (f32[2,80,256]{2,1,0:T(8,128)S(1)}, f32[2,80,256]{2,1,0:T(8,128)S(1)}, u32[]{:S(2)}, u32[]{:S(2)}) collective-permute-start(f32[2,80,256]{2,1,0:T(8,128)S(1)} %get-tuple-element.40), channel_id=1, source_target_pairs={{0,1},{1,2},{2,3},{3,4},{4,5},{5,6},{6,7},{7,8},{8,9},{9,10},{10,1... | collective-permute-start | bytes 491528 | tf_op jit(solution)/shard_map/ppermute | solution.py:246
  123.9 8.6 %collective-permute-start.13 = (f32[2,80,256]{2,1,0:T(8,128)S(1)}, f32[2,80,256]{2,1,0:T(8,128)S(1)}, u32[]{:S(2)}, u32[]{:S(2)}) collective-permute-start(f32[2,80,256]{2,1,0:T(8,128)S(1)} %get-tuple-element.41), channel_id=1, source_target_pairs={{1,0},{2,1},{3,2},{4,3},{5,4},{6,5},{7,6},{8,7},{9,8},{10,9},{11,1... | collective-permute-start | bytes 491528 | tf_op jit(solution)/shard_map/ppermute | solution.py:246
where the time goes:
time: 134 us
  waiting for transfers between devices  57.1 us (43%)
  starting transfers between devices  48.5 us (36%)
  Pallas kernels  23.5 us (18%)
  local copies, waits for them, and re-layouts  2.77 us (2%)
  between operations  1.48 us (1%)
    ppermute x7, waiting for transfers between devices, exchange(): lax.ppermute(to_before, axis, down)  34.8 us
    ppermute x7, starting transfers between devices, exchange(): lax.ppermute(to_after, axis, up)  24.8 us
    ppermute x7, starting transfers between devices, exchange(): lax.ppermute(to_before, axis, down)  23.7 us
    pallas_call x9, Pallas kernels, call(): pl.pallas_call(kernel, in_specs=specs, out_specs=jax.tree.map(lambda _: V...  23.5 us
    ppermute x7, waiting for transfers between devices, exchange(): lax.ppermute(to_after, axis, up)  22.4 us
    unnamed x20, local copies, waits for them, and re-layouts  2.68 us
  transfers between devices with their start and end apart: 14, of which 14 were waited for; matrix products, arithmetic and copies ran while one was open for 0% of the time, Pallas kernels for 1%

commit v1 on v0

v1 whole, which is shorter than its diff:
```python
import math

import jax
import jax.numpy as jnp
import numpy as np
from jax import lax
from jax.experimental import pallas as pl
from jax.experimental.pallas import tpu as pltpu
from jax.sharding import PartitionSpec as P

ITERS = 2

smoothing = 0.01
step_size = 0.25

W = 256
H = 128
REACH = 80
PART = W // 2 + REACH
HALF = PART + REACH

VMEM = pl.BlockSpec(memory_space=pltpu.VMEM)
SMEM = pl.BlockSpec(memory_space=pltpu.SMEM)
f32 = jnp.float32
bf16 = jnp.bfloat16


def shape(*dims):
    return jax.ShapeDtypeStruct(dims, f32)


def dft_tables():
    k = np.arange(H)[:, None]
    mats = []
    for odd in (0, 1):
        freq = 2 * np.arange(H)[None, :] + odd
        angle = -2.0 * math.pi * ((k * freq) % W) / W
        c, s = np.cos(angle) / 16.0, np.sin(angle) / 16.0
        mats.append(np.block([[c, s], [-s, c]]))
    mats = [mats[0], mats[1], mats[0].T, mats[1].T]
    out = []
    for m in mats:
        m = m.astype(np.float32)
        hi = m.astype(jnp.bfloat16)
        lo = (m - hi.astype(np.float32)).astype(jnp.bfloat16)
        out.extend([hi, lo])
    return np.stack(out)


def split(x):
    hi = x.astype(bf16)
    lo = (x - hi.astype(f32)).astype(bf16)
    return hi, lo


def dot(a, b):
    return lax.dot_general(a, b, (((1,), (0,)), ((), ())), preferred_element_type=f32)


def right(x, tables, i):
    hi, lo = split(x)
    t_hi, t_lo = tables[2 * i], tables[2 * i + 1]
    return dot(
        jnp.concatenate([hi, lo, hi], axis=1), jnp.concatenate([t_hi, t_hi, t_lo], axis=0)
    )


def left(tables, i, x):
    hi, lo = split(x)
    t_hi, t_lo = tables[2 * i], tables[2 * i + 1]
    return dot(
        jnp.concatenate([t_hi, t_hi, t_lo], axis=1), jnp.concatenate([hi, lo, hi], axis=0)
    )


def cat(a, b, axis):
    return jnp.concatenate([a, b], axis=axis)


def roots_kernel(intensity, out):
    row = lax.broadcasted_iota(jnp.int32, (W, W), 0)
    col = lax.broadcasted_iota(jnp.int32, (W, W), 1)
    source = jnp.where(col < H, 2 * col, 2 * (col - H) + 1)
    perm = jnp.where(row == source, 1.0, 0.0).astype(bf16)
    perm3 = jnp.concatenate([perm, perm, perm], axis=0)
    for p in range(out.shape[0]):
        x = jnp.sqrt(intensity[p])
        hi = x.astype(bf16)
        rest = x - hi.astype(f32)
        mid = rest.astype(bf16)
        lo = (rest - mid.astype(f32)).astype(bf16)
        y = dot(jnp.concatenate([hi, mid, lo], axis=1), perm3)
        y = y.reshape(H, 2, W)
        out[p, pl.ds(0, H), :] = y[:, 0, :]
        out[p, pl.ds(H, H), :] = y[:, 1, :]


def rows_at(start, size):
    return pl.ds(pl.multiple_of(start, 8), size)


def columns_for(flags, left, right, even, odd):
    flip = flags[0] == 1
    for comp in range(2):
        even[comp] = jnp.where(flip, left[comp], right[comp])
        odd[comp] = jnp.where(flip, right[comp], left[comp])


def columns_from(flags, even, odd, comp):
    flip = flags[0] == 1
    return jnp.where(flip, even[comp], odd[comp]), jnp.where(flip, odd[comp], even[comp])


def corners_for(flags, left, right, first, second):
    flip = flags[1] == 1
    for comp in range(2):
        first[comp] = jnp.where(flip, right[comp], left[comp])
        second[comp] = jnp.where(flip, left[comp], right[comp])


def corners_from(flags, first, second, comp):
    flip = flags[1] == 1
    return jnp.where(flip, second[comp], first[comp]), jnp.where(flip, first[comp], second[comp])


def send_object(flags, re, im, even, odd, off, first, second):
    rows = rows_at((W - REACH) * flags[1], REACH)
    left, right, c_left, c_right = [], [], [], []
    for comp, x in enumerate((re, im)):
        left.append(x[:, 0:H].T[:REACH])
        right.append(x[:, H:W].T[H - REACH :])
        c_left.append(x[rows, 0:H])
        c_right.append(x[rows, H:W])
        off[comp, 0] = c_left[comp]
        off[comp, 1] = c_right[comp]
    columns_for(flags, left, right, even, odd)
    corners_for(flags, c_left, c_right, first, second)


def sides_kernel(flags, re, im, even, odd, mid, on):
    blank = jnp.zeros((H - REACH, W), f32)
    for comp, x in enumerate((re, im)):
        from_left, from_right = columns_from(flags, even, odd, comp)
        mid[comp, 0] = cat(blank, from_left, 0).T
        mid[comp, 1] = x[:, 0:H]
        mid[comp, 2] = x[:, H:W]
        mid[comp, 3] = cat(from_right, blank, 0).T
    on[...] = mid[:, :, rows_at((W - REACH) * (1 - flags[1]), REACH), :]


def half_gradient(a, offsets, counts, roots, probe_re, probe_im, tables, ext, acc):
    acc[...] = jnp.zeros(acc.shape, f32)
    lane = lax.broadcasted_iota(jnp.int32, (W, H), 1)

    def position(base, carry):
        p = 2 * a + base
        shift = offsets[p, 1] - H * base
        rows = pl.ds(offsets[p, 0] - (H - REACH) - H * a, W)
        o = []
        for comp in range(2):
            rolled = [pltpu.roll(ext[comp, base + j, rows, :], H - shift, 1) for j in range(3)]
            o.append([jnp.where(lane < H - shift, rolled[j], rolled[j + 1]) for j in range(2)])
        w_re, w_im = [], []
        for j in range(2):
            p_re, p_im = probe_re[:, j * H : (j + 1) * H], probe_im[:, j * H : (j + 1) * H]
            w_re.append(o[0][j] * p_re - o[1][j] * p_im)
            w_im.append(o[0][j] * p_im + o[1][j] * p_re)
        e = right(cat(w_re[0] + w_re[1], w_im[0] + w_im[1], 1), tables, 0)
        d = right(cat(w_re[0] - w_re[1], w_im[0] - w_im[1], 1), tables, 1)
        h_re = cat(e[:, :H], d[:, :H], 1)
        h_im = cat(e[:, H:], d[:, H:], 1)
        far_e = left(tables, 2, cat(h_re[:H] + h_re[H:], h_im[:H] + h_im[H:], 0))
        far_d = left(tables, 3, cat(h_re[:H] - h_re[H:], h_im[:H] - h_im[H:], 0))

        def residual(far, root):
            power = far[:H] * far[:H] + far[H:] * far[H:] + smoothing
            factor = 1.0 - root * lax.rsqrt(power)
            return far * cat(factor, factor, 0)

        x = left(tables, 0, residual(far_e, roots[p, pl.ds(0, H), :]))
        y = left(tables, 1, residual(far_d, roots[p, pl.ds(H, H), :]))
        upper, lower = x + y, x - y
        h_re = cat(upper[:H], lower[:H], 0)
        h_im = cat(upper[H:], lower[H:], 0)
        x = right(cat(h_re[:, :H], h_im[:, :H], 1), tables, 2)
        y = right(cat(h_re[:, H:], h_im[:, H:], 1), tables, 3)
        weight = jnp.where(p < counts[0, 0], 1.0, 0.0).astype(f32)
        g_re, g_im = [], []
        for j, z in enumerate((x + y, x - y)):
            p_re, p_im = probe_re[:, j * H : (j + 1) * H], probe_im[:, j * H : (j + 1) * H]
            p_re, p_im = p_re * weight, p_im * weight
            g_re.append(z[:, :H] * p_re + z[:, H:] * p_im)
            g_im.append(z[:, H:] * p_re - z[:, :H] * p_im)
        for comp, g in enumerate((g_re, g_im)):
            r = [pltpu.roll(g[j], shift, 1) for j in range(2)]
            acc[comp, base, rows, :] += jnp.where(lane >= shift, r[0], 0.0)
            acc[comp, base + 1, rows, :] += jnp.where(lane >= shift, r[1], r[0])
            acc[comp, base + 2, rows, :] += jnp.where(lane < shift, r[1], 0.0)
        return carry

    lax.fori_loop(0, 2, position, 0)


def margin_rows(a):
    return rows_at(PART * a, REACH)


def own_rows(a):
    return rows_at(REACH - REACH * a, PART)


def covered_rows(a):
    return rows_at((W - PART) * a, PART)


def on_kernel(
    flags, offsets, counts, mid, from_on, roots, probe_re, probe_im, tables, part, to_on, ext, acc
):
    a = 1 - flags[1]
    ext[:, :, own_rows(a), :] = mid[:, :, covered_rows(a), :]
    ext[:, :, margin_rows(a), :] = from_on[...]
    half_gradient(a, offsets, counts, roots, probe_re, probe_im, tables, ext, acc)
    part[...] = acc[:, :, own_rows(a), :]
    to_on[...] = acc[:, :, margin_rows(a), :]


def off_kernel(
    flags, offsets, counts, mid, off, first, second, part, from_on, roots, probe_re, probe_im, tables,
    total, to_even, to_odd, to_off, to_first, to_second, ext, acc, centre,
):
    a = flags[1]
    ext[:, :, own_rows(a), :] = mid[:, :, covered_rows(a), :]
    margin = margin_rows(a)
    for comp in range(2):
        left, right = corners_from(flags, first, second, comp)
        ext[comp, 0, margin, :] = left
        ext[comp, 1, margin, :] = off[comp, 0]
        ext[comp, 2, margin, :] = off[comp, 1]
        ext[comp, 3, margin, :] = right
    half_gradient(a, offsets, counts, roots, probe_re, probe_im, tables, ext, acc)
    for j in range(2):
        to_off[:, j] = acc[:, 1 + j, margin, :]
    corners_for(
        flags, [acc[c, 0, margin, :] for c in range(2)], [acc[c, 3, margin, :] for c in range(2)],
        to_first, to_second,
    )
    centre[...] = jnp.zeros(centre.shape, f32)
    centre[:, :, covered_rows(1 - a), :] = part[...]
    centre[:, :, covered_rows(a), :] += acc[:, :, own_rows(a), :]
    centre[:, :, rows_at((W - REACH) * (1 - a), REACH), :] += from_on[...]
    left = [centre[c, 0].T[H - REACH :] for c in range(2)]
    right = [centre[c, 3].T[:REACH] for c in range(2)]
    columns_for(flags, left, right, to_even, to_odd)
    for j in range(2):
        total[:, j] = centre[:, 1 + j]


def step_kernel(flags, re, im, total, even, odd, off, first, second, out_re, out_im, *sends):
    *sends, work = sends
    blank = jnp.zeros((H - REACH, W), f32)
    rows = rows_at((W - REACH) * flags[1], REACH)
    for comp in range(2):
        from_left, from_right = columns_from(flags, even, odd, comp)
        work[comp, 0] = total[comp, 0] + cat(from_left, blank, 0).T
        work[comp, 1] = total[comp, 1] + cat(blank, from_right, 0).T
        corners = corners_from(flags, first, second, comp)
        for j in range(2):
            work[comp, j, rows, :] += off[comp, j] + corners[j]
    for comp, (x, out) in enumerate(((re, out_re), (im, out_im))):
        for j in range(2):
            out[:, j * H : (j + 1) * H] = x[:, j * H : (j + 1) * H] - step_size * work[comp, j]
    if sends:
        send_object(flags, out_re, out_im, *sends)


def call(kernel, scalars, out_shape, *args, scratch=(), flops=0, read=0):
    return pl.pallas_call(
        kernel,
        in_specs=[SMEM] * scalars + [VMEM] * (len(args) - scalars),
        out_specs=jax.tree.map(lambda _: VMEM, out_shape),
        out_shape=out_shape,
        scratch_shapes=scratch,
        compiler_params=pltpu.CompilerParams(vmem_limit_bytes=48 * 1024 * 1024),
        cost_estimate=pl.CostEstimate(flops=flops, bytes_accessed=read, transcendentals=0),
    )(*args)


def swaps(size, bit):
    return [p for i in range(bit, size - 1, 2) for p in ((i, i + 1), (i + 1, i))]


def exchange(even, odd, off, first, second):
    height, width = lax.axis_size("row"), lax.axis_size("col")
    diagonal = ([], [])
    for r in range(1, height - 1, 2):
        for c in range(width):
            for k, d in enumerate((c + 1, c - 1)):
                if 0 <= d < width:
                    diagonal[k].extend([(r * width + c, r * width + width + d), (r * width + width + d, r * width + c)])
    both = ("row", "col")
    moves = (
        (even, "col", swaps(width, 0)),
        (odd, "col", swaps(width, 1)),
        (off, "row", swaps(height, 1)),
        (first, both, diagonal[0]),
        (second, both, diagonal[1]),
    )
    got = []
    for x, axis, pairs in moves:
        got.append(lax.ppermute(x, axis, pairs))
    return got


def shards(object_re, object_im, probe_re, probe_im, intensity, offsets, counts):
    slots = intensity.shape[2]
    placed = offsets[0, 0]
    tables = jnp.asarray(dft_tables())
    flags = jnp.stack([lax.axis_index("col") % 2, lax.axis_index("row") % 2]).astype(jnp.int32)
    on_chip = swaps(lax.axis_size("row"), 0)

    tile = shape(W, W)
    strip = shape(2, REACH, W)
    corner = shape(2, REACH, H)
    sends = (strip, strip, shape(2, 2, REACH, H), corner, corner)
    rows = shape(2, 4, REACH, H)
    full = shape(2, 4, W, H)
    part = shape(2, 4, PART, H)
    halves = [pltpu.VMEM((2, 4, HALF, H), f32)] * 2
    fixed = (probe_re, probe_im, tables)

    re, im = object_re, object_im
    out = call(send_object, 1, sends, flags, re, im, read=1 << 20)
    roots = call(roots_kernel, 0, shape(slots, W, W), intensity[0, 0], flops=1 << 29, read=1 << 21)
    for sweep in range(ITERS):
        even, odd, off, first, second = exchange(*out)
        mid, on = call(sides_kernel, 1, (full, rows), flags, re, im, even, odd, read=1 << 21)
        from_on = lax.ppermute(on, "row", on_chip)
        upper, to_on = call(
            on_kernel, 3, (part, rows), flags, placed, counts, mid, from_on, roots, *fixed,
            scratch=halves, flops=1 << 31, read=1 << 22,
        )
        from_on = lax.ppermute(to_on, "row", on_chip)
        total, *back = call(
            off_kernel, 3, (shape(2, 2, W, H), *sends),
            flags, placed, counts, mid, off, first, second, upper, from_on, roots, *fixed,
            scratch=halves + [pltpu.VMEM((2, 4, W, H), f32)], flops=1 << 31, read=1 << 22,
        )
        back = exchange(*back)
        more = () if sweep == ITERS - 1 else sends
        re, im, *out = call(
            step_kernel, 1, (tile, tile, *more), flags, re, im, total, *back,
            scratch=[pltpu.VMEM((2, 2, W, H), f32)], read=1 << 21,
        )
    return re, im


def solution(mesh):
    return jax.shard_map(
        shards,
        mesh=mesh,
        in_specs=(
            P("row", "col"),
            P("row", "col"),
            P(),
            P(),
            P("row", "col", None, None, None),
            P("row", "col", None, None),
            P("row", "col"),
        ),
        out_specs=(P("row", "col"), P("row", "col")),
        check_vma=False,
    )
```

time: 134 us -> 142 us (1.060)
  starting transfers between devices: 48.5 us -> 76.7 us
  waiting for transfers between devices: 57.1 us -> 34.2 us
  Pallas kernels: 23.5 us -> 26.5 us
    ppermute x14 -> x24, starting transfers between devices: 48.5 us -> 76.7 us  [the longest x20 74.2 us: exchange(): got.append(lax.ppermute(x, axis, pairs))]
    ppermute x14 -> x24, waiting for transfers between devices: 57.1 us -> 34.2 us  [the longest x20 32.5 us: exchange(): got.append(lax.ppermute(x, axis, pairs))]
    pallas_call x9 -> x10, Pallas kernels: 23.5 us -> 26.5 us  [call(): pl.pallas_call(kernel, in_specs=[SMEM] * scalars + [VMEM] * (len(args) -...]
  transfers between devices with their start and end apart: 14 -> 24, of which waited for: 14 -> 12; matrix products, arithmetic and copies ran while one was open for 0% -> 0% of each run, Pallas kernels for 1% -> 1%
where the time goes in v1:
time: 142 us
  starting transfers between devices  76.7 us (54%)
  waiting for transfers between devices  34.2 us (24%)
  Pallas kernels  26.5 us (19%)
  local copies, waits for them, and re-layouts  2.7 us (2%)
  between operations  1.64 us (1%)
    ppermute x20, starting transfers between devices, exchange(): got.append(lax.ppermute(x, axis, pairs))  74.2 us
    ppermute x20, waiting for transfers between devices, exchange(): got.append(lax.ppermute(x, axis, pairs))  32.5 us
    pallas_call x10, Pallas kernels, call(): pl.pallas_call(kernel, in_specs=[SMEM] * scalars + [VMEM] * (len(args) -...  26.5 us
  transfers between devices with their start and end apart: 24, of which 12 were waited for; matrix products, arithmetic and copies ran while one was open for 0% of the time, Pallas kernels for 1%

profile of v1, /device:TPU:69, one launch (start us, length us, event | category | flops | bytes accessed | tf_op | source)
XLA Modules:
  0.0 141.7 jit_solution(16084190711492910369)
XLA Ops:
  0.7 0.9 copy-done
  1.7 0.9 copy-done.2
  2.6 0.7 shard_map.95
  3.4 1.7 %collective-permute-start = (f32[2,80,256]{2,1,0:T(8,128)S(1)}, f32[2,80,256]{2,1,0:T(8,128)S(1)}, u32[]{:S(2)}, u32[]{:S(2)}) collective-permute-start(f32[2,80,256]{2,1,0:T(8,128)S(1)} %get-tuple-element.34), channel_id=1, source_target_pairs={{0,1},{1,0},{2,3},{3,2},{4,5},{5,4},{6,7},{7,6},{8,9},{9,8},{10,11... | collective-permute-start | bytes 491528 | tf_op jit(solution)/shard_map/ppermute | solution.py:310
  5.1 4.3 %collective-permute-start.1 = (f32[2,80,256]{2,1,0:T(8,128)S(1)}, f32[2,80,256]{2,1,0:T(8,128)S(1)}, u32[]{:S(2)}, u32[]{:S(2)}) collective-permute-start(f32[2,80,256]{2,1,0:T(8,128)S(1)} %get-tuple-element.35), channel_id=1, source_target_pairs={{1,2},{2,1},{3,4},{4,3},{5,6},{6,5},{7,8},{8,7},{9,10},{10,9},{11,... | collective-permute-start | bytes 491528 | tf_op jit(solution)/shard_map/ppermute | solution.py:310
  9.5 5.3 %collective-permute-done.1.odd = f32[2,80,256]{2,1,0:T(8,128)S(1)} collective-permute-done((f32[2,80,256]{2,1,0:T(8,128)S(1)}, f32[2,80,256]{2,1,0:T(8,128)S(1)}, u32[]{:S(2)}, u32[]{:S(2)}) %collective-permute-start.1) | collective-permute-done | bytes 163872 | tf_op jit(solution)/shard_map/ppermute | solution.py:310
  14.8 0.8 shard_map.96
  15.6 1.9 %collective-permute-start.5 = (f32[2,4,80,128]{3,2,1,0:T(8,128)S(1)}, f32[2,4,80,128]{3,2,1,0:T(8,128)S(1)}, u32[]{:S(2)}, u32[]{:S(2)}) collective-permute-start(f32[2,4,80,128]{3,2,1,0:T(8,128)S(1)} %get-tuple-element.40), channel_id=1, source_target_pairs={{0,32},{32,0},{64,96},{96,64},{128,160},{160,128},{192,224},{224,1... | collective-permute-start | bytes 983048 | tf_op jit(solution)/shard_map/ppermute | solution.py:337
  18.1 0.7 copy-done.9
  18.9 1.5 %shard_map.97.roots = f32[4,256,256]{2,1,0:T(8,128)S(1)} custom-call(f32[4,256,256]{2,1,0:T(8,128)S(1)} %bitcast.4), custom_call_target="tpu_custom_call" | custom-call | flops 536870912 | bytes 2097152 | tf_op jit(solution)/shard_map/pallas_call | solution.py:277
  20.5 4.5 %shard_map.98 = (f32[2,4,208,128]{3,2,1,0:T(8,128)S(1)}, f32[2,4,80,128]{3,2,1,0:T(8,128)S(1)}) custom-call(s32[2]{0:T(128)S(1)} %pad_add_fusion.flags, s32[4,2]{1,0:T(4,128)S(1)} %copy.11.offsets, s32[1,1]{1,0:T(1,128)S(6)} %copy.14.counts, f32[2,4,256,128]{3,2,1,0:T(8,128)S(1)} %get-tuple-element.36.mid, ...), custom_call_target="tpu_custom_call" | custom-call | flops 2147483648 | bytes 4194304 | tf_op jit(solution)/shard_map/pallas_call | solution.py:277
  25.0 0.1 collective-permute-start.6
  25.1 5.9 %collective-permute-start.2 = (f32[2,2,80,128]{3,2,1,0:T(8,128)S(1)}, f32[2,2,80,128]{3,2,1,0:T(8,128)S(1)}, u32[]{:S(2)}, u32[]{:S(2)}) collective-permute-start(f32[2,2,80,128]{3,2,1,0:T(8,128)S(1)} %get-tuple-element.37), channel_id=1, source_target_pairs={{32,64},{64,32},{96,128},{128,96},{160,192},{192,160},{33,65},{65,... | collective-permute-start | bytes 491528 | tf_op jit(solution)/shard_map/ppermute | solution.py:310
  31.0 1.9 %collective-permute-start.3 = (f32[2,80,128]{2,1,0:T(8,128)S(1)}, f32[2,80,128]{2,1,0:T(8,128)S(1)}, u32[]{:S(2)}, u32[]{:S(2)}) collective-permute-start(f32[2,80,128]{2,1,0:T(8,128)S(1)} %get-tuple-element.38), channel_id=1, source_target_pairs={{32,65},{65,32},{33,66},{66,33},{34,67},{67,34},{35,68},{68,35},{3... | collective-permute-start | bytes 245768 | tf_op jit(solution)/shard_map/ppermute | solution.py:310
  32.9 6.8 %collective-permute-start.4 = (f32[2,80,128]{2,1,0:T(8,128)S(1)}, f32[2,80,128]{2,1,0:T(8,128)S(1)}, u32[]{:S(2)}, u32[]{:S(2)}) collective-permute-start(f32[2,80,128]{2,1,0:T(8,128)S(1)} %get-tuple-element.39), channel_id=1, source_target_pairs={{33,64},{64,33},{34,65},{65,34},{35,66},{66,35},{36,67},{67,36},{3... | collective-permute-start | bytes 245768 | tf_op jit(solution)/shard_map/ppermute | solution.py:310
  39.8 0.6 collective-permute-done.3.first
  40.4 5.0 %collective-permute-done.4.second = f32[2,80,128]{2,1,0:T(8,128)S(1)} collective-permute-done((f32[2,80,128]{2,1,0:T(8,128)S(1)}, f32[2,80,128]{2,1,0:T(8,128)S(1)}, u32[]{:S(2)}, u32[]{:S(2)}) %collective-permute-start.4) | collective-permute-done | bytes 81952 | tf_op jit(solution)/shard_map/ppermute | solution.py:310
  45.5 5.5 %shard_map.99 = (f32[2,2,256,128]{3,2,1,0:T(8,128)S(1)}, f32[2,80,256]{2,1,0:T(8,128)S(1)}, f32[2,80,256]{2,1,0:T(8,128)S(1)}, f32[2,2,80,128]{3,2,1,0:T(8,128)S...) custom-call(s32[2]{0:T(128)S(1)} %pad_add_fusion.flags, s32[4,2]{1,0:T(4,128)S(1)} %copy.11.offsets, ...), custom_call_target="tpu_custom_call" | custom-call | flops 2147483648 | bytes 4194304 | tf_op jit(solution)/shard_map/pallas_call | solution.py:277
  51.0 0.1 collective-permute-start.7
  51.1 3.3 %collective-permute-start.8 = (f32[2,80,256]{2,1,0:T(8,128)S(1)}, f32[2,80,256]{2,1,0:T(8,128)S(1)}, u32[]{:S(2)}, u32[]{:S(2)}) collective-permute-start(f32[2,80,256]{2,1,0:T(8,128)S(1)} %get-tuple-element.45), channel_id=1, source_target_pairs={{1,2},{2,1},{3,4},{4,3},{5,6},{6,5},{7,8},{8,7},{9,10},{10,9},{11,... | collective-permute-start | bytes 491528 | tf_op jit(solution)/shard_map/ppermute | solution.py:310
  54.4 5.4 %collective-permute-start.9 = (f32[2,2,80,128]{3,2,1,0:T(8,128)S(1)}, f32[2,2,80,128]{3,2,1,0:T(8,128)S(1)}, u32[]{:S(2)}, u32[]{:S(2)}) collective-permute-start(f32[2,2,80,128]{3,2,1,0:T(8,128)S(1)} %get-tuple-element.46), channel_id=1, source_target_pairs={{32,64},{64,32},{96,128},{128,96},{160,192},{192,160},{33,65},{65,... | collective-permute-start | bytes 491528 | tf_op jit(solution)/shard_map/ppermute | solution.py:310
  59.8 2.1 %collective-permute-start.10 = (f32[2,80,128]{2,1,0:T(8,128)S(1)}, f32[2,80,128]{2,1,0:T(8,128)S(1)}, u32[]{:S(2)}, u32[]{:S(2)}) collective-permute-start(f32[2,80,128]{2,1,0:T(8,128)S(1)} %get-tuple-element.47), channel_id=1, source_target_pairs={{32,65},{65,32},{33,66},{66,33},{34,67},{67,34},{35,68},{68,35},{3... | collective-permute-start | bytes 245768 | tf_op jit(solution)/shard_map/ppermute | solution.py:310
  61.9 6.5 %collective-permute-start.11 = (f32[2,80,128]{2,1,0:T(8,128)S(1)}, f32[2,80,128]{2,1,0:T(8,128)S(1)}, u32[]{:S(2)}, u32[]{:S(2)}) collective-permute-start(f32[2,80,128]{2,1,0:T(8,128)S(1)} %get-tuple-element.48), channel_id=1, source_target_pairs={{33,64},{64,33},{34,65},{65,34},{35,66},{66,35},{36,67},{67,36},{3... | collective-permute-start | bytes 245768 | tf_op jit(solution)/shard_map/ppermute | solution.py:310
  68.4 0.5 collective-permute-done.10.first
  68.9 4.8 %collective-permute-done.11.second = f32[2,80,128]{2,1,0:T(8,128)S(1)} collective-permute-done((f32[2,80,128]{2,1,0:T(8,128)S(1)}, f32[2,80,128]{2,1,0:T(8,128)S(1)}, u32[]{:S(2)}, u32[]{:S(2)}) %collective-permute-start.11) | collective-permute-done | bytes 81952 | tf_op jit(solution)/shard_map/ppermute | solution.py:310
  73.7 1.0 shard_map.100
  74.7 0.1 collective-permute-start.12
  74.8 4.3 %collective-permute-start.13 = (f32[2,80,256]{2,1,0:T(8,128)S(1)}, f32[2,80,256]{2,1,0:T(8,128)S(1)}, u32[]{:S(2)}, u32[]{:S(2)}) collective-permute-start(f32[2,80,256]{2,1,0:T(8,128)S(1)} %get-tuple-element.52), channel_id=1, source_target_pairs={{1,2},{2,1},{3,4},{4,3},{5,6},{6,5},{7,8},{8,7},{9,10},{10,9},{11,... | collective-permute-start | bytes 491528 | tf_op jit(solution)/shard_map/ppermute | solution.py:310
  79.1 0.2 collective-permute-done.12.even
  79.3 4.6 %collective-permute-done.13.odd = f32[2,80,256]{2,1,0:T(8,128)S(1)} collective-permute-done((f32[2,80,256]{2,1,0:T(8,128)S(1)}, f32[2,80,256]{2,1,0:T(8,128)S(1)}, u32[]{:S(2)}, u32[]{:S(2)}) %collective-permute-start.13) | collective-permute-done | bytes 163872 | tf_op jit(solution)/shard_map/ppermute | solution.py:310
  83.9 0.8 shard_map.101
  84.7 0.1 collective-permute-start.17
  84.8 1.6 %collective-permute-done.17.from_on = f32[2,4,80,128]{3,2,1,0:T(8,128)S(1)} collective-permute-done((f32[2,4,80,128]{3,2,1,0:T(8,128)S(1)}, f32[2,4,80,128]{3,2,1,0:T(8,128)S(1)}, u32[]{:S(2)}, u32[]{:S(2)}) %collective-permute-start.17) | collective-permute-done | bytes 327712 | tf_op jit(solution)/shard_map/ppermute | solution.py:337
  86.4 4.5 %shard_map.102 = (f32[2,4,208,128]{3,2,1,0:T(8,128)S(1)}, f32[2,4,80,128]{3,2,1,0:T(8,128)S(1)}) custom-call(s32[2]{0:T(128)S(1)} %pad_add_fusion.flags, s32[4,2]{1,0:T(4,128)S(1)} %copy.11.offsets, s32[1,1]{1,0:T(1,128)S(6)} %copy.14.counts, f32[2,4,256,128]{3,2,1,0:T(8,128)S(1)} %get-tuple-element.53.mid, ...), custom_call_target="tpu_custom_call" | custom-call | flops 2147483648 | bytes 4194304 | tf_op jit(solution)/shard_map/pallas_call | solution.py:277
  90.9 0.4 collective-permute-start.18
  91.3 7.0 %collective-permute-start.14 = (f32[2,2,80,128]{3,2,1,0:T(8,128)S(1)}, f32[2,2,80,128]{3,2,1,0:T(8,128)S(1)}, u32[]{:S(2)}, u32[]{:S(2)}) collective-permute-start(f32[2,2,80,128]{3,2,1,0:T(8,128)S(1)} %get-tuple-element.54), channel_id=1, source_target_pairs={{32,64},{64,32},{96,128},{128,96},{160,192},{192,160},{33,65},{65,... | collective-permute-start | bytes 491528 | tf_op jit(solution)/shard_map/ppermute | solution.py:310
  98.3 1.9 %collective-permute-start.15 = (f32[2,80,128]{2,1,0:T(8,128)S(1)}, f32[2,80,128]{2,1,0:T(8,128)S(1)}, u32[]{:S(2)}, u32[]{:S(2)}) collective-permute-start(f32[2,80,128]{2,1,0:T(8,128)S(1)} %get-tuple-element.55), channel_id=1, source_target_pairs={{32,65},{65,32},{33,66},{66,33},{34,67},{67,34},{35,68},{68,35},{3... | collective-permute-start | bytes 245768 | tf_op jit(solution)/shard_map/ppermute | solution.py:310
  100.2 5.9 %collective-permute-start.16 = (f32[2,80,128]{2,1,0:T(8,128)S(1)}, f32[2,80,128]{2,1,0:T(8,128)S(1)}, u32[]{:S(2)}, u32[]{:S(2)}) collective-permute-start(f32[2,80,128]{2,1,0:T(8,128)S(1)} %get-tuple-element.56), channel_id=1, source_target_pairs={{33,64},{64,33},{34,65},{65,34},{35,66},{66,35},{36,67},{67,36},{3... | collective-permute-start | bytes 245768 | tf_op jit(solution)/shard_map/ppermute | solution.py:310
  106.1 1.9 %collective-permute-done.15.first = f32[2,80,128]{2,1,0:T(8,128)S(1)} collective-permute-done((f32[2,80,128]{2,1,0:T(8,128)S(1)}, f32[2,80,128]{2,1,0:T(8,128)S(1)}, u32[]{:S(2)}, u32[]{:S(2)}) %collective-permute-start.15) | collective-permute-done | bytes 81952 | tf_op jit(solution)/shard_map/ppermute | solution.py:310
  108.0 4.0 %collective-permute-done.16.second = f32[2,80,128]{2,1,0:T(8,128)S(1)} collective-permute-done((f32[2,80,128]{2,1,0:T(8,128)S(1)}, f32[2,80,128]{2,1,0:T(8,128)S(1)}, u32[]{:S(2)}, u32[]{:S(2)}) %collective-permute-start.16) | collective-permute-done | bytes 81952 | tf_op jit(solution)/shard_map/ppermute | solution.py:310
  112.0 5.5 %shard_map.103 = (f32[2,2,256,128]{3,2,1,0:T(8,128)S(1)}, f32[2,80,256]{2,1,0:T(8,128)S(1)}, f32[2,80,256]{2,1,0:T(8,128)S(1)}, f32[2,2,80,128]{3,2,1,0:T(8,128)...) custom-call(s32[2]{0:T(128)S(1)} %pad_add_fusion.flags, s32[4,2]{1,0:T(4,128)S(1)} %copy.11.offsets, ...), custom_call_target="tpu_custom_call" | custom-call | flops 2147483648 | bytes 4194304 | tf_op jit(solution)/shard_map/pallas_call | solution.py:277
  117.6 2.1 %collective-permute-start.20 = (f32[2,80,256]{2,1,0:T(8,128)S(1)}, f32[2,80,256]{2,1,0:T(8,128)S(1)}, u32[]{:S(2)}, u32[]{:S(2)}) collective-permute-start(f32[2,80,256]{2,1,0:T(8,128)S(1)} %get-tuple-element.62), channel_id=1, source_target_pairs={{1,2},{2,1},{3,4},{4,3},{5,6},{6,5},{7,8},{8,7},{9,10},{10,9},{11,... | collective-permute-start | bytes 491528 | tf_op jit(solution)/shard_map/ppermute | solution.py:310
  119.7 6.3 %collective-permute-start.21 = (f32[2,2,80,128]{3,2,1,0:T(8,128)S(1)}, f32[2,2,80,128]{3,2,1,0:T(8,128)S(1)}, u32[]{:S(2)}, u32[]{:S(2)}) collective-permute-start(f32[2,2,80,128]{3,2,1,0:T(8,128)S(1)} %get-tuple-element.63), channel_id=1, source_target_pairs={{32,64},{64,32},{96,128},{128,96},{160,192},{192,160},{33,65},{65,... | collective-permute-start | bytes 491528 | tf_op jit(solution)/shard_map/ppermute | solution.py:310
  126.0 2.4 %collective-permute-start.22 = (f32[2,80,128]{2,1,0:T(8,128)S(1)}, f32[2,80,128]{2,1,0:T(8,128)S(1)}, u32[]{:S(2)}, u32[]{:S(2)}) collective-permute-start(f32[2,80,128]{2,1,0:T(8,128)S(1)} %get-tuple-element.64), channel_id=1, source_target_pairs={{32,65},{65,32},{33,66},{66,33},{34,67},{67,34},{35,68},{68,35},{3... | collective-permute-start | bytes 245768 | tf_op jit(solution)/shard_map/ppermute | solution.py:310
  128.4 6.2 %collective-permute-start.23 = (f32[2,80,128]{2,1,0:T(8,128)S(1)}, f32[2,80,128]{2,1,0:T(8,128)S(1)}, u32[]{:S(2)}, u32[]{:S(2)}) collective-permute-start(f32[2,80,128]{2,1,0:T(8,128)S(1)} %get-tuple-element.65), channel_id=1, source_target_pairs={{33,64},{64,33},{34,65},{65,34},{35,66},{66,35},{36,67},{67,36},{3... | collective-permute-start | bytes 245768 | tf_op jit(solution)/shard_map/ppermute | solution.py:310
  134.6 0.3 collective-permute-done.22.first
  134.8 5.3 %collective-permute-done.23.second = f32[2,80,128]{2,1,0:T(8,128)S(1)} collective-permute-done((f32[2,80,128]{2,1,0:T(8,128)S(1)}, f32[2,80,128]{2,1,0:T(8,128)S(1)}, u32[]{:S(2)}, u32[]{:S(2)}) %collective-permute-start.23) | collective-permute-done | bytes 81952 | tf_op jit(solution)/shard_map/ppermute | solution.py:310
  140.1 1.6 %shard_map.104 = (f32[256,256]{1,0:T(8,128)}, f32[256,256]{1,0:T(8,128)}) custom-call(s32[2]{0:T(128)S(1)} %pad_add_fusion.flags, f32[256,256]{1,0:T(8,128)S(1)} %get-tuple-element.49.re, f32[256,256]{1,0:T(8,128)S(1)} %get-tuple-element.50.im, f32[2,2,256,128]{3,2,1,0:T(8,128)S(1)} %get-tuple-element.60.total, ...), custom_call_target="tpu_custom_call" | custom-call | bytes 2097152 | tf_op jit(solution)/shard_map/pallas_call | solution.py:277
  (32 shorter events, 0.3 us)
Async XLA Ops:
  0.7 1.0 copy-start
  1.7 0.9 copy-start.2
  2.6 16.3 %copy-start.4 = (f32[1,1,4,256,256]{4,3,2,1,0:T(8,128)S(1)}, f32[1,1,4,256,256]{4,3,2,1,0:T(8,128)}, u32[]{:S(2)}) copy-start(f32[1,1,4,256,256]{4,3,2,1,0:T(8,128)} %param.12) | copy-start | bytes 3145732
  3.4 6.1 %collective-permute-start = (f32[2,80,256]{2,1,0:T(8,128)S(1)}, f32[2,80,256]{2,1,0:T(8,128)S(1)}, u32[]{:S(2)}, u32[]{:S(2)}) collective-permute-start(f32[2,80,256]{2,1,0:T(8,128)S(1)} %get-tuple-element.34), channel_id=1, source_target_pairs={{0,1},{1,0},{2,3},{3,2},{4,5},{5,4},{6,7},{7,6},{8,9},{9,8},{10,11... | collective-permute-start | bytes 491528 | tf_op jit(solution)/shard_map/ppermute | solution.py:310
  5.1 9.7 %collective-permute-start.1 = (f32[2,80,256]{2,1,0:T(8,128)S(1)}, f32[2,80,256]{2,1,0:T(8,128)S(1)}, u32[]{:S(2)}, u32[]{:S(2)}) collective-permute-start(f32[2,80,256]{2,1,0:T(8,128)S(1)} %get-tuple-element.35), channel_id=1, source_target_pairs={{1,2},{2,1},{3,4},{4,3},{5,6},{6,5},{7,8},{8,7},{9,10},{10,9},{11,... | collective-permute-start | bytes 491528 | tf_op jit(solution)/shard_map/ppermute | solution.py:310
  15.6 4.9 %collective-permute-start.5 = (f32[2,4,80,128]{3,2,1,0:T(8,128)S(1)}, f32[2,4,80,128]{3,2,1,0:T(8,128)S(1)}, u32[]{:S(2)}, u32[]{:S(2)}) collective-permute-start(f32[2,4,80,128]{3,2,1,0:T(8,128)S(1)} %get-tuple-element.40), channel_id=1, source_target_pairs={{0,32},{32,0},{64,96},{96,64},{128,160},{160,128},{192,224},{224,1... | collective-permute-start | bytes 983048 | tf_op jit(solution)/shard_map/ppermute | solution.py:337
  18.1 0.7 copy-start.9
  18.9 1.6 %copy-start.5 = (f32[256,256]{1,0:T(8,128)S(1)}, f32[256,256]{1,0:T(8,128)}, u32[]{:S(2)}) copy-start(f32[256,256]{1,0:T(8,128)} %probe_re.7) | copy-start | bytes 786436
  18.9 1.6 %copy-start.6 = (f32[256,256]{1,0:T(8,128)S(1)}, f32[256,256]{1,0:T(8,128)}, u32[]{:S(2)}) copy-start(f32[256,256]{1,0:T(8,128)} %probe_im.7) | copy-start | bytes 786436
  18.9 1.6 %copy-start.7 = (bf16[8,256,256]{2,1,0:T(8,128)(2,1)S(1)}, bf16[8,256,256]{2,1,0:T(8,128)(2,1)}, u32[]{:S(2)}) copy-start(bf16[8,256,256]{2,1,0:T(8,128)(2,1)} %constant.28.clone.tables) | copy-start | bytes 3145732
  25.0 20.4 %collective-permute-start.6 = (f32[2,4,80,128]{3,2,1,0:T(8,128)S(1)}, f32[2,4,80,128]{3,2,1,0:T(8,128)S(1)}, u32[]{:S(2)}, u32[]{:S(2)}) collective-permute-start(f32[2,4,80,128]{3,2,1,0:T(8,128)S(1)} %get-tuple-element.42), channel_id=1, source_target_pairs={{0,32},{32,0},{64,96},{96,64},{128,160},{160,128},{192,224},{224,1... | collective-permute-start | bytes 983048 | tf_op jit(solution)/shard_map/ppermute | solution.py:342
  25.1 20.3 %collective-permute-start.2 = (f32[2,2,80,128]{3,2,1,0:T(8,128)S(1)}, f32[2,2,80,128]{3,2,1,0:T(8,128)S(1)}, u32[]{:S(2)}, u32[]{:S(2)}) collective-permute-start(f32[2,2,80,128]{3,2,1,0:T(8,128)S(1)} %get-tuple-element.37), channel_id=1, source_target_pairs={{32,64},{64,32},{96,128},{128,96},{160,192},{192,160},{33,65},{65,... | collective-permute-start | bytes 491528 | tf_op jit(solution)/shard_map/ppermute | solution.py:310
  31.0 9.4 %collective-permute-start.3 = (f32[2,80,128]{2,1,0:T(8,128)S(1)}, f32[2,80,128]{2,1,0:T(8,128)S(1)}, u32[]{:S(2)}, u32[]{:S(2)}) collective-permute-start(f32[2,80,128]{2,1,0:T(8,128)S(1)} %get-tuple-element.38), channel_id=1, source_target_pairs={{32,65},{65,32},{33,66},{66,33},{34,67},{67,34},{35,68},{68,35},{3... | collective-permute-start | bytes 245768 | tf_op jit(solution)/shard_map/ppermute | solution.py:310
  32.9 12.5 %collective-permute-start.4 = (f32[2,80,128]{2,1,0:T(8,128)S(1)}, f32[2,80,128]{2,1,0:T(8,128)S(1)}, u32[]{:S(2)}, u32[]{:S(2)}) collective-permute-start(f32[2,80,128]{2,1,0:T(8,128)S(1)} %get-tuple-element.39), channel_id=1, source_target_pairs={{33,64},{64,33},{34,65},{65,34},{35,66},{66,35},{36,67},{67,36},{3... | collective-permute-start | bytes 245768 | tf_op jit(solution)/shard_map/ppermute | solution.py:310
  45.5 28.2 %copy-start.1 = (f32[256,256]{1,0:T(8,128)S(1)}, f32[256,256]{1,0:T(8,128)}, u32[]{:S(2)}) copy-start(f32[256,256]{1,0:T(8,128)} %re.5) | copy-start | bytes 786436
  45.5 28.2 %copy-start.3 = (f32[256,256]{1,0:T(8,128)S(1)}, f32[256,256]{1,0:T(8,128)}, u32[]{:S(2)}) copy-start(f32[256,256]{1,0:T(8,128)} %im.5) | copy-start | bytes 786436
  51.0 22.7 %collective-permute-start.7 = (f32[2,80,256]{2,1,0:T(8,128)S(1)}, f32[2,80,256]{2,1,0:T(8,128)S(1)}, u32[]{:S(2)}, u32[]{:S(2)}) collective-permute-start(f32[2,80,256]{2,1,0:T(8,128)S(1)} %get-tuple-element.44), channel_id=1, source_target_pairs={{0,1},{1,0},{2,3},{3,2},{4,5},{5,4},{6,7},{7,6},{8,9},{9,8},{10,11... | collective-permute-start | bytes 491528 | tf_op jit(solution)/shard_map/ppermute | solution.py:310
  51.1 22.6 %collective-permute-start.8 = (f32[2,80,256]{2,1,0:T(8,128)S(1)}, f32[2,80,256]{2,1,0:T(8,128)S(1)}, u32[]{:S(2)}, u32[]{:S(2)}) collective-permute-start(f32[2,80,256]{2,1,0:T(8,128)S(1)} %get-tuple-element.45), channel_id=1, source_target_pairs={{1,2},{2,1},{3,4},{4,3},{5,6},{6,5},{7,8},{8,7},{9,10},{10,9},{11,... | collective-permute-start | bytes 491528 | tf_op jit(solution)/shard_map/ppermute | solution.py:310
  54.4 19.3 %collective-permute-start.9 = (f32[2,2,80,128]{3,2,1,0:T(8,128)S(1)}, f32[2,2,80,128]{3,2,1,0:T(8,128)S(1)}, u32[]{:S(2)}, u32[]{:S(2)}) collective-permute-start(f32[2,2,80,128]{3,2,1,0:T(8,128)S(1)} %get-tuple-element.46), channel_id=1, source_target_pairs={{32,64},{64,32},{96,128},{128,96},{160,192},{192,160},{33,65},{65,... | collective-permute-start | bytes 491528 | tf_op jit(solution)/shard_map/ppermute | solution.py:310
  59.8 9.0 %collective-permute-start.10 = (f32[2,80,128]{2,1,0:T(8,128)S(1)}, f32[2,80,128]{2,1,0:T(8,128)S(1)}, u32[]{:S(2)}, u32[]{:S(2)}) collective-permute-start(f32[2,80,128]{2,1,0:T(8,128)S(1)} %get-tuple-element.47), channel_id=1, source_target_pairs={{32,65},{65,32},{33,66},{66,33},{34,67},{67,34},{35,68},{68,35},{3... | collective-permute-start | bytes 245768 | tf_op jit(solution)/shard_map/ppermute | solution.py:310
  61.9 11.8 %collective-permute-start.11 = (f32[2,80,128]{2,1,0:T(8,128)S(1)}, f32[2,80,128]{2,1,0:T(8,128)S(1)}, u32[]{:S(2)}, u32[]{:S(2)}) collective-permute-start(f32[2,80,128]{2,1,0:T(8,128)S(1)} %get-tuple-element.48), channel_id=1, source_target_pairs={{33,64},{64,33},{34,65},{65,34},{35,66},{66,35},{36,67},{67,36},{3... | collective-permute-start | bytes 245768 | tf_op jit(solution)/shard_map/ppermute | solution.py:310
  73.7 12.7 %copy-start.8 = (bf16[8,256,256]{2,1,0:T(8,128)(2,1)S(1)}, bf16[8,256,256]{2,1,0:T(8,128)(2,1)}, u32[]{:S(2)}) copy-start(bf16[8,256,256]{2,1,0:T(8,128)(2,1)} %constant.28.clone.tables) | copy-start | bytes 3145732
  74.7 4.6 %collective-permute-start.12 = (f32[2,80,256]{2,1,0:T(8,128)S(1)}, f32[2,80,256]{2,1,0:T(8,128)S(1)}, u32[]{:S(2)}, u32[]{:S(2)}) collective-permute-start(f32[2,80,256]{2,1,0:T(8,128)S(1)} %get-tuple-element.51), channel_id=1, source_target_pairs={{0,1},{1,0},{2,3},{3,2},{4,5},{5,4},{6,7},{7,6},{8,9},{9,8},{10,11... | collective-permute-start | bytes 491528 | tf_op jit(solution)/shard_map/ppermute | solution.py:310
  74.8 9.1 %collective-permute-start.13 = (f32[2,80,256]{2,1,0:T(8,128)S(1)}, f32[2,80,256]{2,1,0:T(8,128)S(1)}, u32[]{:S(2)}, u32[]{:S(2)}) collective-permute-start(f32[2,80,256]{2,1,0:T(8,128)S(1)} %get-tuple-element.52), channel_id=1, source_target_pairs={{1,2},{2,1},{3,4},{4,3},{5,6},{6,5},{7,8},{8,7},{9,10},{10,9},{11,... | collective-permute-start | bytes 491528 | tf_op jit(solution)/shard_map/ppermute | solution.py:310
  84.7 1.7 %collective-permute-start.17 = (f32[2,4,80,128]{3,2,1,0:T(8,128)S(1)}, f32[2,4,80,128]{3,2,1,0:T(8,128)S(1)}, u32[]{:S(2)}, u32[]{:S(2)}) collective-permute-start(f32[2,4,80,128]{3,2,1,0:T(8,128)S(1)} %get-tuple-element.57), channel_id=1, source_target_pairs={{0,32},{32,0},{64,96},{96,64},{128,160},{160,128},{192,224},{224,1... | collective-permute-start | bytes 983048 | tf_op jit(solution)/shard_map/ppermute | solution.py:337
  90.9 21.1 %collective-permute-start.18 = (f32[2,4,80,128]{3,2,1,0:T(8,128)S(1)}, f32[2,4,80,128]{3,2,1,0:T(8,128)S(1)}, u32[]{:S(2)}, u32[]{:S(2)}) collective-permute-start(f32[2,4,80,128]{3,2,1,0:T(8,128)S(1)} %get-tuple-element.59), channel_id=1, source_target_pairs={{0,32},{32,0},{64,96},{96,64},{128,160},{160,128},{192,224},{224,1... | collective-permute-start | bytes 983048 | tf_op jit(solution)/shard_map/ppermute | solution.py:342
  91.3 20.7 %collective-permute-start.14 = (f32[2,2,80,128]{3,2,1,0:T(8,128)S(1)}, f32[2,2,80,128]{3,2,1,0:T(8,128)S(1)}, u32[]{:S(2)}, u32[]{:S(2)}) collective-permute-start(f32[2,2,80,128]{3,2,1,0:T(8,128)S(1)} %get-tuple-element.54), channel_id=1, source_target_pairs={{32,64},{64,32},{96,128},{128,96},{160,192},{192,160},{33,65},{65,... | collective-permute-start | bytes 491528 | tf_op jit(solution)/shard_map/ppermute | solution.py:310
  98.3 9.7 %collective-permute-start.15 = (f32[2,80,128]{2,1,0:T(8,128)S(1)}, f32[2,80,128]{2,1,0:T(8,128)S(1)}, u32[]{:S(2)}, u32[]{:S(2)}) collective-permute-start(f32[2,80,128]{2,1,0:T(8,128)S(1)} %get-tuple-element.55), channel_id=1, source_target_pairs={{32,65},{65,32},{33,66},{66,33},{34,67},{67,34},{35,68},{68,35},{3... | collective-permute-start | bytes 245768 | tf_op jit(solution)/shard_map/ppermute | solution.py:310
  100.2 11.8 %collective-permute-start.16 = (f32[2,80,128]{2,1,0:T(8,128)S(1)}, f32[2,80,128]{2,1,0:T(8,128)S(1)}, u32[]{:S(2)}, u32[]{:S(2)}) collective-permute-start(f32[2,80,128]{2,1,0:T(8,128)S(1)} %get-tuple-element.56), channel_id=1, source_target_pairs={{33,64},{64,33},{34,65},{65,34},{35,66},{66,35},{36,67},{67,36},{3... | collective-permute-start | bytes 245768 | tf_op jit(solution)/shard_map/ppermute | solution.py:310
  117.5 22.7 %collective-permute-start.19 = (f32[2,80,256]{2,1,0:T(8,128)S(1)}, f32[2,80,256]{2,1,0:T(8,128)S(1)}, u32[]{:S(2)}, u32[]{:S(2)}) collective-permute-start(f32[2,80,256]{2,1,0:T(8,128)S(1)} %get-tuple-element.61), channel_id=1, source_target_pairs={{0,1},{1,0},{2,3},{3,2},{4,5},{5,4},{6,7},{7,6},{8,9},{9,8},{10,11... | collective-permute-start | bytes 491528 | tf_op jit(solution)/shard_map/ppermute | solution.py:310
  117.6 22.6 %collective-permute-start.20 = (f32[2,80,256]{2,1,0:T(8,128)S(1)}, f32[2,80,256]{2,1,0:T(8,128)S(1)}, u32[]{:S(2)}, u32[]{:S(2)}) collective-permute-start(f32[2,80,256]{2,1,0:T(8,128)S(1)} %get-tuple-element.62), channel_id=1, source_target_pairs={{1,2},{2,1},{3,4},{4,3},{5,6},{6,5},{7,8},{8,7},{9,10},{10,9},{11,... | collective-permute-start | bytes 491528 | tf_op jit(solution)/shard_map/ppermute | solution.py:310
  119.7 20.4 %collective-permute-start.21 = (f32[2,2,80,128]{3,2,1,0:T(8,128)S(1)}, f32[2,2,80,128]{3,2,1,0:T(8,128)S(1)}, u32[]{:S(2)}, u32[]{:S(2)}) collective-permute-start(f32[2,2,80,128]{3,2,1,0:T(8,128)S(1)} %get-tuple-element.63), channel_id=1, source_target_pairs={{32,64},{64,32},{96,128},{128,96},{160,192},{192,160},{33,65},{65,... | collective-permute-start | bytes 491528 | tf_op jit(solution)/shard_map/ppermute | solution.py:310
  126.0 8.8 %collective-permute-start.22 = (f32[2,80,128]{2,1,0:T(8,128)S(1)}, f32[2,80,128]{2,1,0:T(8,128)S(1)}, u32[]{:S(2)}, u32[]{:S(2)}) collective-permute-start(f32[2,80,128]{2,1,0:T(8,128)S(1)} %get-tuple-element.64), channel_id=1, source_target_pairs={{32,65},{65,32},{33,66},{66,33},{34,67},{67,34},{35,68},{68,35},{3... | collective-permute-start | bytes 245768 | tf_op jit(solution)/shard_map/ppermute | solution.py:310
  128.4 11.8 %collective-permute-start.23 = (f32[2,80,128]{2,1,0:T(8,128)S(1)}, f32[2,80,128]{2,1,0:T(8,128)S(1)}, u32[]{:S(2)}, u32[]{:S(2)}) collective-permute-start(f32[2,80,128]{2,1,0:T(8,128)S(1)} %get-tuple-element.65), channel_id=1, source_target_pairs={{33,64},{64,33},{34,65},{65,34},{35,66},{66,35},{36,67},{67,36},{3... | collective-permute-start | bytes 245768 | tf_op jit(solution)/shard_map/ppermute | solution.py:310

commit v2 on v1

--- a/solution.py
+++ b/solution.py
@@ -111,33 +111,53 @@
     return jnp.where(flip, even[comp], odd[comp]), jnp.where(flip, odd[comp], even[comp])
 
 
-def corners_for(flags, left, right, first, second):
-    flip = flags[1] == 1
-    for comp in range(2):
-        first[comp] = jnp.where(flip, right[comp], left[comp])
-        second[comp] = jnp.where(flip, left[comp], right[comp])
-
-
-def corners_from(flags, first, second, comp):
-    flip = flags[1] == 1
-    return jnp.where(flip, second[comp], first[comp]), jnp.where(flip, first[comp], second[comp])
-
-
-def send_object(flags, re, im, even, odd, off, first, second):
-    rows = rows_at((W - REACH) * flags[1], REACH)
-    left, right, c_left, c_right = [], [], [], []
-    for comp, x in enumerate((re, im)):
-        left.append(x[:, 0:H].T[:REACH])
-        right.append(x[:, H:W].T[H - REACH :])
-        c_left.append(x[rows, 0:H])
-        c_right.append(x[rows, H:W])
-        off[comp, 0] = c_left[comp]
-        off[comp, 1] = c_right[comp]
+def pack_rows(tiles, out):
+    lane = lax.broadcasted_iota(jnp.int32, (REACH, H), 1)
+    gap = H - REACH
+    for comp in range(2):
+        for j in range(2):
+            out[pl.ds((2 * comp + j) * REACH, REACH), :] = tiles(comp, 1 + j)
+        out[pl.ds((4 + comp) * REACH, REACH), :] = jnp.where(lane < gap, tiles(comp, 3), tiles(comp, 0))
+    rest = jnp.where(lane < REACH, tiles(0, 3), pltpu.roll(tiles(1, 3), REACH - gap, 1))
+    half = REACH // 2
+    inside = (lane[:half] >= gap) & (lane[:half] < gap + 64)
+    out[pl.ds(6 * REACH, half), :] = jnp.where(inside, rest[:half], pltpu.roll(rest[half:], 64, 1))
+
+
+def unpack_rows(packed):
+    lane = lax.broadcasted_iota(jnp.int32, (REACH, H), 1)
+    gap, half = H - REACH, REACH // 2
+    last = packed[pl.ds(6 * REACH, half), :]
+    rest = cat(last, pltpu.roll(last, 64, 1), 0)
+    tiles = []
+    for comp in range(2):
+        outer = packed[pl.ds((4 + comp) * REACH, REACH), :]
+        tail = rest if comp == 0 else pltpu.roll(rest, H - (REACH - gap), 1)
+        tiles.append(
+            [
+                jnp.where(lane >= gap, outer, 0.0),
+                packed[pl.ds(2 * comp * REACH, REACH), :],
+                packed[pl.ds((2 * comp + 1) * REACH, REACH), :],
+                jnp.where(lane < gap, outer, jnp.where(lane < REACH, tail, 0.0)),
+            ]
+        )
+    return tiles
+
+
+def send_columns(flags, re, im, even, odd):
+    left = [x[:, 0:H].T[:REACH] for x in (re, im)]
+    right = [x[:, H:W].T[H - REACH :] for x in (re, im)]
     columns_for(flags, left, right, even, odd)
-    corners_for(flags, c_left, c_right, first, second)
-
-
-def sides_kernel(flags, re, im, even, odd, mid, on):
+
+
+def send_rows(flags, mid, on, off):
+    on_rows = rows_at((W - REACH) * (1 - flags[1]), REACH)
+    off_rows = rows_at((W - REACH) * flags[1], REACH)
+    pack_rows(lambda comp, j: mid[comp, j, on_rows, :], on)
+    pack_rows(lambda comp, j: mid[comp, j, off_rows, :], off)
+
+
+def sides_kernel(flags, re, im, even, odd, mid, on, off):
     blank = jnp.zeros((H - REACH, W), f32)
     for comp, x in enumerate((re, im)):
         from_left, from_right = columns_from(flags, even, odd, comp)
@@ -145,7 +165,7 @@
         mid[comp, 1] = x[:, 0:H]
         mid[comp, 2] = x[:, H:W]
         mid[comp, 3] = cat(from_right, blank, 0).T
-    on[...] = mid[:, :, rows_at((W - REACH) * (1 - flags[1]), REACH), :]
+    send_rows(flags, mid, on, off)
 
 
 def half_gradient(a, offsets, counts, roots, probe_re, probe_im, tables, ext, acc):
@@ -213,64 +233,85 @@
     return rows_at((W - PART) * a, PART)
 
 
+def load_half(a, mid, margin, ext):
+    ext[:, :, own_rows(a), :] = mid[:, :, covered_rows(a), :]
+    tiles = unpack_rows(margin)
+    for comp in range(2):
+        for j in range(4):
+            ext[comp, j, margin_rows(a), :] = tiles[comp][j]
+
+
 def on_kernel(
-    flags, offsets, counts, mid, from_on, roots, probe_re, probe_im, tables, part, to_on, ext, acc
+    flags, offsets, counts, mid, on, roots, probe_re, probe_im, tables, part, to_on, ext, acc
 ):
     a = 1 - flags[1]
-    ext[:, :, own_rows(a), :] = mid[:, :, covered_rows(a), :]
-    ext[:, :, margin_rows(a), :] = from_on[...]
+    load_half(a, mid, on, ext)
     half_gradient(a, offsets, counts, roots, probe_re, probe_im, tables, ext, acc)
     part[...] = acc[:, :, own_rows(a), :]
-    to_on[...] = acc[:, :, margin_rows(a), :]
+    pack_rows(lambda comp, j: acc[comp, j, margin_rows(a), :], to_on)
+
+
+def add_rows(start, packed, out):
+    tiles = unpack_rows(packed)
+    for comp in range(2):
+        for j in range(4):
+            out[comp, j, rows_at(start, REACH), :] += tiles[comp][j]
 
 
 def off_kernel(
-    flags, offsets, counts, mid, off, first, second, part, from_on, roots, probe_re, probe_im, tables,
-    total, to_even, to_odd, to_off, to_first, to_second, ext, acc, centre,
+    flags, offsets, counts, mid, off, part, on, roots, probe_re, probe_im, tables,
+    centre, to_off, ext, acc,
 ):
     a = flags[1]
-    ext[:, :, own_rows(a), :] = mid[:, :, covered_rows(a), :]
-    margin = margin_rows(a)
-    for comp in range(2):
-        left, right = corners_from(flags, first, second, comp)
-        ext[comp, 0, margin, :] = left
-        ext[comp, 1, margin, :] = off[comp, 0]
-        ext[comp, 2, margin, :] = off[comp, 1]
-        ext[comp, 3, margin, :] = right
+    load_half(a, mid, off, ext)
     half_gradient(a, offsets, counts, roots, probe_re, probe_im, tables, ext, acc)
-    for j in range(2):
-        to_off[:, j] = acc[:, 1 + j, margin, :]
-    corners_for(
-        flags, [acc[c, 0, margin, :] for c in range(2)], [acc[c, 3, margin, :] for c in range(2)],
-        to_first, to_second,
-    )
+    pack_rows(lambda comp, j: acc[comp, j, margin_rows(a), :], to_off)
     centre[...] = jnp.zeros(centre.shape, f32)
     centre[:, :, covered_rows(1 - a), :] = part[...]
     centre[:, :, covered_rows(a), :] += acc[:, :, own_rows(a), :]
-    centre[:, :, rows_at((W - REACH) * (1 - a), REACH), :] += from_on[...]
-    left = [centre[c, 0].T[H - REACH :] for c in range(2)]
-    right = [centre[c, 3].T[:REACH] for c in range(2)]
-    columns_for(flags, left, right, to_even, to_odd)
-    for j in range(2):
-        total[:, j] = centre[:, 1 + j]
-
-
-def step_kernel(flags, re, im, total, even, odd, off, first, second, out_re, out_im, *sends):
-    *sends, work = sends
+    add_rows((W - REACH) * (1 - a), on, centre)
+
+
+def rows_kernel(flags, centre, off, total, even, odd):
+    total[...] = centre[...]
+    add_rows((W - REACH) * flags[1], off, total)
+    wide = even.shape[1] > REACH
+    left, right = [], []
+    for comp in range(2):
+        outer = total[comp, 0].T[H - REACH :]
+        left.append(cat(outer, total[comp, 1].T[:REACH], 0) if wide else outer)
+        outer = total[comp, 3].T[:REACH]
+        right.append(cat(total[comp, 2].T[H - REACH :], outer, 0) if wide else outer)
+    columns_for(flags, left, right, even, odd)
+
+
+def step_kernel(flags, mid, total, even, odd, out, to_on, to_off):
     blank = jnp.zeros((H - REACH, W), f32)
-    rows = rows_at((W - REACH) * flags[1], REACH)
+    keep_left = jnp.where(flags[2] == 1, 0.0, 1.0).astype(f32)
+    keep_right = jnp.where(flags[3] == 1, 0.0, 1.0).astype(f32)
     for comp in range(2):
         from_left, from_right = columns_from(flags, even, odd, comp)
-        work[comp, 0] = total[comp, 0] + cat(from_left, blank, 0).T
-        work[comp, 1] = total[comp, 1] + cat(blank, from_right, 0).T
-        corners = corners_from(flags, first, second, comp)
+        add = [
+            cat(blank, from_left[:REACH], 0).T,
+            cat(from_left[REACH:], blank, 0).T,
+            cat(blank, from_right[:REACH], 0).T,
+            cat(from_right[REACH:], blank, 0).T,
+        ]
+        for j in range(4):
+            value = mid[comp, j] - step_size * (total[comp, j] + add[j])
+            if j in (0, 3):
+                value *= keep_left if j == 0 else keep_right
+            out[comp, j] = value
+    send_rows(flags, out, to_on, to_off)
+
+
+def final_kernel(flags, mid, total, even, odd, out_re, out_im):
+    blank = jnp.zeros((H - REACH, W), f32)
+    for comp, out in enumerate((out_re, out_im)):
+        from_left, from_right = columns_from(flags, even, odd, comp)
+        add = [cat(from_left, blank, 0).T, cat(blank, from_right, 0).T]
         for j in range(2):
-            work[comp, j, rows, :] += off[comp, j] + corners[j]
-    for comp, (x, out) in enumerate(((re, out_re), (im, out_im))):
-        for j in range(2):
-            out[:, j * H : (j + 1) * H] = x[:, j * H : (j + 1) * H] - step_size * work[comp, j]
-    if sends:
-        send_object(flags, out_re, out_im, *sends)
+            out[:, j * H : (j + 1) * H] = mid[comp, 1 + j] - step_size * (total[comp, 1 + j] + add[j])
 
 
 def call(kernel, scalars, out_shape, *args, scratch=(), flops=0, read=0):
@@ -289,69 +330,60 @@
     return [p for i in range(bit, size - 1, 2) for p in ((i, i + 1), (i + 1, i))]
 
 
-def exchange(even, odd, off, first, second):
-    height, width = lax.axis_size("row"), lax.axis_size("col")
-    diagonal = ([], [])
-    for r in range(1, height - 1, 2):
-        for c in range(width):
-            for k, d in enumerate((c + 1, c - 1)):
-                if 0 <= d < width:
-                    diagonal[k].extend([(r * width + c, r * width + width + d), (r * width + width + d, r * width + c)])
-    both = ("row", "col")
-    moves = (
-        (even, "col", swaps(width, 0)),
-        (odd, "col", swaps(width, 1)),
-        (off, "row", swaps(height, 1)),
-        (first, both, diagonal[0]),
-        (second, both, diagonal[1]),
-    )
-    got = []
-    for x, axis, pairs in moves:
-        got.append(lax.ppermute(x, axis, pairs))
-    return got
+def swap(x, axis, bit):
+    return lax.ppermute(x, axis, swaps(lax.axis_size(axis), bit))
+
+
+def columns(even, odd):
+    return swap(even, "col", 0), swap(odd, "col", 1)
 
 
 def shards(object_re, object_im, probe_re, probe_im, intensity, offsets, counts):
     slots = intensity.shape[2]
     placed = offsets[0, 0]
     tables = jnp.asarray(dft_tables())
-    flags = jnp.stack([lax.axis_index("col") % 2, lax.axis_index("row") % 2]).astype(jnp.int32)
-    on_chip = swaps(lax.axis_size("row"), 0)
+    column, row = lax.axis_index("col"), lax.axis_index("row")
+    last = lax.axis_size("col") - 1
+    flags = jnp.stack([column % 2, row % 2, column == 0, column == last]).astype(jnp.int32)
 
     tile = shape(W, W)
     strip = shape(2, REACH, W)
-    corner = shape(2, REACH, H)
-    sends = (strip, strip, shape(2, 2, REACH, H), corner, corner)
-    rows = shape(2, 4, REACH, H)
+    wide = shape(2, 2 * REACH, W)
+    rows = shape(6 * REACH + REACH // 2, H)
     full = shape(2, 4, W, H)
     part = shape(2, 4, PART, H)
     halves = [pltpu.VMEM((2, 4, HALF, H), f32)] * 2
     fixed = (probe_re, probe_im, tables)
 
-    re, im = object_re, object_im
-    out = call(send_object, 1, sends, flags, re, im, read=1 << 20)
+    even, odd = columns(*call(send_columns, 1, (strip, strip), flags, object_re, object_im, read=1 << 20))
     roots = call(roots_kernel, 0, shape(slots, W, W), intensity[0, 0], flops=1 << 29, read=1 << 21)
+    mid, on, off = call(
+        sides_kernel, 1, (full, rows, rows), flags, object_re, object_im, even, odd, read=1 << 21
+    )
     for sweep in range(ITERS):
-        even, odd, off, first, second = exchange(*out)
-        mid, on = call(sides_kernel, 1, (full, rows), flags, re, im, even, odd, read=1 << 21)
-        from_on = lax.ppermute(on, "row", on_chip)
-        upper, to_on = call(
-            on_kernel, 3, (part, rows), flags, placed, counts, mid, from_on, roots, *fixed,
+        final = sweep == ITERS - 1
+        on = swap(on, "row", 0)
+        off = swap(off, "row", 1)
+        upper, on = call(
+            on_kernel, 3, (part, rows), flags, placed, counts, mid, on, roots, *fixed,
             scratch=halves, flops=1 << 31, read=1 << 22,
         )
-        from_on = lax.ppermute(to_on, "row", on_chip)
-        total, *back = call(
-            off_kernel, 3, (shape(2, 2, W, H), *sends),
-            flags, placed, counts, mid, off, first, second, upper, from_on, roots, *fixed,
-            scratch=halves + [pltpu.VMEM((2, 4, W, H), f32)], flops=1 << 31, read=1 << 22,
+        on = swap(on, "row", 0)
+        centre, off = call(
+            off_kernel, 3, (full, rows), flags, placed, counts, mid, off, upper, on, roots, *fixed,
+            scratch=halves, flops=1 << 31, read=1 << 22,
         )
-        back = exchange(*back)
-        more = () if sweep == ITERS - 1 else sends
-        re, im, *out = call(
-            step_kernel, 1, (tile, tile, *more), flags, re, im, total, *back,
-            scratch=[pltpu.VMEM((2, 2, W, H), f32)], read=1 << 21,
+        off = swap(off, "row", 1)
+        strips = strip if final else wide
+        total, even, odd = call(
+            rows_kernel, 1, (full, strips, strips), flags, centre, off, read=1 << 21
         )
-    return re, im
+        even, odd = columns(even, odd)
+        if final:
+            return call(final_kernel, 1, (tile, tile), flags, mid, total, even, odd, read=1 << 21)
+        mid, on, off = call(
+            step_kernel, 1, (full, rows, rows), flags, mid, total, even, odd, read=1 << 21
+        )
 
 
 def solution(mesh):

time: 142 us -> 111 us (0.78)
  starting transfers between devices: 76.7 us -> 39.1 us
  waiting for transfers between devices: 34.2 us -> 39.9 us
    ppermute x24 -> x14, starting transfers between devices: 76.7 us -> 39.1 us  [swap(): return lax.ppermute(x, axis, swaps(lax.axis_size(axis), bit))]
    ppermute x24 -> x14, waiting for transfers between devices: 34.2 us -> 39.9 us  [swap(): return lax.ppermute(x, axis, swaps(lax.axis_size(axis), bit))]
    pallas_call x10 -> x11, Pallas kernels: 26.5 us -> 27.7 us  [call(): pl.pallas_call(kernel, in_specs=[SMEM] * scalars + [VMEM] * (len(args) -...]
  transfers between devices with their start and end apart: 24 -> 14, of which waited for: 12 -> 9; matrix products, arithmetic and copies ran while one was open for 0% -> 0% of each run, Pallas kernels for 1% -> 10%
where the time goes in v2:
time: 111 us
  waiting for transfers between devices  39.9 us (36%)
  starting transfers between devices  39.1 us (35%)
  Pallas kernels  27.7 us (25%)
  local copies, waits for them, and re-layouts  2.69 us (2%)
  between operations  1.51 us (1%)
    ppermute x14, waiting for transfers between devices, swap(): return lax.ppermute(x, axis, swaps(lax.axis_size(axis), bit))  39.9 us
    ppermute x14, starting transfers between devices, swap(): return lax.ppermute(x, axis, swaps(lax.axis_size(axis), bit))  39.1 us
    pallas_call x11, Pallas kernels, call(): pl.pallas_call(kernel, in_specs=[SMEM] * scalars + [VMEM] * (len(args) -...  27.7 us
    unnamed x16, local copies, waits for them, and re-layouts  2.59 us
  transfers between devices with their start and end apart: 14, of which 9 were waited for; matrix products, arithmetic and copies ran while one was open for 0% of the time, Pallas kernels for 10%

profile of v2, /device:TPU:69, one launch (start us, length us, event | category | flops | bytes accessed | tf_op | source)
XLA Modules:
  0.0 110.8 jit_solution(7100074566391929258)
XLA Ops:
  0.7 0.1 pad_add_fusion.flags
  0.7 0.9 copy-done
  1.7 0.9 copy-done.1
  2.6 0.7 shard_map.95
  3.4 1.7 %collective-permute-start = (f32[2,80,256]{2,1,0:T(8,128)S(1)}, f32[2,80,256]{2,1,0:T(8,128)S(1)}, u32[]{:S(2)}, u32[]{:S(2)}) collective-permute-start(f32[2,80,256]{2,1,0:T(8,128)S(1)} %get-tuple-element.24), channel_id=1, source_target_pairs={{0,1},{1,0},{2,3},{3,2},{4,5},{5,4},{6,7},{7,6},{8,9},{9,8},{10,11... | collective-permute-start | bytes 491528 | tf_op jit(solution)/shard_map/ppermute | solution.py:334
  5.1 4.3 %collective-permute-start.1 = (f32[2,80,256]{2,1,0:T(8,128)S(1)}, f32[2,80,256]{2,1,0:T(8,128)S(1)}, u32[]{:S(2)}, u32[]{:S(2)}) collective-permute-start(f32[2,80,256]{2,1,0:T(8,128)S(1)} %get-tuple-element.25), channel_id=1, source_target_pairs={{1,2},{2,1},{3,4},{4,3},{5,6},{6,5},{7,8},{8,7},{9,10},{10,9},{11,... | collective-permute-start | bytes 491528 | tf_op jit(solution)/shard_map/ppermute | solution.py:334
  9.5 0.0 collective-permute-done.even
  9.5 5.3 %collective-permute-done.1.odd = f32[2,80,256]{2,1,0:T(8,128)S(1)} collective-permute-done((f32[2,80,256]{2,1,0:T(8,128)S(1)}, f32[2,80,256]{2,1,0:T(8,128)S(1)}, u32[]{:S(2)}, u32[]{:S(2)}) %collective-permute-start.1) | collective-permute-done | bytes 163872 | tf_op jit(solution)/shard_map/ppermute | solution.py:334
  14.8 0.9 shard_map.96
  15.7 1.9 %collective-permute-start.3 = (f32[520,128]{1,0:T(8,128)S(1)}, f32[520,128]{1,0:T(8,128)S(1)}, u32[]{:S(2)}, u32[]{:S(2)}) collective-permute-start(f32[520,128]{1,0:T(8,128)S(1)} %get-tuple-element.28), channel_id=1, source_target_pairs={{0,32},{32,0},{64,96},{96,64},{128,160},{160,128},{192,224},{224,1... | collective-permute-start | bytes 798728 | tf_op jit(solution)/shard_map/ppermute | solution.py:334
  18.3 0.0 copy-start.7
  18.3 0.7 copy-done.7
  18.9 0.1 copy.11.offsets
  19.0 0.0 copy-done.2
  19.0 1.5 %shard_map.97.roots = f32[4,256,256]{2,1,0:T(8,128)S(1)} custom-call(f32[4,256,256]{2,1,0:T(8,128)S(1)} %bitcast.6), custom_call_target="tpu_custom_call" | custom-call | flops 536870912 | bytes 2097152 | tf_op jit(solution)/shard_map/pallas_call | solution.py:318
  20.6 5.4 %collective-permute-start.2 = (f32[520,128]{1,0:T(8,128)S(1)}, f32[520,128]{1,0:T(8,128)S(1)}, u32[]{:S(2)}, u32[]{:S(2)}) collective-permute-start(f32[520,128]{1,0:T(8,128)S(1)} %get-tuple-element.27), channel_id=1, source_target_pairs={{32,64},{64,32},{96,128},{128,96},{160,192},{192,160},{33,65},{65,... | collective-permute-start | bytes 798728 | tf_op jit(solution)/shard_map/ppermute | solution.py:334
  26.0 0.0 collective-permute-done.3.on
  26.0 0.0 copy-done.3
  26.0 0.0 copy-done.4
  26.1 4.6 %shard_map.98 = (f32[2,4,208,128]{3,2,1,0:T(8,128)S(1)}, f32[520,128]{1,0:T(8,128)S(1)}) custom-call(s32[4]{0:T(128)S(1)} %pad_add_fusion.flags, s32[4,2]{1,0:T(4,128)S(1)} %copy.11.offsets, s32[1,1]{1,0:T(1,128)S(6)} %copy.14.counts, f32[2,4,256,128]{3,2,1,0:T(8,128)S(1)} %get-tuple-element.26.mid, f32[520,128]{1,0:T(8,128)S(1)} %collective-permute-done.3.on, ...), custom_call_target="tpu_custom_call" | custom-call | flops 2147483648 | bytes 4194304 | tf_op jit(solution)/shard_map/pallas_call | solution.py:318
  30.6 0.0 collective-permute-start.4
  30.7 1.9 %collective-permute-done.2.off = f32[520,128]{1,0:T(8,128)S(1)} collective-permute-done((f32[520,128]{1,0:T(8,128)S(1)}, f32[520,128]{1,0:T(8,128)S(1)}, u32[]{:S(2)}, u32[]{:S(2)}) %collective-permute-start.2) | collective-permute-done | bytes 266272 | tf_op jit(solution)/shard_map/ppermute | solution.py:334
  32.6 0.0 collective-permute-done.4.on
  32.6 5.3 %shard_map.99 = (f32[2,4,256,128]{3,2,1,0:T(8,128)S(1)}, f32[520,128]{1,0:T(8,128)S(1)}) custom-call(s32[4]{0:T(128)S(1)} %pad_add_fusion.flags, s32[4,2]{1,0:T(4,128)S(1)} %copy.11.offsets, s32[1,1]{1,0:T(1,128)S(6)} %copy.14.counts, f32[2,4,256,128]{3,2,1,0:T(8,128)S(1)} %get-tuple-element.26.mid, f32[520,128]{1,0:T(8,128)S(1)} %collective-permute-done.2.off, ...), custom_call_target="tpu_custom_call" | custom-call | flops 2147483648 | bytes 4194304 | tf_op jit(solution)/shard_map/pallas_call | solution.py:318
  38.0 4.5 %collective-permute-start.5 = (f32[520,128]{1,0:T(8,128)S(1)}, f32[520,128]{1,0:T(8,128)S(1)}, u32[]{:S(2)}, u32[]{:S(2)}) collective-permute-start(f32[520,128]{1,0:T(8,128)S(1)} %get-tuple-element.32), channel_id=1, source_target_pairs={{32,64},{64,32},{96,128},{128,96},{160,192},{192,160},{33,65},{65,... | collective-permute-start | bytes 798728 | tf_op jit(solution)/shard_map/ppermute | solution.py:334
  42.5 6.9 %collective-permute-done.5.off = f32[520,128]{1,0:T(8,128)S(1)} collective-permute-done((f32[520,128]{1,0:T(8,128)S(1)}, f32[520,128]{1,0:T(8,128)S(1)}, u32[]{:S(2)}, u32[]{:S(2)}) %collective-permute-start.5) | collective-permute-done | bytes 266272 | tf_op jit(solution)/shard_map/ppermute | solution.py:334
  49.3 1.1 shard_map.100
  50.4 0.1 collective-permute-start.6
  50.5 5.8 %collective-permute-start.7 = (f32[2,160,256]{2,1,0:T(8,128)S(1)}, f32[2,160,256]{2,1,0:T(8,128)S(1)}, u32[]{:S(2)}, u32[]{:S(2)}) collective-permute-start(f32[2,160,256]{2,1,0:T(8,128)S(1)} %get-tuple-element.35), channel_id=1, source_target_pairs={{1,2},{2,1},{3,4},{4,3},{5,6},{6,5},{7,8},{8,7},{9,10},{10,9},{11,... | collective-permute-start | bytes 983048 | tf_op jit(solution)/shard_map/ppermute | solution.py:334
  56.3 3.9 %collective-permute-done.6.even = f32[2,160,256]{2,1,0:T(8,128)S(1)} collective-permute-done((f32[2,160,256]{2,1,0:T(8,128)S(1)}, f32[2,160,256]{2,1,0:T(8,128)S(1)}, u32[]{:S(2)}, u32[]{:S(2)}) %collective-permute-start.6) | collective-permute-done | bytes 327712 | tf_op jit(solution)/shard_map/ppermute | solution.py:334
  60.2 7.5 %collective-permute-done.7.odd = f32[2,160,256]{2,1,0:T(8,128)S(1)} collective-permute-done((f32[2,160,256]{2,1,0:T(8,128)S(1)}, f32[2,160,256]{2,1,0:T(8,128)S(1)}, u32[]{:S(2)}, u32[]{:S(2)}) %collective-permute-start.7) | collective-permute-done | bytes 327712 | tf_op jit(solution)/shard_map/ppermute | solution.py:334
  67.8 1.1 shard_map.101
  68.8 0.1 collective-permute-start.9
  68.9 5.6 %collective-permute-start.8 = (f32[520,128]{1,0:T(8,128)S(1)}, f32[520,128]{1,0:T(8,128)S(1)}, u32[]{:S(2)}, u32[]{:S(2)}) collective-permute-start(f32[520,128]{1,0:T(8,128)S(1)} %get-tuple-element.37), channel_id=1, source_target_pairs={{32,64},{64,32},{96,128},{128,96},{160,192},{192,160},{33,65},{65,... | collective-permute-start | bytes 798728 | tf_op jit(solution)/shard_map/ppermute | solution.py:334
  74.5 0.0 collective-permute-done.9.on
  74.6 4.6 %shard_map.102 = (f32[2,4,208,128]{3,2,1,0:T(8,128)S(1)}, f32[520,128]{1,0:T(8,128)S(1)}) custom-call(s32[4]{0:T(128)S(1)} %pad_add_fusion.flags, s32[4,2]{1,0:T(4,128)S(1)} %copy.11.offsets, s32[1,1]{1,0:T(1,128)S(6)} %copy.14.counts, f32[2,4,256,128]{3,2,1,0:T(8,128)S(1)} %get-tuple-element.36.mid, f32[520,128]{1,0:T(8,128)S(1)} %collective-permute-done.9.on, ...), custom_call_target="tpu_custom_call" | custom-call | flops 2147483648 | bytes 4194304 | tf_op jit(solution)/shard_map/pallas_call | solution.py:318
  79.2 0.2 collective-permute-start.10
  79.4 2.2 %collective-permute-done.8.off = f32[520,128]{1,0:T(8,128)S(1)} collective-permute-done((f32[520,128]{1,0:T(8,128)S(1)}, f32[520,128]{1,0:T(8,128)S(1)}, u32[]{:S(2)}, u32[]{:S(2)}) %collective-permute-start.8) | collective-permute-done | bytes 266272 | tf_op jit(solution)/shard_map/ppermute | solution.py:334
  81.6 0.0 collective-permute-done.10.on
  81.6 5.3 %shard_map.103 = (f32[2,4,256,128]{3,2,1,0:T(8,128)S(1)}, f32[520,128]{1,0:T(8,128)S(1)}) custom-call(s32[4]{0:T(128)S(1)} %pad_add_fusion.flags, s32[4,2]{1,0:T(4,128)S(1)} %copy.11.offsets, s32[1,1]{1,0:T(1,128)S(6)} %copy.14.counts, f32[2,4,256,128]{3,2,1,0:T(8,128)S(1)} %get-tuple-element.36.mid, f32[520,128]{1,0:T(8,128)S(1)} %collective-permute-done.8.off, ...), custom_call_target="tpu_custom_call" | custom-call | flops 2147483648 | bytes 4194304 | tf_op jit(solution)/shard_map/pallas_call | solution.py:318
  87.0 4.2 %collective-permute-start.11 = (f32[520,128]{1,0:T(8,128)S(1)}, f32[520,128]{1,0:T(8,128)S(1)}, u32[]{:S(2)}, u32[]{:S(2)}) collective-permute-start(f32[520,128]{1,0:T(8,128)S(1)} %get-tuple-element.42), channel_id=1, source_target_pairs={{32,64},{64,32},{96,128},{128,96},{160,192},{192,160},{33,65},{65,... | collective-permute-start | bytes 798728 | tf_op jit(solution)/shard_map/ppermute | solution.py:334
  91.2 6.2 %collective-permute-done.11.off = f32[520,128]{1,0:T(8,128)S(1)} collective-permute-done((f32[520,128]{1,0:T(8,128)S(1)}, f32[520,128]{1,0:T(8,128)S(1)}, u32[]{:S(2)}, u32[]{:S(2)}) %collective-permute-start.11) | collective-permute-done | bytes 266272 | tf_op jit(solution)/shard_map/ppermute | solution.py:334
  97.4 0.9 shard_map.104
  98.4 0.1 collective-permute-start.12
  98.5 5.0 %collective-permute-start.13 = (f32[2,80,256]{2,1,0:T(8,128)S(1)}, f32[2,80,256]{2,1,0:T(8,128)S(1)}, u32[]{:S(2)}, u32[]{:S(2)}) collective-permute-start(f32[2,80,256]{2,1,0:T(8,128)S(1)} %get-tuple-element.45), channel_id=1, source_target_pairs={{1,2},{2,1},{3,4},{4,3},{5,6},{6,5},{7,8},{8,7},{9,10},{10,9},{11,... | collective-permute-start | bytes 491528 | tf_op jit(solution)/shard_map/ppermute | solution.py:334
  103.5 0.9 collective-permute-done.12.even
  104.4 5.0 %collective-permute-done.13.odd = f32[2,80,256]{2,1,0:T(8,128)S(1)} collective-permute-done((f32[2,80,256]{2,1,0:T(8,128)S(1)}, f32[2,80,256]{2,1,0:T(8,128)S(1)}, u32[]{:S(2)}, u32[]{:S(2)}) %collective-permute-start.13) | collective-permute-done | bytes 163872 | tf_op jit(solution)/shard_map/ppermute | solution.py:334
  109.4 1.5 %shard_map.105 = (f32[256,256]{1,0:T(8,128)}, f32[256,256]{1,0:T(8,128)}) custom-call(s32[4]{0:T(128)S(1)} %pad_add_fusion.flags, f32[2,4,256,128]{3,2,1,0:T(8,128)S(1)} %get-tuple-element.36.mid, f32[2,4,256,128]{3,2,1,0:T(8,128)S(1)} %get-tuple-element.43.total, f32[2,80,256]{2,1,0:T(8,128)S(1)} %collective-permute-done.12.even, ...), custom_call_target="tpu_custom_call" | custom-call | bytes 2097152 | tf_op jit(solution)/shard_map/pallas_call | solution.py:318
  (9 shorter events, 0.0 us)
Async XLA Ops:
  0.7 1.0 copy-start
  1.7 0.9 copy-start.1
  2.6 16.4 %copy-start.2 = (f32[1,1,4,256,256]{4,3,2,1,0:T(8,128)S(1)}, f32[1,1,4,256,256]{4,3,2,1,0:T(8,128)}, u32[]{:S(2)}) copy-start(f32[1,1,4,256,256]{4,3,2,1,0:T(8,128)} %param.12) | copy-start | bytes 3145732
  3.4 6.1 %collective-permute-start = (f32[2,80,256]{2,1,0:T(8,128)S(1)}, f32[2,80,256]{2,1,0:T(8,128)S(1)}, u32[]{:S(2)}, u32[]{:S(2)}) collective-permute-start(f32[2,80,256]{2,1,0:T(8,128)S(1)} %get-tuple-element.24), channel_id=1, source_target_pairs={{0,1},{1,0},{2,3},{3,2},{4,5},{5,4},{6,7},{7,6},{8,9},{9,8},{10,11... | collective-permute-start | bytes 491528 | tf_op jit(solution)/shard_map/ppermute | solution.py:334
  5.1 9.7 %collective-permute-start.1 = (f32[2,80,256]{2,1,0:T(8,128)S(1)}, f32[2,80,256]{2,1,0:T(8,128)S(1)}, u32[]{:S(2)}, u32[]{:S(2)}) collective-permute-start(f32[2,80,256]{2,1,0:T(8,128)S(1)} %get-tuple-element.25), channel_id=1, source_target_pairs={{1,2},{2,1},{3,4},{4,3},{5,6},{6,5},{7,8},{8,7},{9,10},{10,9},{11,... | collective-permute-start | bytes 491528 | tf_op jit(solution)/shard_map/ppermute | solution.py:334
  15.7 10.3 %collective-permute-start.3 = (f32[520,128]{1,0:T(8,128)S(1)}, f32[520,128]{1,0:T(8,128)S(1)}, u32[]{:S(2)}, u32[]{:S(2)}) collective-permute-start(f32[520,128]{1,0:T(8,128)S(1)} %get-tuple-element.28), channel_id=1, source_target_pairs={{0,32},{32,0},{64,96},{96,64},{128,160},{160,128},{192,224},{224,1... | collective-permute-start | bytes 798728 | tf_op jit(solution)/shard_map/ppermute | solution.py:334
  18.3 0.7 copy-start.7
  19.0 7.0 %copy-start.3 = (f32[256,256]{1,0:T(8,128)S(1)}, f32[256,256]{1,0:T(8,128)}, u32[]{:S(2)}) copy-start(f32[256,256]{1,0:T(8,128)} %probe_re.7) | copy-start | bytes 786436
  19.0 7.0 %copy-start.4 = (f32[256,256]{1,0:T(8,128)S(1)}, f32[256,256]{1,0:T(8,128)}, u32[]{:S(2)}) copy-start(f32[256,256]{1,0:T(8,128)} %probe_im.7) | copy-start | bytes 786436
  19.0 7.0 %copy-start.5 = (bf16[8,256,256]{2,1,0:T(8,128)(2,1)S(1)}, bf16[8,256,256]{2,1,0:T(8,128)(2,1)}, u32[]{:S(2)}) copy-start(bf16[8,256,256]{2,1,0:T(8,128)(2,1)} %constant.31.clone.tables) | copy-start | bytes 3145732
  20.6 12.0 %collective-permute-start.2 = (f32[520,128]{1,0:T(8,128)S(1)}, f32[520,128]{1,0:T(8,128)S(1)}, u32[]{:S(2)}, u32[]{:S(2)}) collective-permute-start(f32[520,128]{1,0:T(8,128)S(1)} %get-tuple-element.27), channel_id=1, source_target_pairs={{32,64},{64,32},{96,128},{128,96},{160,192},{192,160},{33,65},{65,... | collective-permute-start | bytes 798728 | tf_op jit(solution)/shard_map/ppermute | solution.py:334
  30.6 2.0 %collective-permute-start.4 = (f32[520,128]{1,0:T(8,128)S(1)}, f32[520,128]{1,0:T(8,128)S(1)}, u32[]{:S(2)}, u32[]{:S(2)}) collective-permute-start(f32[520,128]{1,0:T(8,128)S(1)} %get-tuple-element.30), channel_id=1, source_target_pairs={{0,32},{32,0},{64,96},{96,64},{128,160},{160,128},{192,224},{224,1... | collective-permute-start | bytes 798728 | tf_op jit(solution)/shard_map/ppermute | solution.py:334
  38.0 11.3 %collective-permute-start.5 = (f32[520,128]{1,0:T(8,128)S(1)}, f32[520,128]{1,0:T(8,128)S(1)}, u32[]{:S(2)}, u32[]{:S(2)}) collective-permute-start(f32[520,128]{1,0:T(8,128)S(1)} %get-tuple-element.32), channel_id=1, source_target_pairs={{32,64},{64,32},{96,128},{128,96},{160,192},{192,160},{33,65},{65,... | collective-permute-start | bytes 798728 | tf_op jit(solution)/shard_map/ppermute | solution.py:334
  50.4 9.8 %collective-permute-start.6 = (f32[2,160,256]{2,1,0:T(8,128)S(1)}, f32[2,160,256]{2,1,0:T(8,128)S(1)}, u32[]{:S(2)}, u32[]{:S(2)}) collective-permute-start(f32[2,160,256]{2,1,0:T(8,128)S(1)} %get-tuple-element.34), channel_id=1, source_target_pairs={{0,1},{1,0},{2,3},{3,2},{4,5},{5,4},{6,7},{7,6},{8,9},{9,8},{10,11... | collective-permute-start | bytes 983048 | tf_op jit(solution)/shard_map/ppermute | solution.py:334
  50.5 17.3 %collective-permute-start.7 = (f32[2,160,256]{2,1,0:T(8,128)S(1)}, f32[2,160,256]{2,1,0:T(8,128)S(1)}, u32[]{:S(2)}, u32[]{:S(2)}) collective-permute-start(f32[2,160,256]{2,1,0:T(8,128)S(1)} %get-tuple-element.35), channel_id=1, source_target_pairs={{1,2},{2,1},{3,4},{4,3},{5,6},{6,5},{7,8},{8,7},{9,10},{10,9},{11,... | collective-permute-start | bytes 983048 | tf_op jit(solution)/shard_map/ppermute | solution.py:334
  67.8 6.8 %copy-start.6 = (bf16[8,256,256]{2,1,0:T(8,128)(2,1)S(1)}, bf16[8,256,256]{2,1,0:T(8,128)(2,1)}, u32[]{:S(2)}) copy-start(bf16[8,256,256]{2,1,0:T(8,128)(2,1)} %constant.31.clone.tables) | copy-start | bytes 3145732
  68.8 5.7 %collective-permute-start.9 = (f32[520,128]{1,0:T(8,128)S(1)}, f32[520,128]{1,0:T(8,128)S(1)}, u32[]{:S(2)}, u32[]{:S(2)}) collective-permute-start(f32[520,128]{1,0:T(8,128)S(1)} %get-tuple-element.38), channel_id=1, source_target_pairs={{0,32},{32,0},{64,96},{96,64},{128,160},{160,128},{192,224},{224,1... | collective-permute-start | bytes 798728 | tf_op jit(solution)/shard_map/ppermute | solution.py:334
  68.9 12.7 %collective-permute-start.8 = (f32[520,128]{1,0:T(8,128)S(1)}, f32[520,128]{1,0:T(8,128)S(1)}, u32[]{:S(2)}, u32[]{:S(2)}) collective-permute-start(f32[520,128]{1,0:T(8,128)S(1)} %get-tuple-element.37), channel_id=1, source_target_pairs={{32,64},{64,32},{96,128},{128,96},{160,192},{192,160},{33,65},{65,... | collective-permute-start | bytes 798728 | tf_op jit(solution)/shard_map/ppermute | solution.py:334
  79.2 2.4 %collective-permute-start.10 = (f32[520,128]{1,0:T(8,128)S(1)}, f32[520,128]{1,0:T(8,128)S(1)}, u32[]{:S(2)}, u32[]{:S(2)}) collective-permute-start(f32[520,128]{1,0:T(8,128)S(1)} %get-tuple-element.40), channel_id=1, source_target_pairs={{0,32},{32,0},{64,96},{96,64},{128,160},{160,128},{192,224},{224,1... | collective-permute-start | bytes 798728 | tf_op jit(solution)/shard_map/ppermute | solution.py:334
  87.0 10.5 %collective-permute-start.11 = (f32[520,128]{1,0:T(8,128)S(1)}, f32[520,128]{1,0:T(8,128)S(1)}, u32[]{:S(2)}, u32[]{:S(2)}) collective-permute-start(f32[520,128]{1,0:T(8,128)S(1)} %get-tuple-element.42), channel_id=1, source_target_pairs={{32,64},{64,32},{96,128},{128,96},{160,192},{192,160},{33,65},{65,... | collective-permute-start | bytes 798728 | tf_op jit(solution)/shard_map/ppermute | solution.py:334
  98.4 6.0 %collective-permute-start.12 = (f32[2,80,256]{2,1,0:T(8,128)S(1)}, f32[2,80,256]{2,1,0:T(8,128)S(1)}, u32[]{:S(2)}, u32[]{:S(2)}) collective-permute-start(f32[2,80,256]{2,1,0:T(8,128)S(1)} %get-tuple-element.44), channel_id=1, source_target_pairs={{0,1},{1,0},{2,3},{3,2},{4,5},{5,4},{6,7},{7,6},{8,9},{9,8},{10,11... | collective-permute-start | bytes 491528 | tf_op jit(solution)/shard_map/ppermute | solution.py:334
  98.5 10.9 %collective-permute-start.13 = (f32[2,80,256]{2,1,0:T(8,128)S(1)}, f32[2,80,256]{2,1,0:T(8,128)S(1)}, u32[]{:S(2)}, u32[]{:S(2)}) collective-permute-start(f32[2,80,256]{2,1,0:T(8,128)S(1)} %get-tuple-element.45), channel_id=1, source_target_pairs={{1,2},{2,1},{3,4},{4,3},{5,6},{6,5},{7,8},{8,7},{9,10},{10,9},{11,... | collective-permute-start | bytes 491528 | tf_op jit(solution)/shard_map/ppermute | solution.py:334

commit v3 on v2

--- a/solution.py
+++ b/solution.py
@@ -21,6 +21,7 @@
 
 VMEM = pl.BlockSpec(memory_space=pltpu.VMEM)
 SMEM = pl.BlockSpec(memory_space=pltpu.SMEM)
+ANY = pl.BlockSpec(memory_space=pltpu.HBM)
 f32 = jnp.float32
 bf16 = jnp.bfloat16
 
@@ -77,14 +78,30 @@
     return jnp.concatenate([a, b], axis=axis)
 
 
-def roots_kernel(intensity, out):
+def roots_kernel(
+    flags, intensity, probe_re, probe_im, tables, out, probe_out, tables_out, held, sems
+):
+    slots = out.shape[0]
+    copies = [pltpu.make_async_copy(intensity.at[p], held.at[p], sems.at[p]) for p in range(slots)]
+    for comp, x in enumerate((probe_re, probe_im)):
+        for j in range(2):
+            k = 2 * comp + j
+            copies.append(
+                pltpu.make_async_copy(
+                    x.at[:, pl.ds(j * H, H)], probe_out.at[comp, j], sems.at[slots + k]
+                )
+            )
+    copies.append(pltpu.make_async_copy(tables, tables_out, sems.at[slots + 4]))
+    for c in copies:
+        c.start()
     row = lax.broadcasted_iota(jnp.int32, (W, W), 0)
     col = lax.broadcasted_iota(jnp.int32, (W, W), 1)
     source = jnp.where(col < H, 2 * col, 2 * (col - H) + 1)
     perm = jnp.where(row == source, 1.0, 0.0).astype(bf16)
     perm3 = jnp.concatenate([perm, perm, perm], axis=0)
-    for p in range(out.shape[0]):
-        x = jnp.sqrt(intensity[p])
+    for p in range(slots):
+        copies[p].wait()
+        x = jnp.sqrt(held[p])
         hi = x.astype(bf16)
         rest = x - hi.astype(f32)
         mid = rest.astype(bf16)
@@ -93,6 +110,12 @@
         y = y.reshape(H, 2, W)
         out[p, pl.ds(0, H), :] = y[:, 0, :]
         out[p, pl.ds(H, H), :] = y[:, 1, :]
+    for c in copies[slots:]:
+        c.wait()
+
+
+OFFSETS = 5
+COUNT = 13
 
 
 def rows_at(start, size):
@@ -108,7 +131,9 @@
 
 def columns_from(flags, even, odd, comp):
     flip = flags[0] == 1
-    return jnp.where(flip, even[comp], odd[comp]), jnp.where(flip, odd[comp], even[comp])
+    e = even[comp]
+    o = jnp.where(flags[2] + flags[3] == 0, odd[comp], 0.0)
+    return jnp.where(flip, e, o), jnp.where(flip, o, e)
 
 
 def pack_rows(tiles, out):
@@ -124,29 +149,33 @@
     out[pl.ds(6 * REACH, half), :] = jnp.where(inside, rest[:half], pltpu.roll(rest[half:], 64, 1))
 
 
-def unpack_rows(packed):
+def unpack_rows(packed, keep=None):
+    def load(start, size):
+        x = packed[pl.ds(start, size), :]
+        return x if keep is None else jnp.where(keep, x, 0.0)
+
     lane = lax.broadcasted_iota(jnp.int32, (REACH, H), 1)
     gap, half = H - REACH, REACH // 2
-    last = packed[pl.ds(6 * REACH, half), :]
+    last = load(6 * REACH, half)
     rest = cat(last, pltpu.roll(last, 64, 1), 0)
     tiles = []
     for comp in range(2):
-        outer = packed[pl.ds((4 + comp) * REACH, REACH), :]
+        outer = load((4 + comp) * REACH, REACH)
         tail = rest if comp == 0 else pltpu.roll(rest, H - (REACH - gap), 1)
         tiles.append(
             [
                 jnp.where(lane >= gap, outer, 0.0),
-                packed[pl.ds(2 * comp * REACH, REACH), :],
-                packed[pl.ds((2 * comp + 1) * REACH, REACH), :],
+                load(2 * comp * REACH, REACH),
+                load((2 * comp + 1) * REACH, REACH),
                 jnp.where(lane < gap, outer, jnp.where(lane < REACH, tail, 0.0)),
             ]
         )
     return tiles
 
 
-def send_columns(flags, re, im, even, odd):
-    left = [x[:, 0:H].T[:REACH] for x in (re, im)]
-    right = [x[:, H:W].T[H - REACH :] for x in (re, im)]
+def send_columns(flags, mid, even, odd):
+    left = [mid[comp, 1].T[:REACH] for comp in range(2)]
+    right = [mid[comp, 2].T[H - REACH :] for comp in range(2)]
     columns_for(flags, left, right, even, odd)
 
 
@@ -157,32 +186,30 @@
     pack_rows(lambda comp, j: mid[comp, j, off_rows, :], off)
 
 
-def sides_kernel(flags, re, im, even, odd, mid, on, off):
+def sides_kernel(flags, even, odd, mid, out, on, off):
     blank = jnp.zeros((H - REACH, W), f32)
-    for comp, x in enumerate((re, im)):
+    for comp in range(2):
         from_left, from_right = columns_from(flags, even, odd, comp)
-        mid[comp, 0] = cat(blank, from_left, 0).T
-        mid[comp, 1] = x[:, 0:H]
-        mid[comp, 2] = x[:, H:W]
-        mid[comp, 3] = cat(from_right, blank, 0).T
-    send_rows(flags, mid, on, off)
-
-
-def half_gradient(a, offsets, counts, roots, probe_re, probe_im, tables, ext, acc):
+        out[comp, 0] = cat(blank, from_left, 0).T
+        out[comp, 3] = cat(from_right, blank, 0).T
+    send_rows(flags, out, on, off)
+
+
+def half_gradient(a, flags, roots, probe, tables, ext, acc):
     acc[...] = jnp.zeros(acc.shape, f32)
     lane = lax.broadcasted_iota(jnp.int32, (W, H), 1)
 
     def position(base, carry):
         p = 2 * a + base
-        shift = offsets[p, 1] - H * base
-        rows = pl.ds(offsets[p, 0] - (H - REACH) - H * a, W)
+        shift = flags[OFFSETS + 2 * p + 1] - H * base
+        rows = pl.ds(flags[OFFSETS + 2 * p] - (H - REACH) - H * a, W)
         o = []
         for comp in range(2):
             rolled = [pltpu.roll(ext[comp, base + j, rows, :], H - shift, 1) for j in range(3)]
             o.append([jnp.where(lane < H - shift, rolled[j], rolled[j + 1]) for j in range(2)])
         w_re, w_im = [], []
         for j in range(2):
-            p_re, p_im = probe_re[:, j * H : (j + 1) * H], probe_im[:, j * H : (j + 1) * H]
+            p_re, p_im = probe[0, j], probe[1, j]
             w_re.append(o[0][j] * p_re - o[1][j] * p_im)
             w_im.append(o[0][j] * p_im + o[1][j] * p_re)
         e = right(cat(w_re[0] + w_re[1], w_im[0] + w_im[1], 1), tables, 0)
@@ -204,11 +231,10 @@
         h_im = cat(upper[H:], lower[H:], 0)
         x = right(cat(h_re[:, :H], h_im[:, :H], 1), tables, 2)
         y = right(cat(h_re[:, H:], h_im[:, H:], 1), tables, 3)
-        weight = jnp.where(p < counts[0, 0], 1.0, 0.0).astype(f32)
+        weight = jnp.where(p < flags[COUNT], 1.0, 0.0).astype(f32)
         g_re, g_im = [], []
         for j, z in enumerate((x + y, x - y)):
-            p_re, p_im = probe_re[:, j * H : (j + 1) * H], probe_im[:, j * H : (j + 1) * H]
-            p_re, p_im = p_re * weight, p_im * weight
+            p_re, p_im = probe[0, j] * weight, probe[1, j] * weight
             g_re.append(z[:, :H] * p_re + z[:, H:] * p_im)
             g_im.append(z[:, H:] * p_re - z[:, :H] * p_im)
         for comp, g in enumerate((g_re, g_im)):
@@ -233,38 +259,33 @@
     return rows_at((W - PART) * a, PART)
 
 
-def load_half(a, mid, margin, ext):
+def load_half(a, mid, margin, ext, keep=None):
     ext[:, :, own_rows(a), :] = mid[:, :, covered_rows(a), :]
-    tiles = unpack_rows(margin)
+    tiles = unpack_rows(margin, keep)
     for comp in range(2):
         for j in range(4):
             ext[comp, j, margin_rows(a), :] = tiles[comp][j]
 
 
-def on_kernel(
-    flags, offsets, counts, mid, on, roots, probe_re, probe_im, tables, part, to_on, ext, acc
-):
+def on_kernel(flags, mid, on, roots, probe, tables, part, to_on, ext, acc):
     a = 1 - flags[1]
     load_half(a, mid, on, ext)
-    half_gradient(a, offsets, counts, roots, probe_re, probe_im, tables, ext, acc)
+    half_gradient(a, flags, roots, probe, tables, ext, acc)
     part[...] = acc[:, :, own_rows(a), :]
     pack_rows(lambda comp, j: acc[comp, j, margin_rows(a), :], to_on)
 
 
-def add_rows(start, packed, out):
-    tiles = unpack_rows(packed)
+def add_rows(start, packed, out, keep=None):
+    tiles = unpack_rows(packed, keep)
     for comp in range(2):
         for j in range(4):
             out[comp, j, rows_at(start, REACH), :] += tiles[comp][j]
 
 
-def off_kernel(
-    flags, offsets, counts, mid, off, part, on, roots, probe_re, probe_im, tables,
-    centre, to_off, ext, acc,
-):
+def off_kernel(flags, mid, off, part, on, roots, probe, tables, centre, to_off, ext, acc):
     a = flags[1]
-    load_half(a, mid, off, ext)
-    half_gradient(a, offsets, counts, roots, probe_re, probe_im, tables, ext, acc)
+    load_half(a, mid, off, ext, flags[4] == 0)
+    half_gradient(a, flags, roots, probe, tables, ext, acc)
     pack_rows(lambda comp, j: acc[comp, j, margin_rows(a), :], to_off)
     centre[...] = jnp.zeros(centre.shape, f32)
     centre[:, :, covered_rows(1 - a), :] = part[...]
@@ -273,8 +294,7 @@
 
 
 def rows_kernel(flags, centre, off, total, even, odd):
-    total[...] = centre[...]
-    add_rows((W - REACH) * flags[1], off, total)
+    add_rows((W - REACH) * flags[1], off, total, flags[4] == 0)
     wide = even.shape[1] > REACH
     left, right = [], []
     for comp in range(2):
@@ -314,20 +334,21 @@
             out[:, j * H : (j + 1) * H] = mid[comp, 1 + j] - step_size * (total[comp, 1 + j] + add[j])
 
 
-def call(kernel, scalars, out_shape, *args, scratch=(), flops=0, read=0):
+def call(kernel, specs, out_shape, *args, scratch=(), flops=0, read=0, alias={}):
     return pl.pallas_call(
         kernel,
-        in_specs=[SMEM] * scalars + [VMEM] * (len(args) - scalars),
+        in_specs=[SMEM] + specs + [VMEM] * (len(args) - 1 - len(specs)),
         out_specs=jax.tree.map(lambda _: VMEM, out_shape),
         out_shape=out_shape,
         scratch_shapes=scratch,
-        compiler_params=pltpu.CompilerParams(vmem_limit_bytes=48 * 1024 * 1024),
+        input_output_aliases=alias,
+        compiler_params=pltpu.CompilerParams(vmem_limit_bytes=24 * 1024 * 1024),
         cost_estimate=pl.CostEstimate(flops=flops, bytes_accessed=read, transcendentals=0),
     )(*args)
 
 
 def swaps(size, bit):
-    return [p for i in range(bit, size - 1, 2) for p in ((i, i + 1), (i + 1, i))]
+    return [p for i in range(bit, size, 2) for p in ((i, (i + 1) % size), ((i + 1) % size, i))]
 
 
 def swap(x, axis, bit):
@@ -340,11 +361,11 @@
 
 def shards(object_re, object_im, probe_re, probe_im, intensity, offsets, counts):
     slots = intensity.shape[2]
-    placed = offsets[0, 0]
-    tables = jnp.asarray(dft_tables())
     column, row = lax.axis_index("col"), lax.axis_index("row")
-    last = lax.axis_size("col") - 1
-    flags = jnp.stack([column % 2, row % 2, column == 0, column == last]).astype(jnp.int32)
+    last, lowest = lax.axis_size("col") - 1, lax.axis_size("row") - 1
+    edge = (row == 0) | (row == lowest)
+    flags = jnp.stack([column % 2, row % 2, column == 0, column == last, edge]).astype(jnp.int32)
+    known = jnp.concatenate([flags, offsets.reshape(-1), counts.reshape(-1)])
 
     tile = shape(W, W)
     strip = shape(2, REACH, W)
@@ -353,36 +374,49 @@
     full = shape(2, 4, W, H)
     part = shape(2, 4, PART, H)
     halves = [pltpu.VMEM((2, 4, HALF, H), f32)] * 2
-    fixed = (probe_re, probe_im, tables)
-
-    even, odd = columns(*call(send_columns, 1, (strip, strip), flags, object_re, object_im, read=1 << 20))
-    roots = call(roots_kernel, 0, shape(slots, W, W), intensity[0, 0], flops=1 << 29, read=1 << 21)
+
+    blank = jnp.zeros((W, H), f32)
+    mid = jnp.stack(
+        [jnp.stack([blank, x[:, 0:H], x[:, H:W], blank]) for x in (object_re, object_im)]
+    )
+    even, odd = call(send_columns, [], (strip, strip), flags, mid, read=1 << 20)
+    even, odd = columns(even, odd)
+    tables = jnp.asarray(dft_tables())
+    fixed = call(
+        roots_kernel,
+        [ANY] * 4,
+        (shape(slots, W, W), shape(2, 2, W, H), jax.ShapeDtypeStruct(tables.shape, bf16)),
+        known, intensity[0, 0], probe_re, probe_im, tables,
+        scratch=[pltpu.VMEM((slots, W, W), f32), pltpu.SemaphoreType.DMA((slots + 5,))],
+        flops=1 << 29, read=1 << 21,
+    )
     mid, on, off = call(
-        sides_kernel, 1, (full, rows, rows), flags, object_re, object_im, even, odd, read=1 << 21
+        sides_kernel, [], (full, rows, rows), flags, even, odd, mid, read=1 << 21, alias={3: 0}
     )
     for sweep in range(ITERS):
         final = sweep == ITERS - 1
         on = swap(on, "row", 0)
         off = swap(off, "row", 1)
         upper, on = call(
-            on_kernel, 3, (part, rows), flags, placed, counts, mid, on, roots, *fixed,
+            on_kernel, [], (part, rows), known, mid, on, *fixed,
             scratch=halves, flops=1 << 31, read=1 << 22,
         )
         on = swap(on, "row", 0)
         centre, off = call(
-            off_kernel, 3, (full, rows), flags, placed, counts, mid, off, upper, on, roots, *fixed,
+            off_kernel, [], (full, rows), known, mid, off, upper, on, *fixed,
             scratch=halves, flops=1 << 31, read=1 << 22,
         )
         off = swap(off, "row", 1)
         strips = strip if final else wide
         total, even, odd = call(
-            rows_kernel, 1, (full, strips, strips), flags, centre, off, read=1 << 21
+            rows_kernel, [], (full, strips, strips), known, centre, off, read=1 << 21, alias={1: 0}
         )
         even, odd = columns(even, odd)
         if final:
-            return call(final_kernel, 1, (tile, tile), flags, mid, total, even, odd, read=1 << 21)
+            return call(final_kernel, [], (tile, tile), known, mid, total, even, odd, read=1 << 21)
         mid, on, off = call(
-            step_kernel, 1, (full, rows, rows), flags, mid, total, even, odd, read=1 << 21
+            step_kernel, [], (full, rows, rows), known, mid, total, even, odd, read=1 << 21,
+            alias={1: 0},
         )
 
 

time: 111 us -> 108 us (0.973)
  the two profiles are of different devices: /device:TPU:69 before, /device:TPU:1 now
where the time goes in v3:
time: 108 us
  waiting for transfers between devices  41.8 us (39%)
  starting transfers between devices  32.7 us (30%)
  Pallas kernels  28.7 us (27%)
  local copies, waits for them, and re-layouts  3.17 us (3%)
  between operations  1.44 us (1%)
    ppermute x14, waiting for transfers between devices, swap(): return lax.ppermute(x, axis, swaps(lax.axis_size(axis), bit))  41.8 us
    ppermute x14, starting transfers between devices, swap(): return lax.ppermute(x, axis, swaps(lax.axis_size(axis), bit))  32.7 us
    pallas_call x11, Pallas kernels, call(): pl.pallas_call(kernel, in_specs=[SMEM] + specs + [VMEM] * (len(args) - 1...  28.7 us
  transfers between devices with their start and end apart: 14, of which 10 were waited for; matrix products, arithmetic and copies ran while one was open for 0% of the time, Pallas kernels for 11%

profile of v3, /device:TPU:1, one launch (start us, length us, event | category | flops | bytes accessed | tf_op | source)
XLA Modules:
  0.0 107.9 jit_solution(16411508517816727594)
XLA Ops:
  0.7 1.1 %slice_bitcast_fusion.1 = (f32[1,256,128]{2,1,0:T(8,128)S(1)}, f32[1,256,128]{2,1,0:T(8,128)S(1)}, f32[1,256,128]{2,1,0:T(8,128)S(1)}, f32[1,256,128]{2,1,0:T(8,128)S(1)}) fusion(f32[256,256]{1,0:T(8,128)} %param.9, f32[256,256]{1,0:T(8,128)} %param.8), kind=kLoop, calls=%fused_computation.10 | loop fusion | bytes 1048576 | tf_op jit(solution)/shard_map/stack | solution.py:380
  1.8 0.1 fusion.2
  1.9 0.1 pad_maximum_fusion.mid
  2.0 0.1 stack.62.flags
  2.1 0.7 shard_map.95
  2.8 2.5 %collective-permute-start = (f32[2,80,256]{2,1,0:T(8,128)S(1)}, f32[2,80,256]{2,1,0:T(8,128)S(1)}, u32[]{:S(2)}, u32[]{:S(2)}) collective-permute-start(f32[2,80,256]{2,1,0:T(8,128)S(1)} %get-tuple-element.27), channel_id=1, source_target_pairs={{0,1},{1,0},{2,3},{3,2},{4,5},{5,4},{6,7},{7,6},{8,9},{9,8},{10,11... | collective-permute-start | bytes 491528 | tf_op jit(solution)/shard_map/ppermute | solution.py:355
  5.4 4.8 %collective-permute-start.1 = (f32[2,80,256]{2,1,0:T(8,128)S(1)}, f32[2,80,256]{2,1,0:T(8,128)S(1)}, u32[]{:S(2)}, u32[]{:S(2)}) collective-permute-start(f32[2,80,256]{2,1,0:T(8,128)S(1)} %get-tuple-element.28), channel_id=1, source_target_pairs={{1,2},{2,1},{3,4},{4,3},{5,6},{6,5},{7,8},{8,7},{9,10},{10,9},{11,... | collective-permute-start | bytes 491528 | tf_op jit(solution)/shard_map/ppermute | solution.py:355
  10.1 0.0 collective-permute-done.even
  10.1 7.2 %collective-permute-done.1.odd = f32[2,80,256]{2,1,0:T(8,128)S(1)} collective-permute-done((f32[2,80,256]{2,1,0:T(8,128)S(1)}, f32[2,80,256]{2,1,0:T(8,128)S(1)}, u32[]{:S(2)}, u32[]{:S(2)}) %collective-permute-start.1) | collective-permute-done | bytes 163872 | tf_op jit(solution)/shard_map/ppermute | solution.py:355
  17.3 1.6 %shard_map.96 = (f32[2,4,256,128]{3,2,1,0:T(8,128)S(1)}, f32[520,128]{1,0:T(8,128)}, f32[520,128]{1,0:T(8,128)S(1)}) custom-call(s32[5]{0:T(128)S(1)} %stack.62.flags, f32[2,80,256]{2,1,0:T(8,128)S(1)} %collective-permute-done.even, f32[2,80,256]{2,1,0:T(8,128)S(1)} %collective-permute-done.1.odd, ...), custom_call_target="tpu_custom_call", output_to_operand_aliasing={{0}: (3, {})} | custom-call | bytes 2097152 | tf_op jit(solution)/shard_map/pallas_call | solution.py:338
  18.9 0.7 copy-done.4
  19.6 1.4 %collective-permute-start.3 = (f32[520,128]{1,0:T(8,128)}, f32[520,128]{1,0:T(8,128)}, u32[]{:S(2)}, u32[]{:S(2)}) collective-permute-start(f32[520,128]{1,0:T(8,128)} %get-tuple-element.31), channel_id=1, source_target_pairs={{0,32},{32,0},{64,96},{96,64},{128,160},{160,128},{192,224},{224,1... | collective-permute-start | bytes 798728 | tf_op jit(solution)/shard_map/ppermute | solution.py:355
  21.6 0.1 copy.15
  21.7 0.1 reshape.10
  21.8 0.1 concatenate.4.flags
  21.9 0.0 copy-start.3
  21.9 0.9 copy-done.3
  22.9 2.9 %shard_map.97 = (f32[4,256,256]{2,1,0:T(8,128)S(1)}, f32[2,2,256,128]{3,2,1,0:T(8,128)S(1)}, bf16[8,256,256]{2,1,0:T(8,128)(2,1)S(1)}) custom-call(s32[14]{0:T(128)S(1)} %concatenate.4.flags, f32[4,256,256]{2,1,0:T(8,128)S(1)} %bitcast.20, f32[256,256]{1,0:T(8,128)S(1)} %copy-done.2, f32[256,256]{1,0:T(8,128)S(1)} %copy-done.3, ...), custom_call_target="tpu_custom_call" | custom-call | flops 536870912 | bytes 2097152 | tf_op jit(solution)/shard_map/pallas_call | solution.py:338
  25.8 3.0 %collective-permute-start.2 = (f32[520,128]{1,0:T(8,128)S(1)}, f32[520,128]{1,0:T(8,128)S(1)}, u32[]{:S(2)}, u32[]{:S(2)}) collective-permute-start(f32[520,128]{1,0:T(8,128)S(1)} %copy-done.5), channel_id=1, source_target_pairs={{32,64},{64,32},{96,128},{128,96},{160,192},{192,160},{224,0},{0,2... | collective-permute-start | bytes 798728 | tf_op jit(solution)/shard_map/ppermute | solution.py:355
  28.8 4.9 %shard_map.98 = (f32[2,4,208,128]{3,2,1,0:T(8,128)S(1)}, f32[520,128]{1,0:T(8,128)S(1)}) custom-call(s32[14]{0:T(128)S(1)} %concatenate.4.flags, f32[2,4,256,128]{3,2,1,0:T(8,128)S(1)} %get-tuple-element.29.mid, f32[520,128]{1,0:T(8,128)} %collective-permute-done.3.on, f32[4,256,256]{2,1,0:T(8,128)S(1)} %get-tuple-element.32.roots, ...), custom_call_target="tpu_custom_call" | custom-call | flops 2147483648 | bytes 4194304 | tf_op jit(solution)/shard_map/pallas_call | solution.py:338
  33.7 3.4 %collective-permute-start.4 = (f32[520,128]{1,0:T(8,128)S(1)}, f32[520,128]{1,0:T(8,128)S(1)}, u32[]{:S(2)}, u32[]{:S(2)}) collective-permute-start(f32[520,128]{1,0:T(8,128)S(1)} %get-tuple-element.36), channel_id=1, source_target_pairs={{0,32},{32,0},{64,96},{96,64},{128,160},{160,128},{192,224},{224,1... | collective-permute-start | bytes 798728 | tf_op jit(solution)/shard_map/ppermute | solution.py:355
  37.1 0.0 collective-permute-done.2.off
  37.1 1.2 %collective-permute-done.4.on = f32[520,128]{1,0:T(8,128)S(1)} collective-permute-done((f32[520,128]{1,0:T(8,128)S(1)}, f32[520,128]{1,0:T(8,128)S(1)}, u32[]{:S(2)}, u32[]{:S(2)}) %collective-permute-start.4) | collective-permute-done | bytes 266272 | tf_op jit(solution)/shard_map/ppermute | solution.py:355
  38.2 4.7 %shard_map.99 = (f32[2,4,256,128]{3,2,1,0:T(8,128)S(1)}, f32[520,128]{1,0:T(8,128)S(1)}) custom-call(s32[14]{0:T(128)S(1)} %concatenate.4.flags, f32[2,4,256,128]{3,2,1,0:T(8,128)S(1)} %get-tuple-element.29.mid, f32[520,128]{1,0:T(8,128)S(1)} %collective-permute-done.2.off, f32[2,4,208,128]{3,2,1,0:T(8,128)S(1)} %get-tuple-element.35.part, ...), custom_call_target="tpu_custom_call" | custom-call | flops 2147483648 | bytes 4194304 | tf_op jit(solution)/shard_map/pallas_call | solution.py:338
  43.0 1.1 %collective-permute-start.5 = (f32[520,128]{1,0:T(8,128)S(1)}, f32[520,128]{1,0:T(8,128)S(1)}, u32[]{:S(2)}, u32[]{:S(2)}) collective-permute-start(f32[520,128]{1,0:T(8,128)S(1)} %get-tuple-element.38), channel_id=1, source_target_pairs={{32,64},{64,32},{96,128},{128,96},{160,192},{192,160},{224,0},{0,2... | collective-permute-start | bytes 798728 | tf_op jit(solution)/shard_map/ppermute | solution.py:355
  44.1 6.1 %collective-permute-done.5.off = f32[520,128]{1,0:T(8,128)S(1)} collective-permute-done((f32[520,128]{1,0:T(8,128)S(1)}, f32[520,128]{1,0:T(8,128)S(1)}, u32[]{:S(2)}, u32[]{:S(2)}) %collective-permute-start.5) | collective-permute-done | bytes 266272 | tf_op jit(solution)/shard_map/ppermute | solution.py:355
  50.1 1.0 shard_map.100
  51.1 0.1 collective-permute-start.6
  51.2 4.3 %collective-permute-start.7 = (f32[2,160,256]{2,1,0:T(8,128)S(1)}, f32[2,160,256]{2,1,0:T(8,128)S(1)}, u32[]{:S(2)}, u32[]{:S(2)}) collective-permute-start(f32[2,160,256]{2,1,0:T(8,128)S(1)} %get-tuple-element.41), channel_id=1, source_target_pairs={{1,2},{2,1},{3,4},{4,3},{5,6},{6,5},{7,8},{8,7},{9,10},{10,9},{11,... | collective-permute-start | bytes 983048 | tf_op jit(solution)/shard_map/ppermute | solution.py:355
  55.6 1.9 %collective-permute-done.6.even = f32[2,160,256]{2,1,0:T(8,128)S(1)} collective-permute-done((f32[2,160,256]{2,1,0:T(8,128)S(1)}, f32[2,160,256]{2,1,0:T(8,128)S(1)}, u32[]{:S(2)}, u32[]{:S(2)}) %collective-permute-start.6) | collective-permute-done | bytes 327712 | tf_op jit(solution)/shard_map/ppermute | solution.py:355
  57.5 10.9 %collective-permute-done.7.odd = f32[2,160,256]{2,1,0:T(8,128)S(1)} collective-permute-done((f32[2,160,256]{2,1,0:T(8,128)S(1)}, f32[2,160,256]{2,1,0:T(8,128)S(1)}, u32[]{:S(2)}, u32[]{:S(2)}) %collective-permute-start.7) | collective-permute-done | bytes 327712 | tf_op jit(solution)/shard_map/ppermute | solution.py:355
  68.3 1.3 %shard_map.101 = (f32[2,4,256,128]{3,2,1,0:T(8,128)S(1)}, f32[520,128]{1,0:T(8,128)S(1)}, f32[520,128]{1,0:T(8,128)S(1)}) custom-call(s32[14]{0:T(128)S(1)} %concatenate.4.flags, f32[2,4,256,128]{3,2,1,0:T(8,128)S(1)} %get-tuple-element.29.mid, f32[2,4,256,128]{3,2,1,0:T(8,128)S(1)} %get-tuple-element.39.total, ...), custom_call_target="tpu_custom_call", output_to_operand_aliasing={{0}: (1, {})} | custom-call | bytes 2097152 | tf_op jit(solution)/shard_map/pallas_call | solution.py:338
  69.6 2.9 %collective-permute-start.9 = (f32[520,128]{1,0:T(8,128)S(1)}, f32[520,128]{1,0:T(8,128)S(1)}, u32[]{:S(2)}, u32[]{:S(2)}) collective-permute-start(f32[520,128]{1,0:T(8,128)S(1)} %get-tuple-element.44), channel_id=1, source_target_pairs={{0,32},{32,0},{64,96},{96,64},{128,160},{160,128},{192,224},{224,1... | collective-permute-start | bytes 798728 | tf_op jit(solution)/shard_map/ppermute | solution.py:355
  72.5 0.8 collective-permute-start.8
  73.3 0.4 collective-permute-done.9.on
  73.7 4.5 %shard_map.102 = (f32[2,4,208,128]{3,2,1,0:T(8,128)S(1)}, f32[520,128]{1,0:T(8,128)S(1)}) custom-call(s32[14]{0:T(128)S(1)} %concatenate.4.flags, f32[2,4,256,128]{3,2,1,0:T(8,128)S(1)} %get-tuple-element.42.mid, f32[520,128]{1,0:T(8,128)S(1)} %collective-permute-done.9.on, f32[4,256,256]{2,1,0:T(8,128)S(1)} %get-tuple-element.32.roots, ...), custom_call_target="tpu_custom_call" | custom-call | flops 2147483648 | bytes 4194304 | tf_op jit(solution)/shard_map/pallas_call | solution.py:338
  78.2 0.4 collective-permute-start.10
  78.6 1.1 %collective-permute-done.8.off = f32[520,128]{1,0:T(8,128)S(1)} collective-permute-done((f32[520,128]{1,0:T(8,128)S(1)}, f32[520,128]{1,0:T(8,128)S(1)}, u32[]{:S(2)}, u32[]{:S(2)}) %collective-permute-start.8) | collective-permute-done | bytes 266272 | tf_op jit(solution)/shard_map/ppermute | solution.py:355
  79.7 0.1 collective-permute-done.10.on
  79.8 4.7 %shard_map.103 = (f32[2,4,256,128]{3,2,1,0:T(8,128)S(1)}, f32[520,128]{1,0:T(8,128)S(1)}) custom-call(s32[14]{0:T(128)S(1)} %concatenate.4.flags, f32[2,4,256,128]{3,2,1,0:T(8,128)S(1)} %get-tuple-element.42.mid, f32[520,128]{1,0:T(8,128)S(1)} %collective-permute-done.8.off, f32[2,4,208,128]{3,2,1,0:T(8,128)S(1)} %get-tuple-element.45.part, ...), custom_call_target="tpu_custom_call" | custom-call | flops 2147483648 | bytes 4194304 | tf_op jit(solution)/shard_map/pallas_call | solution.py:338
  84.5 2.3 %collective-permute-start.11 = (f32[520,128]{1,0:T(8,128)S(1)}, f32[520,128]{1,0:T(8,128)S(1)}, u32[]{:S(2)}, u32[]{:S(2)}) collective-permute-start(f32[520,128]{1,0:T(8,128)S(1)} %get-tuple-element.48), channel_id=1, source_target_pairs={{32,64},{64,32},{96,128},{128,96},{160,192},{192,160},{224,0},{0,2... | collective-permute-start | bytes 798728 | tf_op jit(solution)/shard_map/ppermute | solution.py:355
  86.7 5.7 %collective-permute-done.11.off = f32[520,128]{1,0:T(8,128)S(1)} collective-permute-done((f32[520,128]{1,0:T(8,128)S(1)}, f32[520,128]{1,0:T(8,128)S(1)}, u32[]{:S(2)}, u32[]{:S(2)}) %collective-permute-start.11) | collective-permute-done | bytes 266272 | tf_op jit(solution)/shard_map/ppermute | solution.py:355
  92.5 0.9 shard_map.104
  93.4 0.1 collective-permute-start.12
  93.5 5.7 %collective-permute-start.13 = (f32[2,80,256]{2,1,0:T(8,128)S(1)}, f32[2,80,256]{2,1,0:T(8,128)S(1)}, u32[]{:S(2)}, u32[]{:S(2)}) collective-permute-start(f32[2,80,256]{2,1,0:T(8,128)S(1)} %get-tuple-element.51), channel_id=1, source_target_pairs={{1,2},{2,1},{3,4},{4,3},{5,6},{6,5},{7,8},{8,7},{9,10},{10,9},{11,... | collective-permute-start | bytes 491528 | tf_op jit(solution)/shard_map/ppermute | solution.py:355
  99.1 0.0 collective-permute-done.12.even
  99.1 7.3 %collective-permute-done.13.odd = f32[2,80,256]{2,1,0:T(8,128)S(1)} collective-permute-done((f32[2,80,256]{2,1,0:T(8,128)S(1)}, f32[2,80,256]{2,1,0:T(8,128)S(1)}, u32[]{:S(2)}, u32[]{:S(2)}) %collective-permute-start.13) | collective-permute-done | bytes 163872 | tf_op jit(solution)/shard_map/ppermute | solution.py:355
  106.4 1.5 %shard_map.105 = (f32[256,256]{1,0:T(8,128)}, f32[256,256]{1,0:T(8,128)}) custom-call(s32[14]{0:T(128)S(1)} %concatenate.4.flags, f32[2,4,256,128]{3,2,1,0:T(8,128)S(1)} %get-tuple-element.42.mid, f32[2,4,256,128]{3,2,1,0:T(8,128)S(1)} %get-tuple-element.49.total, f32[2,80,256]{2,1,0:T(8,128)S(1)} %collective-permute-done.12.even, ...), custom_call_target="tpu_custom_call" | custom-call | bytes 2097152 | tf_op jit(solution)/shard_map/pallas_call | solution.py:338
  (13 shorter events, 0.0 us)
Async XLA Ops:
  2.1 19.8 %copy-start = (f32[1,1,4,256,256]{4,3,2,1,0:T(8,128)S(1)}, f32[1,1,4,256,256]{4,3,2,1,0:T(8,128)}, u32[]{:S(2)}) copy-start(f32[1,1,4,256,256]{4,3,2,1,0:T(8,128)} %param.12) | copy-start | bytes 3145732
  2.1 19.8 %copy-start.1 = (bf16[8,256,256]{2,1,0:T(8,128)(2,1)S(1)}, bf16[8,256,256]{2,1,0:T(8,128)(2,1)}, u32[]{:S(2)}) copy-start(bf16[8,256,256]{2,1,0:T(8,128)(2,1)} %constant.35.clone.tables) | copy-start | bytes 3145732
  2.8 7.3 %collective-permute-start = (f32[2,80,256]{2,1,0:T(8,128)S(1)}, f32[2,80,256]{2,1,0:T(8,128)S(1)}, u32[]{:S(2)}, u32[]{:S(2)}) collective-permute-start(f32[2,80,256]{2,1,0:T(8,128)S(1)} %get-tuple-element.27), channel_id=1, source_target_pairs={{0,1},{1,0},{2,3},{3,2},{4,5},{5,4},{6,7},{7,6},{8,9},{9,8},{10,11... | collective-permute-start | bytes 491528 | tf_op jit(solution)/shard_map/ppermute | solution.py:355
  5.3 16.5 %copy-start.2 = (f32[256,256]{1,0:T(8,128)S(1)}, f32[256,256]{1,0:T(8,128)}, u32[]{:S(2)}) copy-start(f32[256,256]{1,0:T(8,128)} %probe_re.1) | copy-start | bytes 786436
  5.4 12.0 %collective-permute-start.1 = (f32[2,80,256]{2,1,0:T(8,128)S(1)}, f32[2,80,256]{2,1,0:T(8,128)S(1)}, u32[]{:S(2)}, u32[]{:S(2)}) collective-permute-start(f32[2,80,256]{2,1,0:T(8,128)S(1)} %get-tuple-element.28), channel_id=1, source_target_pairs={{1,2},{2,1},{3,4},{4,3},{5,6},{6,5},{7,8},{8,7},{9,10},{10,9},{11,... | collective-permute-start | bytes 491528 | tf_op jit(solution)/shard_map/ppermute | solution.py:355
  18.9 0.7 copy-start.4
  19.6 2.0 %copy-start.6 = (s32[1,1,4,2]{2,3,1,0:T(2,128)S(1)}, s32[1,1,4,2]{2,3,1,0:T(2,128)}, u32[]{:S(2)}) copy-start(s32[1,1,4,2]{2,3,1,0:T(2,128)} %param.13) | copy-start | bytes 100
  19.6 9.2 %collective-permute-start.3 = (f32[520,128]{1,0:T(8,128)}, f32[520,128]{1,0:T(8,128)}, u32[]{:S(2)}, u32[]{:S(2)}) collective-permute-start(f32[520,128]{1,0:T(8,128)} %get-tuple-element.31), channel_id=1, source_target_pairs={{0,32},{32,0},{64,96},{96,64},{128,160},{160,128},{192,224},{224,1... | collective-permute-start | bytes 798728 | tf_op jit(solution)/shard_map/ppermute | solution.py:355
  21.9 1.0 copy-start.3
  22.9 2.9 %copy-start.5 = (f32[520,128]{1,0:T(8,128)S(1)}, f32[520,128]{1,0:T(8,128)}, u32[]{:S(2)}) copy-start(f32[520,128]{1,0:T(8,128)} %copy-done.4) | copy-start | bytes 798724
  25.8 11.3 %collective-permute-start.2 = (f32[520,128]{1,0:T(8,128)S(1)}, f32[520,128]{1,0:T(8,128)S(1)}, u32[]{:S(2)}, u32[]{:S(2)}) collective-permute-start(f32[520,128]{1,0:T(8,128)S(1)} %copy-done.5), channel_id=1, source_target_pairs={{32,64},{64,32},{96,128},{128,96},{160,192},{192,160},{224,0},{0,2... | collective-permute-start | bytes 798728 | tf_op jit(solution)/shard_map/ppermute | solution.py:355
  33.7 4.6 %collective-permute-start.4 = (f32[520,128]{1,0:T(8,128)S(1)}, f32[520,128]{1,0:T(8,128)S(1)}, u32[]{:S(2)}, u32[]{:S(2)}) collective-permute-start(f32[520,128]{1,0:T(8,128)S(1)} %get-tuple-element.36), channel_id=1, source_target_pairs={{0,32},{32,0},{64,96},{96,64},{128,160},{160,128},{192,224},{224,1... | collective-permute-start | bytes 798728 | tf_op jit(solution)/shard_map/ppermute | solution.py:355
  43.0 7.2 %collective-permute-start.5 = (f32[520,128]{1,0:T(8,128)S(1)}, f32[520,128]{1,0:T(8,128)S(1)}, u32[]{:S(2)}, u32[]{:S(2)}) collective-permute-start(f32[520,128]{1,0:T(8,128)S(1)} %get-tuple-element.38), channel_id=1, source_target_pairs={{32,64},{64,32},{96,128},{128,96},{160,192},{192,160},{224,0},{0,2... | collective-permute-start | bytes 798728 | tf_op jit(solution)/shard_map/ppermute | solution.py:355
  51.1 6.3 %collective-permute-start.6 = (f32[2,160,256]{2,1,0:T(8,128)S(1)}, f32[2,160,256]{2,1,0:T(8,128)S(1)}, u32[]{:S(2)}, u32[]{:S(2)}) collective-permute-start(f32[2,160,256]{2,1,0:T(8,128)S(1)} %get-tuple-element.40), channel_id=1, source_target_pairs={{0,1},{1,0},{2,3},{3,2},{4,5},{5,4},{6,7},{7,6},{8,9},{9,8},{10,11... | collective-permute-start | bytes 983048 | tf_op jit(solution)/shard_map/ppermute | solution.py:355
  51.2 17.1 %collective-permute-start.7 = (f32[2,160,256]{2,1,0:T(8,128)S(1)}, f32[2,160,256]{2,1,0:T(8,128)S(1)}, u32[]{:S(2)}, u32[]{:S(2)}) collective-permute-start(f32[2,160,256]{2,1,0:T(8,128)S(1)} %get-tuple-element.41), channel_id=1, source_target_pairs={{1,2},{2,1},{3,4},{4,3},{5,6},{6,5},{7,8},{8,7},{9,10},{10,9},{11,... | collective-permute-start | bytes 983048 | tf_op jit(solution)/shard_map/ppermute | solution.py:355
  69.6 4.1 %collective-permute-start.9 = (f32[520,128]{1,0:T(8,128)S(1)}, f32[520,128]{1,0:T(8,128)S(1)}, u32[]{:S(2)}, u32[]{:S(2)}) collective-permute-start(f32[520,128]{1,0:T(8,128)S(1)} %get-tuple-element.44), channel_id=1, source_target_pairs={{0,32},{32,0},{64,96},{96,64},{128,160},{160,128},{192,224},{224,1... | collective-permute-start | bytes 798728 | tf_op jit(solution)/shard_map/ppermute | solution.py:355
  72.5 7.2 %collective-permute-start.8 = (f32[520,128]{1,0:T(8,128)S(1)}, f32[520,128]{1,0:T(8,128)S(1)}, u32[]{:S(2)}, u32[]{:S(2)}) collective-permute-start(f32[520,128]{1,0:T(8,128)S(1)} %get-tuple-element.43), channel_id=1, source_target_pairs={{32,64},{64,32},{96,128},{128,96},{160,192},{192,160},{224,0},{0,2... | collective-permute-start | bytes 798728 | tf_op jit(solution)/shard_map/ppermute | solution.py:355
  78.2 1.6 %collective-permute-start.10 = (f32[520,128]{1,0:T(8,128)S(1)}, f32[520,128]{1,0:T(8,128)S(1)}, u32[]{:S(2)}, u32[]{:S(2)}) collective-permute-start(f32[520,128]{1,0:T(8,128)S(1)} %get-tuple-element.46), channel_id=1, source_target_pairs={{0,32},{32,0},{64,96},{96,64},{128,160},{160,128},{192,224},{224,1... | collective-permute-start | bytes 798728 | tf_op jit(solution)/shard_map/ppermute | solution.py:355
  84.5 8.0 %collective-permute-start.11 = (f32[520,128]{1,0:T(8,128)S(1)}, f32[520,128]{1,0:T(8,128)S(1)}, u32[]{:S(2)}, u32[]{:S(2)}) collective-permute-start(f32[520,128]{1,0:T(8,128)S(1)} %get-tuple-element.48), channel_id=1, source_target_pairs={{32,64},{64,32},{96,128},{128,96},{160,192},{192,160},{224,0},{0,2... | collective-permute-start | bytes 798728 | tf_op jit(solution)/shard_map/ppermute | solution.py:355
  93.4 5.8 %collective-permute-start.12 = (f32[2,80,256]{2,1,0:T(8,128)S(1)}, f32[2,80,256]{2,1,0:T(8,128)S(1)}, u32[]{:S(2)}, u32[]{:S(2)}) collective-permute-start(f32[2,80,256]{2,1,0:T(8,128)S(1)} %get-tuple-element.50), channel_id=1, source_target_pairs={{0,1},{1,0},{2,3},{3,2},{4,5},{5,4},{6,7},{7,6},{8,9},{9,8},{10,11... | collective-permute-start | bytes 491528 | tf_op jit(solution)/shard_map/ppermute | solution.py:355
  93.5 13.0 %collective-permute-start.13 = (f32[2,80,256]{2,1,0:T(8,128)S(1)}, f32[2,80,256]{2,1,0:T(8,128)S(1)}, u32[]{:S(2)}, u32[]{:S(2)}) collective-permute-start(f32[2,80,256]{2,1,0:T(8,128)S(1)} %get-tuple-element.51), channel_id=1, source_target_pairs={{1,2},{2,1},{3,4},{4,3},{5,6},{6,5},{7,8},{8,7},{9,10},{10,9},{11,... | collective-permute-start | bytes 491528 | tf_op jit(solution)/shard_map/ppermute | solution.py:355

commit v4 on v3

v4 whole, which is shorter than its diff:
```python
import functools
import math

import jax
import jax.numpy as jnp
import numpy as np
from jax import lax
from jax.experimental import pallas as pl
from jax.experimental.pallas import tpu as pltpu
from jax.sharding import PartitionSpec as P

ITERS = 2

smoothing = 0.01
step_size = 0.25

W = 256
H = 128
REACH = 80
PART = W // 2 + REACH
HALF = PART + REACH

VMEM = pl.BlockSpec(memory_space=pltpu.VMEM)
SMEM = pl.BlockSpec(memory_space=pltpu.SMEM)
ANY = pl.BlockSpec(memory_space=pltpu.HBM)
f32 = jnp.float32
bf16 = jnp.bfloat16


def shape(*dims):
    return jax.ShapeDtypeStruct(dims, f32)


def dft_tables():
    k = np.arange(H)[:, None]
    mats = []
    for odd in (0, 1):
        freq = 2 * np.arange(H)[None, :] + odd
        angle = -2.0 * math.pi * ((k * freq) % W) / W
        c, s = np.cos(angle) / 16.0, np.sin(angle) / 16.0
        mats.append(np.block([[c, s], [-s, c]]))
    mats = [mats[0], mats[1], mats[0].T, mats[1].T]
    out = []
    for m in mats:
        m = m.astype(np.float32)
        hi = m.astype(jnp.bfloat16)
        lo = (m - hi.astype(np.float32)).astype(jnp.bfloat16)
        out.extend([hi, lo])
    return np.stack(out)


def split(x):
    hi = x.astype(bf16)
    lo = (x - hi.astype(f32)).astype(bf16)
    return hi, lo


def dot(a, b):
    return lax.dot_general(a, b, (((1,), (0,)), ((), ())), preferred_element_type=f32)


def right(x, tables, i):
    hi, lo = split(x)
    t_hi, t_lo = tables[2 * i], tables[2 * i + 1]
    return dot(
        jnp.concatenate([hi, lo, hi], axis=1), jnp.concatenate([t_hi, t_hi, t_lo], axis=0)
    )


def left(tables, i, x):
    hi, lo = split(x)
    t_hi, t_lo = tables[2 * i], tables[2 * i + 1]
    return dot(
        jnp.concatenate([t_hi, t_hi, t_lo], axis=1), jnp.concatenate([hi, lo, hi], axis=0)
    )


def cat(a, b, axis):
    return jnp.concatenate([a, b], axis=axis)


def roots_kernel(
    flags, intensity, probe_re, probe_im, tables, out, probe_out, tables_out, held, sems
):
    slots = out.shape[0]
    copies = [pltpu.make_async_copy(intensity.at[p], held.at[p], sems.at[p]) for p in range(slots)]
    for comp, x in enumerate((probe_re, probe_im)):
        for j in range(2):
            k = 2 * comp + j
            copies.append(
                pltpu.make_async_copy(
                    x.at[:, pl.ds(j * H, H)], probe_out.at[comp, j], sems.at[slots + k]
                )
            )
    copies.append(pltpu.make_async_copy(tables, tables_out, sems.at[slots + 4]))
    for c in copies:
        c.start()
    row = lax.broadcasted_iota(jnp.int32, (W, W), 0)
    col = lax.broadcasted_iota(jnp.int32, (W, W), 1)
    source = jnp.where(col < H, 2 * col, 2 * (col - H) + 1)
    perm = jnp.where(row == source, 1.0, 0.0).astype(bf16)
    perm3 = jnp.concatenate([perm, perm, perm], axis=0)
    for p in range(slots):
        copies[p].wait()
        x = jnp.sqrt(held[p])
        hi = x.astype(bf16)
        rest = x - hi.astype(f32)
        mid = rest.astype(bf16)
        lo = (rest - mid.astype(f32)).astype(bf16)
        y = dot(jnp.concatenate([hi, mid, lo], axis=1), perm3)
        y = y.reshape(H, 2, W)
        out[p, pl.ds(0, H), :] = y[:, 0, :]
        out[p, pl.ds(H, H), :] = y[:, 1, :]
    for c in copies[slots:]:
        c.wait()


OFFSETS = 5
COUNT = 13
GAP = H - REACH
SIDE = 3 * REACH + 24


def rows_at(start, size):
    return pl.ds(pl.multiple_of(start, 8), size)


def side(flags, odd):
    left = 1 - flags[0] if odd else flags[0]
    return left, 2 - left, 3 - 3 * left


def inside(flags, odd):
    return flags[2] + flags[3] == 0 if odd else None


def masked(keep, x):
    return x if keep is None else jnp.where(keep, x, 0.0)


def own_columns(left, x):
    return jnp.where(left == 1, x[:REACH], x[GAP:])


def margin_columns(left, x):
    return jnp.where(left == 1, x[GAP:], x[:REACH])


def columns_out(flags, odd, tiles, out):
    left, inner, outer = side(flags, odd)
    for comp in range(2):
        if out.shape[1] == REACH:
            out[comp] = margin_columns(left, tiles[comp, outer].T)
        else:
            out[comp, 0:REACH] = own_columns(left, tiles[comp, inner].T)
            out[comp, REACH:] = margin_columns(left, tiles[comp, outer].T)


def columns_at(low, x):
    blank = jnp.zeros((GAP, W), f32)
    return jnp.where(low, cat(x, blank, 0), cat(blank, x, 0)).T


def pack_side(flags, odd, tiles, rows, out):
    left, inner, outer = side(flags, odd)
    lane = lax.broadcasted_iota(jnp.int32, (REACH, H), 1)
    for comp in range(2):
        out[pl.ds(comp * REACH, REACH), :] = tiles[comp, inner, rows, :]
    re, im = (pltpu.roll(tiles[comp, outer, rows, :], REACH * left, 1) for comp in range(2))
    out[pl.ds(2 * REACH, REACH), :] = jnp.where(lane < REACH, re, pltpu.roll(im, REACH, 1))
    rest = jnp.zeros((24, H), f32)
    for g in range(4):
        part = im[24 * g : min(24 * g + 24, REACH)]
        part = pltpu.roll(part, (32 * g - GAP) % H, 1)
        if part.shape[0] < 24:
            part = cat(part, jnp.zeros((24 - part.shape[0], H), f32), 0)
        rest = jnp.where(lane[:24] // 32 == g, part, rest)
    out[pl.ds(3 * REACH, 24), :] = rest


def unpack_side(flags, odd, packed, keep):
    left, _, _ = side(flags, odd)
    lane = lax.broadcasted_iota(jnp.int32, (REACH, H), 1)
    mixed = masked(keep, packed[pl.ds(2 * REACH, REACH), :])
    rest = masked(keep, packed[pl.ds(3 * REACH, 24), :])
    tail = jnp.concatenate(
        [pltpu.roll(rest, (GAP - 32 * g) % H, 1)[: min(24, REACH - 24 * g)] for g in range(4)], axis=0
    )
    re = jnp.where(lane < REACH, mixed, 0.0)
    im = jnp.where(lane < GAP, pltpu.roll(mixed, GAP, 1), jnp.where(lane < REACH, tail, 0.0))
    return [
        (masked(keep, packed[pl.ds(comp * REACH, REACH), :]), pltpu.roll(x, GAP * left, 1))
        for comp, x in enumerate((re, im))
    ]


def put_side(flags, odd, packed, tiles, rows, add):
    _, inner, outer = side(flags, odd)
    for comp, pair in enumerate(unpack_side(flags, odd, packed, flags[4] == 0)):
        for tile, x in zip((inner, outer), pair):
            if add:
                tiles[comp, tile, rows, :] += x
            else:
                tiles[comp, tile, rows, :] = x


def first_kernel(flags, mid, even, odd):
    for is_odd, out in enumerate((even, odd)):
        left, inner, _ = side(flags, is_odd)
        for comp in range(2):
            out[comp] = own_columns(left, mid[comp, inner].T)


def send_rows(flags, odd, tiles, off, on):
    pack_side(flags, odd, tiles, rows_at((W - REACH) * flags[1], REACH), off)
    for ref in on:
        ref[...] = tiles[:, :, rows_at((W - REACH) * (1 - flags[1]), REACH), :]


def margin_kernel(odd, flags, strip, mid, out, off, *on):
    left, _, outer = side(flags, odd)
    for comp in range(2):
        out[comp, outer] = columns_at(left == 0, masked(inside(flags, odd), strip[comp]))
    send_rows(flags, odd, out, off, on)


def half_gradient(a, flags, roots, probe, tables, ext, acc):
    acc[...] = jnp.zeros(acc.shape, f32)
    lane = lax.broadcasted_iota(jnp.int32, (W, H), 1)

    def position(base, carry):
        p = 2 * a + base
        shift = flags[OFFSETS + 2 * p + 1] - H * base
        rows = pl.ds(flags[OFFSETS + 2 * p] - (H - REACH) - H * a, W)
        o = []
        for comp in range(2):
            rolled = [pltpu.roll(ext[comp, base + j, rows, :], H - shift, 1) for j in range(3)]
            o.append([jnp.where(lane < H - shift, rolled[j], rolled[j + 1]) for j in range(2)])
        w_re, w_im = [], []
        for j in range(2):
            p_re, p_im = probe[0, j], probe[1, j]
            w_re.append(o[0][j] * p_re - o[1][j] * p_im)
            w_im.append(o[0][j] * p_im + o[1][j] * p_re)
        e = right(cat(w_re[0] + w_re[1], w_im[0] + w_im[1], 1), tables, 0)
        d = right(cat(w_re[0] - w_re[1], w_im[0] - w_im[1], 1), tables, 1)
        h_re = cat(e[:, :H], d[:, :H], 1)
        h_im = cat(e[:, H:], d[:, H:], 1)
        far_e = left(tables, 2, cat(h_re[:H] + h_re[H:], h_im[:H] + h_im[H:], 0))
        far_d = left(tables, 3, cat(h_re[:H] - h_re[H:], h_im[:H] - h_im[H:], 0))

        def residual(far, root):
            power = far[:H] * far[:H] + far[H:] * far[H:] + smoothing
            factor = 1.0 - root * lax.rsqrt(power)
            return far * cat(factor, factor, 0)

        x = left(tables, 0, residual(far_e, roots[p, pl.ds(0, H), :]))
        y = left(tables, 1, residual(far_d, roots[p, pl.ds(H, H), :]))
        upper, lower = x + y, x - y
        h_re = cat(upper[:H], lower[:H], 0)
        h_im = cat(upper[H:], lower[H:], 0)
        x = right(cat(h_re[:, :H], h_im[:, :H], 1), tables, 2)
        y = right(cat(h_re[:, H:], h_im[:, H:], 1), tables, 3)
        weight = jnp.where(p < flags[COUNT], 1.0, 0.0).astype(f32)
        g_re, g_im = [], []
        for j, z in enumerate((x + y, x - y)):
            p_re, p_im = probe[0, j] * weight, probe[1, j] * weight
            g_re.append(z[:, :H] * p_re + z[:, H:] * p_im)
            g_im.append(z[:, H:] * p_re - z[:, :H] * p_im)
        for comp, g in enumerate((g_re, g_im)):
            r = [pltpu.roll(g[j], shift, 1) for j in range(2)]
            acc[comp, base, rows, :] += jnp.where(lane >= shift, r[0], 0.0)
            acc[comp, base + 1, rows, :] += jnp.where(lane >= shift, r[1], r[0])
            acc[comp, base + 2, rows, :] += jnp.where(lane < shift, r[1], 0.0)
        return carry

    lax.fori_loop(0, 2, position, 0)


def margin_rows(a):
    return rows_at(PART * a, REACH)


def own_rows(a):
    return rows_at(REACH - REACH * a, PART)


def covered_rows(a):
    return rows_at((W - PART) * a, PART)


def load_half(a, mid, ext):
    ext[:, :, own_rows(a), :] = mid[:, :, covered_rows(a), :]


def on_kernel(flags, mid, on, roots, probe, tables, part, to_on, ext, acc):
    a = 1 - flags[1]
    load_half(a, mid, ext)
    ext[:, :, margin_rows(a), :] = on[...]
    half_gradient(a, flags, roots, probe, tables, ext, acc)
    part[...] = acc[:, :, own_rows(a), :]
    to_on[...] = acc[:, :, margin_rows(a), :]


def off_kernel(flags, mid, even, odd, part, on, roots, probe, tables, centre, to_even, to_odd, ext, acc):
    a = flags[1]
    load_half(a, mid, ext)
    put_side(flags, 0, even, ext, margin_rows(a), False)
    put_side(flags, 1, odd, ext, margin_rows(a), False)
    half_gradient(a, flags, roots, probe, tables, ext, acc)
    pack_side(flags, 0, acc, margin_rows(a), to_even)
    pack_side(flags, 1, acc, margin_rows(a), to_odd)
    centre[...] = jnp.zeros(centre.shape, f32)
    centre[:, :, covered_rows(1 - a), :] = part[...]
    centre[:, :, covered_rows(a), :] += acc[:, :, own_rows(a), :]
    centre[:, :, rows_at((W - REACH) * (1 - a), REACH), :] += on[...]


def rows_kernel(odd, flags, centre, off, total, strip):
    put_side(flags, odd, off, total, rows_at((W - REACH) * flags[1], REACH), True)
    columns_out(flags, odd, total, strip)


def step_kernel(odd, flags, mid, total, strip, out, off, *on):
    left, inner, outer = side(flags, odd)
    keep = inside(flags, odd)
    for comp in range(2):
        got = masked(keep, strip[comp])
        x = total[comp, outer] + columns_at(left == 0, got[:REACH])
        out[comp, outer] = masked(keep, mid[comp, outer] - step_size * x)
        x = total[comp, inner] + columns_at(left == 1, got[REACH:])
        out[comp, inner] = mid[comp, inner] - step_size * x
    send_rows(flags, odd, out, off, on)


def final_kernel(flags, mid, total, even, odd, out_re, out_im):
    for comp, out in enumerate((out_re, out_im)):
        for is_odd, strip in enumerate((even, odd)):
            left, inner, _ = side(flags, is_odd)
            got = columns_at(left == 1, masked(inside(flags, is_odd), strip[comp]))
            value = mid[comp, inner] - step_size * (total[comp, inner] + got)
            out[:, pl.ds(pl.multiple_of(H * (inner - 1), H), H)] = value


def call(kernel, specs, out_shape, *args, scratch=(), flops=0, read=0, alias={}):
    return pl.pallas_call(
        kernel,
        in_specs=[SMEM] + specs + [VMEM] * (len(args) - 1 - len(specs)),
        out_specs=jax.tree.map(lambda _: VMEM, out_shape),
        out_shape=out_shape,
        scratch_shapes=scratch,
        input_output_aliases=alias,
        compiler_params=pltpu.CompilerParams(vmem_limit_bytes=24 * 1024 * 1024),
        cost_estimate=pl.CostEstimate(flops=flops, bytes_accessed=read, transcendentals=0),
    )(*args)


def swaps(size, bit):
    return [p for i in range(bit, size, 2) for p in ((i, (i + 1) % size), ((i + 1) % size, i))]


def swap(x, axis, bit):
    return lax.ppermute(x, axis, swaps(lax.axis_size(axis), bit))


def shards(object_re, object_im, probe_re, probe_im, intensity, offsets, counts):
    slots = intensity.shape[2]
    column, row = lax.axis_index("col"), lax.axis_index("row")
    last, lowest = lax.axis_size("col") - 1, lax.axis_size("row") - 1
    edge = (row == 0) | (row == lowest)
    flags = jnp.stack([column % 2, row % 2, column == 0, column == last, edge]).astype(jnp.int32)
    known = jnp.concatenate([flags, offsets.reshape(-1), counts.reshape(-1)])

    tile = shape(W, W)
    narrow = shape(2, REACH, W)
    wide = shape(2, 2 * REACH, W)
    half = shape(SIDE, H)
    rows = shape(2, 4, REACH, H)
    full = shape(2, 4, W, H)
    part = shape(2, 4, PART, H)
    halves = [pltpu.VMEM((2, 4, HALF, H), f32)] * 2

    def named(kernel, *args, **options):
        return call(kernel, [], *args, **options)

    for sweep in range(ITERS + 1):
        if sweep == 0:
            blank = jnp.zeros((W, H), f32)
            mid = jnp.stack(
                [jnp.stack([blank, x[:, 0:H], x[:, H:W], blank]) for x in (object_re, object_im)]
            )
            even, odd = named(first_kernel, (narrow, narrow), flags, mid, read=1 << 20)
            even, odd = swap(even, "col", 0), swap(odd, "col", 1)
            tables = jnp.asarray(dft_tables())
            fixed = call(
                roots_kernel,
                [ANY] * 4,
                (shape(slots, W, W), shape(2, 2, W, H), jax.ShapeDtypeStruct(tables.shape, bf16)),
                known, intensity[0, 0], probe_re, probe_im, tables,
                scratch=[pltpu.VMEM((slots, W, W), f32), pltpu.SemaphoreType.DMA((slots + 5,))],
                flops=1 << 29, read=1 << 21,
            )
        else:
            strip = narrow if sweep == ITERS else wide
            to_even = swap(to_even, "row", 1)
            to_odd = swap(to_odd, "row", 1)
            total, even = named(
                functools.partial(rows_kernel, 0), (full, strip), known, total, to_even,
                read=1 << 20, alias={1: 0},
            )
            even = swap(even, "col", 0)
            total, odd = named(
                functools.partial(rows_kernel, 1), (full, strip), known, total, to_odd,
                read=1 << 20, alias={1: 0},
            )
            odd = swap(odd, "col", 1)
        if sweep == ITERS:
            return named(final_kernel, (tile, tile), known, mid, total, even, odd, read=1 << 21)
        if sweep == 0:
            mid, to_even = named(
                functools.partial(margin_kernel, 0), (full, half), known, even, mid,
                read=1 << 20, alias={2: 0},
            )
            to_even = swap(to_even, "row", 1)
            mid, to_odd, on = named(
                functools.partial(margin_kernel, 1), (full, half, rows), known, odd, mid,
                read=1 << 20, alias={2: 0},
            )
        else:
            mid, to_even = named(
                functools.partial(step_kernel, 0), (full, half), known, mid, total, even,
                read=1 << 20, alias={1: 0},
            )
            to_even = swap(to_even, "row", 1)
            mid, to_odd, on = named(
                functools.partial(step_kernel, 1), (full, half, rows), known, mid, total, odd,
                read=1 << 20, alias={1: 0},
            )
        on = swap(on, "row", 0)
        to_odd = swap(to_odd, "row", 1)
        upper, on = named(
            on_kernel, (part, rows), known, mid, on, *fixed,
            scratch=halves, flops=1 << 31, read=1 << 22,
        )
        on = swap(on, "row", 0)
        total, to_even, to_odd = named(
            off_kernel, (full, half, half), known, mid, to_even, to_odd, upper, on, *fixed,
            scratch=halves, flops=1 << 31, read=1 << 22,
        )


def solution(mesh):
    return jax.shard_map(
        shards,
        mesh=mesh,
        in_specs=(
            P("row", "col"),
            P("row", "col"),
            P(),
            P(),
            P("row", "col", None, None, None),
            P("row", "col", None, None),
            P("row", "col"),
        ),
        out_specs=(P("row", "col"), P("row", "col")),
        check_vma=False,
    )
```

time: 108 us -> 111 us (1.028)
  the two profiles are of different devices: /device:TPU:1 before, /device:TPU:69 now
where the time goes in v4:
time: 111 us; the launch traced here: 109 us
  waiting for transfers between devices  45.5 us (41%)
  Pallas kernels  30.6 us (28%)
  starting transfers between devices  29.9 us (27%)
  local copies, waits for them, and re-layouts  1.51 us (1%)
  between operations  1.51 us (1%)
    ppermute x18, waiting for transfers between devices, swap(): return lax.ppermute(x, axis, swaps(lax.axis_size(axis), bit))  45.5 us
    pallas_call x15, Pallas kernels, call(): pl.pallas_call(kernel, in_specs=[SMEM] + specs + [VMEM] * (len(args) - 1...  30.6 us
    ppermute x18, starting transfers between devices, swap(): return lax.ppermute(x, axis, swaps(lax.axis_size(axis), bit))  29.9 us
  transfers between devices with their start and end apart: 18, of which 13 were waited for; matrix products, arithmetic and copies ran while one was open for 0% of the time, Pallas kernels for 7%

profile of v4, /device:TPU:69, one launch (start us, length us, event | category | flops | bytes accessed | tf_op | source)
XLA Modules:
  0.0 109.3 jit_solution(6641732470900675991)
XLA Ops:
  0.7 1.1 %slice_bitcast_fusion.1 = (f32[1,256,128]{2,1,0:T(8,128)S(1)}, f32[1,256,128]{2,1,0:T(8,128)S(1)}, f32[1,256,128]{2,1,0:T(8,128)S(1)}, f32[1,256,128]{2,1,0:T(8,128)S(1)}) fusion(f32[256,256]{1,0:T(8,128)} %param.9, f32[256,256]{1,0:T(8,128)} %param.8), kind=kLoop, calls=%fused_computation.10 | loop fusion | bytes 1048576 | tf_op jit(solution)/shard_map/stack | solution.py:389
  2.0 0.1 stack.62.flags
  2.1 0.7 shard_map.95
  2.8 1.7 %collective-permute-start.1 = (f32[2,80,256]{2,1,0:T(8,128)S(1)}, f32[2,80,256]{2,1,0:T(8,128)S(1)}, u32[]{:S(2)}, u32[]{:S(2)}) collective-permute-start(f32[2,80,256]{2,1,0:T(8,128)S(1)} %get-tuple-element.36), channel_id=1, source_target_pairs={{0,1},{1,0},{2,3},{3,2},{4,5},{5,4},{6,7},{7,6},{8,9},{9,8},{10,11... | collective-permute-start | bytes 491528 | tf_op jit(solution)/shard_map/ppermute | solution.py:362
  4.5 2.5 %collective-permute-start = (f32[2,80,256]{2,1,0:T(8,128)S(1)}, f32[2,80,256]{2,1,0:T(8,128)S(1)}, u32[]{:S(2)}, u32[]{:S(2)}) collective-permute-start(f32[2,80,256]{2,1,0:T(8,128)S(1)} %get-tuple-element.35), channel_id=1, source_target_pairs={{1,2},{2,1},{3,4},{4,3},{5,6},{6,5},{7,8},{8,7},{9,10},{10,9},{11,... | collective-permute-start | bytes 491528 | tf_op jit(solution)/shard_map/ppermute | solution.py:362
  7.7 0.1 copy.19
  7.9 0.1 concatenate.4.flags
  8.0 0.3 collective-permute-done.1.strip
  8.3 0.8 shard_map.96
  9.2 5.1 %collective-permute-done.strip = f32[2,80,256]{2,1,0:T(8,128)S(1)} collective-permute-done((f32[2,80,256]{2,1,0:T(8,128)S(1)}, f32[2,80,256]{2,1,0:T(8,128)S(1)}, u32[]{:S(2)}, u32[]{:S(2)}) %collective-permute-start) | collective-permute-done | bytes 163872 | tf_op jit(solution)/shard_map/ppermute | solution.py:362
  14.3 0.9 shard_map.97
  15.1 1.4 %collective-permute-start.4 = (f32[2,4,80,128]{3,2,1,0:T(8,128)S(1)}, f32[2,4,80,128]{3,2,1,0:T(8,128)S(1)}, u32[]{:S(2)}, u32[]{:S(2)}) collective-permute-start(f32[2,4,80,128]{3,2,1,0:T(8,128)S(1)} %get-tuple-element.41), channel_id=1, source_target_pairs={{0,32},{32,0},{64,96},{96,64},{128,160},{160,128},{192,224},{224,1... | collective-permute-start | bytes 983048 | tf_op jit(solution)/shard_map/ppermute | solution.py:362
  16.6 2.9 %shard_map.98 = (f32[4,256,256]{2,1,0:T(8,128)S(1)}, f32[2,2,256,128]{3,2,1,0:T(8,128)S(1)}, bf16[8,256,256]{2,1,0:T(8,128)(2,1)S(1)}) custom-call(s32[14]{0:T(128)S(1)} %concatenate.4.flags, f32[4,256,256]{2,1,0:T(8,128)S(1)} %bitcast.20, f32[256,256]{1,0:T(8,128)S(1)} %copy-done.2, f32[256,256]{1,0:T(8,128)S(1)} %copy-done.3, ...), custom_call_target="tpu_custom_call" | custom-call | flops 536870912 | bytes 2097152 | tf_op jit(solution)/shard_map/pallas_call | solution.py:345
  19.5 4.5 %shard_map.99 = (f32[2,4,208,128]{3,2,1,0:T(8,128)S(1)}, f32[2,4,80,128]{3,2,1,0:T(8,128)S(1)}) custom-call(s32[14]{0:T(128)S(1)} %concatenate.4.flags, f32[2,4,256,128]{3,2,1,0:T(8,128)S(1)} %get-tuple-element.38.mid, f32[2,4,80,128]{3,2,1,0:T(8,128)S(1)} %collective-permute-done.4.on, f32[4,256,256]{2,1,0:T(8,128)S(1)} %get-tuple-element.42.roots, ...), custom_call_target="tpu_custom_call" | custom-call | flops 2147483648 | bytes 4194304 | tf_op jit(solution)/shard_map/pallas_call | solution.py:345
  24.0 0.1 collective-permute-start.5
  24.2 4.4 %collective-permute-start.2 = (f32[264,128]{1,0:T(8,128)S(1)}, f32[264,128]{1,0:T(8,128)S(1)}, u32[]{:S(2)}, u32[]{:S(2)}) collective-permute-start(f32[264,128]{1,0:T(8,128)S(1)} %get-tuple-element.39), channel_id=1, source_target_pairs={{32,64},{64,32},{96,128},{128,96},{160,192},{192,160},{224,0},{0,2... | collective-permute-start | bytes 405512 | tf_op jit(solution)/shard_map/ppermute | solution.py:362
  28.6 3.4 %collective-permute-done.2.even = f32[264,128]{1,0:T(8,128)S(1)} collective-permute-done((f32[264,128]{1,0:T(8,128)S(1)}, f32[264,128]{1,0:T(8,128)S(1)}, u32[]{:S(2)}, u32[]{:S(2)}) %collective-permute-start.2) | collective-permute-done | bytes 135200 | tf_op jit(solution)/shard_map/ppermute | solution.py:362
  32.0 3.5 %collective-permute-done.3.odd = f32[264,128]{1,0:T(8,128)S(1)} collective-permute-done((f32[264,128]{1,0:T(8,128)S(1)}, f32[264,128]{1,0:T(8,128)S(1)}, u32[]{:S(2)}, u32[]{:S(2)}) %collective-permute-start.3) | collective-permute-done | bytes 135200 | tf_op jit(solution)/shard_map/ppermute | solution.py:362
  35.4 4.8 %shard_map.100 = (f32[2,4,256,128]{3,2,1,0:T(8,128)S(1)}, f32[264,128]{1,0:T(8,128)S(1)}, f32[264,128]{1,0:T(8,128)S(1)}) custom-call(s32[14]{0:T(128)S(1)} %concatenate.4.flags, f32[2,4,256,128]{3,2,1,0:T(8,128)S(1)} %get-tuple-element.38.mid, f32[264,128]{1,0:T(8,128)S(1)} %collective-permute-done.2.even, f32[264,128]{1,0:T(8,128)S(1)} %collective-permute-done.3.odd, ...), custom_call_target="tpu_custom_call" | custom-call | flops 2147483648 | bytes 4194304 | tf_op jit(solution)/shard_map/pallas_call | solution.py:345
  40.2 1.5 %collective-permute-start.6 = (f32[264,128]{1,0:T(8,128)S(1)}, f32[264,128]{1,0:T(8,128)S(1)}, u32[]{:S(2)}, u32[]{:S(2)}) collective-permute-start(f32[264,128]{1,0:T(8,128)S(1)} %get-tuple-element.48), channel_id=1, source_target_pairs={{32,64},{64,32},{96,128},{128,96},{160,192},{192,160},{224,0},{0,2... | collective-permute-start | bytes 405512 | tf_op jit(solution)/shard_map/ppermute | solution.py:362
  41.7 2.4 %collective-permute-start.7 = (f32[264,128]{1,0:T(8,128)S(1)}, f32[264,128]{1,0:T(8,128)S(1)}, u32[]{:S(2)}, u32[]{:S(2)}) collective-permute-start(f32[264,128]{1,0:T(8,128)S(1)} %get-tuple-element.50), channel_id=1, source_target_pairs={{32,64},{64,32},{96,128},{128,96},{160,192},{192,160},{224,0},{0,2... | collective-permute-start | bytes 405512 | tf_op jit(solution)/shard_map/ppermute | solution.py:362
  44.1 2.7 %collective-permute-done.6.off = f32[264,128]{1,0:T(8,128)S(1)} collective-permute-done((f32[264,128]{1,0:T(8,128)S(1)}, f32[264,128]{1,0:T(8,128)S(1)}, u32[]{:S(2)}, u32[]{:S(2)}) %collective-permute-start.6) | collective-permute-done | bytes 135200 | tf_op jit(solution)/shard_map/ppermute | solution.py:362
  46.8 0.9 shard_map.101
  47.7 3.7 %collective-permute-start.8 = (f32[2,160,256]{2,1,0:T(8,128)S(1)}, f32[2,160,256]{2,1,0:T(8,128)S(1)}, u32[]{:S(2)}, u32[]{:S(2)}) collective-permute-start(f32[2,160,256]{2,1,0:T(8,128)S(1)} %get-tuple-element.52), channel_id=1, source_target_pairs={{0,1},{1,0},{2,3},{3,2},{4,5},{5,4},{6,7},{7,6},{8,9},{9,8},{10,11... | collective-permute-start | bytes 983048 | tf_op jit(solution)/shard_map/ppermute | solution.py:362
  51.5 0.9 shard_map.102
  52.4 2.0 %collective-permute-start.9 = (f32[2,160,256]{2,1,0:T(8,128)S(1)}, f32[2,160,256]{2,1,0:T(8,128)S(1)}, u32[]{:S(2)}, u32[]{:S(2)}) collective-permute-start(f32[2,160,256]{2,1,0:T(8,128)S(1)} %get-tuple-element.54), channel_id=1, source_target_pairs={{1,2},{2,1},{3,4},{4,3},{5,6},{6,5},{7,8},{8,7},{9,10},{10,9},{11,... | collective-permute-start | bytes 983048 | tf_op jit(solution)/shard_map/ppermute | solution.py:362
  54.4 5.3 %collective-permute-done.8.strip = f32[2,160,256]{2,1,0:T(8,128)S(1)} collective-permute-done((f32[2,160,256]{2,1,0:T(8,128)S(1)}, f32[2,160,256]{2,1,0:T(8,128)S(1)}, u32[]{:S(2)}, u32[]{:S(2)}) %collective-permute-start.8) | collective-permute-done | bytes 327712 | tf_op jit(solution)/shard_map/ppermute | solution.py:362
  59.8 0.9 shard_map.103
  60.7 3.0 %collective-permute-done.9.strip = f32[2,160,256]{2,1,0:T(8,128)S(1)} collective-permute-done((f32[2,160,256]{2,1,0:T(8,128)S(1)}, f32[2,160,256]{2,1,0:T(8,128)S(1)}, u32[]{:S(2)}, u32[]{:S(2)}) %collective-permute-start.9) | collective-permute-done | bytes 327712 | tf_op jit(solution)/shard_map/ppermute | solution.py:362
  63.7 0.9 shard_map.104
  64.6 0.1 collective-permute-start.12
  64.7 1.6 %collective-permute-done.12.on = f32[2,4,80,128]{3,2,1,0:T(8,128)S(1)} collective-permute-done((f32[2,4,80,128]{3,2,1,0:T(8,128)S(1)}, f32[2,4,80,128]{3,2,1,0:T(8,128)S(1)}, u32[]{:S(2)}, u32[]{:S(2)}) %collective-permute-start.12) | collective-permute-done | bytes 327712 | tf_op jit(solution)/shard_map/ppermute | solution.py:362
  66.3 4.5 %shard_map.105 = (f32[2,4,208,128]{3,2,1,0:T(8,128)S(1)}, f32[2,4,80,128]{3,2,1,0:T(8,128)S(1)}) custom-call(s32[14]{0:T(128)S(1)} %concatenate.4.flags, f32[2,4,256,128]{3,2,1,0:T(8,128)S(1)} %get-tuple-element.55.mid, f32[2,4,80,128]{3,2,1,0:T(8,128)S(1)} %collective-permute-done.12.on, f32[4,256,256]{2,1,0:T(8,128)S(1)} %get-tuple-element.42.roots, ...), custom_call_target="tpu_custom_call" | custom-call | flops 2147483648 | bytes 4194304 | tf_op jit(solution)/shard_map/pallas_call | solution.py:345
  70.8 0.2 collective-permute-start.13
  71.1 5.5 %collective-permute-start.11 = (f32[264,128]{1,0:T(8,128)S(1)}, f32[264,128]{1,0:T(8,128)S(1)}, u32[]{:S(2)}, u32[]{:S(2)}) collective-permute-start(f32[264,128]{1,0:T(8,128)S(1)} %get-tuple-element.57), channel_id=1, source_target_pairs={{32,64},{64,32},{96,128},{128,96},{160,192},{192,160},{224,0},{0,2... | collective-permute-start | bytes 405512 | tf_op jit(solution)/shard_map/ppermute | solution.py:362
  76.6 2.8 %collective-permute-done.11.odd = f32[264,128]{1,0:T(8,128)S(1)} collective-permute-done((f32[264,128]{1,0:T(8,128)S(1)}, f32[264,128]{1,0:T(8,128)S(1)}, u32[]{:S(2)}, u32[]{:S(2)}) %collective-permute-start.11) | collective-permute-done | bytes 135200 | tf_op jit(solution)/shard_map/ppermute | solution.py:362
  79.4 3.7 %collective-permute-done.10.even = f32[264,128]{1,0:T(8,128)S(1)} collective-permute-done((f32[264,128]{1,0:T(8,128)S(1)}, f32[264,128]{1,0:T(8,128)S(1)}, u32[]{:S(2)}, u32[]{:S(2)}) %collective-permute-start.10) | collective-permute-done | bytes 135200 | tf_op jit(solution)/shard_map/ppermute | solution.py:362
  83.1 4.8 %shard_map.106 = (f32[2,4,256,128]{3,2,1,0:T(8,128)S(1)}, f32[264,128]{1,0:T(8,128)S(1)}, f32[264,128]{1,0:T(8,128)S(1)}) custom-call(s32[14]{0:T(128)S(1)} %concatenate.4.flags, f32[2,4,256,128]{3,2,1,0:T(8,128)S(1)} %get-tuple-element.55.mid, f32[264,128]{1,0:T(8,128)S(1)} %collective-permute-done.10.even, f32[264,128]{1,0:T(8,128)S(1)} %collective-permute-done.11.odd, ...), custom_call_target="tpu_custom_call" | custom-call | flops 2147483648 | bytes 4194304 | tf_op jit(solution)/shard_map/pallas_call | solution.py:345
  87.9 2.4 %collective-permute-start.14 = (f32[264,128]{1,0:T(8,128)S(1)}, f32[264,128]{1,0:T(8,128)S(1)}, u32[]{:S(2)}, u32[]{:S(2)}) collective-permute-start(f32[264,128]{1,0:T(8,128)S(1)} %get-tuple-element.62), channel_id=1, source_target_pairs={{32,64},{64,32},{96,128},{128,96},{160,192},{192,160},{224,0},{0,2... | collective-permute-start | bytes 405512 | tf_op jit(solution)/shard_map/ppermute | solution.py:362
  90.2 1.6 %collective-permute-start.15 = (f32[264,128]{1,0:T(8,128)S(1)}, f32[264,128]{1,0:T(8,128)S(1)}, u32[]{:S(2)}, u32[]{:S(2)}) collective-permute-start(f32[264,128]{1,0:T(8,128)S(1)} %get-tuple-element.64), channel_id=1, source_target_pairs={{32,64},{64,32},{96,128},{128,96},{160,192},{192,160},{224,0},{0,2... | collective-permute-start | bytes 405512 | tf_op jit(solution)/shard_map/ppermute | solution.py:362
  91.8 2.7 %collective-permute-done.14.off = f32[264,128]{1,0:T(8,128)S(1)} collective-permute-done((f32[264,128]{1,0:T(8,128)S(1)}, f32[264,128]{1,0:T(8,128)S(1)}, u32[]{:S(2)}, u32[]{:S(2)}) %collective-permute-start.14) | collective-permute-done | bytes 135200 | tf_op jit(solution)/shard_map/ppermute | solution.py:362
  94.5 0.8 shard_map.107
  95.4 4.3 %collective-permute-done.15.off = f32[264,128]{1,0:T(8,128)S(1)} collective-permute-done((f32[264,128]{1,0:T(8,128)S(1)}, f32[264,128]{1,0:T(8,128)S(1)}, u32[]{:S(2)}, u32[]{:S(2)}) %collective-permute-start.15) | collective-permute-done | bytes 135200 | tf_op jit(solution)/shard_map/ppermute | solution.py:362
  99.7 0.8 shard_map.108
  100.5 0.1 collective-permute-start.17
  100.6 0.1 collective-permute-start.16
  100.7 7.1 %collective-permute-done.17.odd = f32[2,80,256]{2,1,0:T(8,128)S(1)} collective-permute-done((f32[2,80,256]{2,1,0:T(8,128)S(1)}, f32[2,80,256]{2,1,0:T(8,128)S(1)}, u32[]{:S(2)}, u32[]{:S(2)}) %collective-permute-start.17) | collective-permute-done | bytes 163872 | tf_op jit(solution)/shard_map/ppermute | solution.py:362
  107.8 1.5 %shard_map.109 = (f32[256,256]{1,0:T(8,128)}, f32[256,256]{1,0:T(8,128)}) custom-call(s32[14]{0:T(128)S(1)} %concatenate.4.flags, f32[2,4,256,128]{3,2,1,0:T(8,128)S(1)} %get-tuple-element.55.mid, f32[2,4,256,128]{3,2,1,0:T(8,128)S(1)} %get-tuple-element.65.total, f32[2,80,256]{2,1,0:T(8,128)S(1)} %collective-permute-done.16.even, ...), custom_call_target="tpu_custom_call" | custom-call | bytes 2097152 | tf_op jit(solution)/shard_map/pallas_call | solution.py:345
  (21 shorter events, 0.4 us)
Async XLA Ops:
  2.1 14.5 %copy-start.3 = (f32[256,256]{1,0:T(8,128)S(1)}, f32[256,256]{1,0:T(8,128)}, u32[]{:S(2)}) copy-start(f32[256,256]{1,0:T(8,128)} %probe_im.1) | copy-start | bytes 786436
  2.8 5.5 %collective-permute-start.1 = (f32[2,80,256]{2,1,0:T(8,128)S(1)}, f32[2,80,256]{2,1,0:T(8,128)S(1)}, u32[]{:S(2)}, u32[]{:S(2)}) collective-permute-start(f32[2,80,256]{2,1,0:T(8,128)S(1)} %get-tuple-element.36), channel_id=1, source_target_pairs={{0,1},{1,0},{2,3},{3,2},{4,5},{5,4},{6,7},{7,6},{8,9},{9,8},{10,11... | collective-permute-start | bytes 491528 | tf_op jit(solution)/shard_map/ppermute | solution.py:362
  4.5 3.2 %copy-start.4 = (s32[1,1,4,2]{2,3,1,0:T(2,128)S(1)}, s32[1,1,4,2]{2,3,1,0:T(2,128)}, u32[]{:S(2)}) copy-start(s32[1,1,4,2]{2,3,1,0:T(2,128)} %param.13) | copy-start | bytes 100
  4.5 9.7 %collective-permute-start = (f32[2,80,256]{2,1,0:T(8,128)S(1)}, f32[2,80,256]{2,1,0:T(8,128)S(1)}, u32[]{:S(2)}, u32[]{:S(2)}) collective-permute-start(f32[2,80,256]{2,1,0:T(8,128)S(1)} %get-tuple-element.35), channel_id=1, source_target_pairs={{1,2},{2,1},{3,4},{4,3},{5,6},{6,5},{7,8},{8,7},{9,10},{10,9},{11,... | collective-permute-start | bytes 491528 | tf_op jit(solution)/shard_map/ppermute | solution.py:362
  8.0 8.6 %copy-start = (f32[1,1,4,256,256]{4,3,2,1,0:T(8,128)S(1)}, f32[1,1,4,256,256]{4,3,2,1,0:T(8,128)}, u32[]{:S(2)}) copy-start(f32[1,1,4,256,256]{4,3,2,1,0:T(8,128)} %param.12) | copy-start | bytes 3145732
  8.0 8.6 %copy-start.1 = (bf16[8,256,256]{2,1,0:T(8,128)(2,1)S(1)}, bf16[8,256,256]{2,1,0:T(8,128)(2,1)}, u32[]{:S(2)}) copy-start(bf16[8,256,256]{2,1,0:T(8,128)(2,1)} %constant.35.clone.tables) | copy-start | bytes 3145732
  14.3 2.3 %copy-start.2 = (f32[256,256]{1,0:T(8,128)S(1)}, f32[256,256]{1,0:T(8,128)}, u32[]{:S(2)}) copy-start(f32[256,256]{1,0:T(8,128)} %probe_re.1) | copy-start | bytes 786436
  15.1 4.4 %collective-permute-start.4 = (f32[2,4,80,128]{3,2,1,0:T(8,128)S(1)}, f32[2,4,80,128]{3,2,1,0:T(8,128)S(1)}, u32[]{:S(2)}, u32[]{:S(2)}) collective-permute-start(f32[2,4,80,128]{3,2,1,0:T(8,128)S(1)} %get-tuple-element.41), channel_id=1, source_target_pairs={{0,32},{32,0},{64,96},{96,64},{128,160},{160,128},{192,224},{224,1... | collective-permute-start | bytes 983048 | tf_op jit(solution)/shard_map/ppermute | solution.py:362
  24.0 11.4 %collective-permute-start.5 = (f32[2,4,80,128]{3,2,1,0:T(8,128)S(1)}, f32[2,4,80,128]{3,2,1,0:T(8,128)S(1)}, u32[]{:S(2)}, u32[]{:S(2)}) collective-permute-start(f32[2,4,80,128]{3,2,1,0:T(8,128)S(1)} %get-tuple-element.46), channel_id=1, source_target_pairs={{0,32},{32,0},{64,96},{96,64},{128,160},{160,128},{192,224},{224,1... | collective-permute-start | bytes 983048 | tf_op jit(solution)/shard_map/ppermute | solution.py:362
  24.2 7.8 %collective-permute-start.2 = (f32[264,128]{1,0:T(8,128)S(1)}, f32[264,128]{1,0:T(8,128)S(1)}, u32[]{:S(2)}, u32[]{:S(2)}) collective-permute-start(f32[264,128]{1,0:T(8,128)S(1)} %get-tuple-element.39), channel_id=1, source_target_pairs={{32,64},{64,32},{96,128},{128,96},{160,192},{192,160},{224,0},{0,2... | collective-permute-start | bytes 405512 | tf_op jit(solution)/shard_map/ppermute | solution.py:362
  28.5 6.9 %collective-permute-start.3 = (f32[264,128]{1,0:T(8,128)S(1)}, f32[264,128]{1,0:T(8,128)S(1)}, u32[]{:S(2)}, u32[]{:S(2)}) collective-permute-start(f32[264,128]{1,0:T(8,128)S(1)} %get-tuple-element.40), channel_id=1, source_target_pairs={{32,64},{64,32},{96,128},{128,96},{160,192},{192,160},{224,0},{0,2... | collective-permute-start | bytes 405512 | tf_op jit(solution)/shard_map/ppermute | solution.py:362
  40.2 6.6 %collective-permute-start.6 = (f32[264,128]{1,0:T(8,128)S(1)}, f32[264,128]{1,0:T(8,128)S(1)}, u32[]{:S(2)}, u32[]{:S(2)}) collective-permute-start(f32[264,128]{1,0:T(8,128)S(1)} %get-tuple-element.48), channel_id=1, source_target_pairs={{32,64},{64,32},{96,128},{128,96},{160,192},{192,160},{224,0},{0,2... | collective-permute-start | bytes 405512 | tf_op jit(solution)/shard_map/ppermute | solution.py:362
  41.7 9.8 %collective-permute-start.7 = (f32[264,128]{1,0:T(8,128)S(1)}, f32[264,128]{1,0:T(8,128)S(1)}, u32[]{:S(2)}, u32[]{:S(2)}) collective-permute-start(f32[264,128]{1,0:T(8,128)S(1)} %get-tuple-element.50), channel_id=1, source_target_pairs={{32,64},{64,32},{96,128},{128,96},{160,192},{192,160},{224,0},{0,2... | collective-permute-start | bytes 405512 | tf_op jit(solution)/shard_map/ppermute | solution.py:362
  47.7 12.0 %collective-permute-start.8 = (f32[2,160,256]{2,1,0:T(8,128)S(1)}, f32[2,160,256]{2,1,0:T(8,128)S(1)}, u32[]{:S(2)}, u32[]{:S(2)}) collective-permute-start(f32[2,160,256]{2,1,0:T(8,128)S(1)} %get-tuple-element.52), channel_id=1, source_target_pairs={{0,1},{1,0},{2,3},{3,2},{4,5},{5,4},{6,7},{7,6},{8,9},{9,8},{10,11... | collective-permute-start | bytes 983048 | tf_op jit(solution)/shard_map/ppermute | solution.py:362
  52.4 11.3 %collective-permute-start.9 = (f32[2,160,256]{2,1,0:T(8,128)S(1)}, f32[2,160,256]{2,1,0:T(8,128)S(1)}, u32[]{:S(2)}, u32[]{:S(2)}) collective-permute-start(f32[2,160,256]{2,1,0:T(8,128)S(1)} %get-tuple-element.54), channel_id=1, source_target_pairs={{1,2},{2,1},{3,4},{4,3},{5,6},{6,5},{7,8},{8,7},{9,10},{10,9},{11,... | collective-permute-start | bytes 983048 | tf_op jit(solution)/shard_map/ppermute | solution.py:362
  64.6 1.7 %collective-permute-start.12 = (f32[2,4,80,128]{3,2,1,0:T(8,128)S(1)}, f32[2,4,80,128]{3,2,1,0:T(8,128)S(1)}, u32[]{:S(2)}, u32[]{:S(2)}) collective-permute-start(f32[2,4,80,128]{3,2,1,0:T(8,128)S(1)} %get-tuple-element.58), channel_id=1, source_target_pairs={{0,32},{32,0},{64,96},{96,64},{128,160},{160,128},{192,224},{224,1... | collective-permute-start | bytes 983048 | tf_op jit(solution)/shard_map/ppermute | solution.py:362
  70.8 12.3 %collective-permute-start.13 = (f32[2,4,80,128]{3,2,1,0:T(8,128)S(1)}, f32[2,4,80,128]{3,2,1,0:T(8,128)S(1)}, u32[]{:S(2)}, u32[]{:S(2)}) collective-permute-start(f32[2,4,80,128]{3,2,1,0:T(8,128)S(1)} %get-tuple-element.60), channel_id=1, source_target_pairs={{0,32},{32,0},{64,96},{96,64},{128,160},{160,128},{192,224},{224,1... | collective-permute-start | bytes 983048 | tf_op jit(solution)/shard_map/ppermute | solution.py:362
  71.1 8.3 %collective-permute-start.11 = (f32[264,128]{1,0:T(8,128)S(1)}, f32[264,128]{1,0:T(8,128)S(1)}, u32[]{:S(2)}, u32[]{:S(2)}) collective-permute-start(f32[264,128]{1,0:T(8,128)S(1)} %get-tuple-element.57), channel_id=1, source_target_pairs={{32,64},{64,32},{96,128},{128,96},{160,192},{192,160},{224,0},{0,2... | collective-permute-start | bytes 405512 | tf_op jit(solution)/shard_map/ppermute | solution.py:362
  76.5 6.5 %collective-permute-start.10 = (f32[264,128]{1,0:T(8,128)S(1)}, f32[264,128]{1,0:T(8,128)S(1)}, u32[]{:S(2)}, u32[]{:S(2)}) collective-permute-start(f32[264,128]{1,0:T(8,128)S(1)} %get-tuple-element.56), channel_id=1, source_target_pairs={{32,64},{64,32},{96,128},{128,96},{160,192},{192,160},{224,0},{0,2... | collective-permute-start | bytes 405512 | tf_op jit(solution)/shard_map/ppermute | solution.py:362
  87.9 6.7 %collective-permute-start.14 = (f32[264,128]{1,0:T(8,128)S(1)}, f32[264,128]{1,0:T(8,128)S(1)}, u32[]{:S(2)}, u32[]{:S(2)}) collective-permute-start(f32[264,128]{1,0:T(8,128)S(1)} %get-tuple-element.62), channel_id=1, source_target_pairs={{32,64},{64,32},{96,128},{128,96},{160,192},{192,160},{224,0},{0,2... | collective-permute-start | bytes 405512 | tf_op jit(solution)/shard_map/ppermute | solution.py:362
  90.2 9.4 %collective-permute-start.15 = (f32[264,128]{1,0:T(8,128)S(1)}, f32[264,128]{1,0:T(8,128)S(1)}, u32[]{:S(2)}, u32[]{:S(2)}) collective-permute-start(f32[264,128]{1,0:T(8,128)S(1)} %get-tuple-element.64), channel_id=1, source_target_pairs={{32,64},{64,32},{96,128},{128,96},{160,192},{192,160},{224,0},{0,2... | collective-permute-start | bytes 405512 | tf_op jit(solution)/shard_map/ppermute | solution.py:362
  100.5 7.3 %collective-permute-start.17 = (f32[2,80,256]{2,1,0:T(8,128)S(1)}, f32[2,80,256]{2,1,0:T(8,128)S(1)}, u32[]{:S(2)}, u32[]{:S(2)}) collective-permute-start(f32[2,80,256]{2,1,0:T(8,128)S(1)} %get-tuple-element.67), channel_id=1, source_target_pairs={{1,2},{2,1},{3,4},{4,3},{5,6},{6,5},{7,8},{8,7},{9,10},{10,9},{11,... | collective-permute-start | bytes 491528 | tf_op jit(solution)/shard_map/ppermute | solution.py:362
  100.6 7.2 %collective-permute-start.16 = (f32[2,80,256]{2,1,0:T(8,128)S(1)}, f32[2,80,256]{2,1,0:T(8,128)S(1)}, u32[]{:S(2)}, u32[]{:S(2)}) collective-permute-start(f32[2,80,256]{2,1,0:T(8,128)S(1)} %get-tuple-element.66), channel_id=1, source_target_pairs={{0,1},{1,0},{2,3},{3,2},{4,5},{5,4},{6,7},{7,6},{8,9},{9,8},{10,11... | collective-permute-start | bytes 491528 | tf_op jit(solution)/shard_map/ppermute | solution.py:362
